TPU v7x, 32 devices: a whole 2x2x4 slice. The times are simulated.
32 devices in a mesh: leaf: 4 (over x, core), sub: 8 (over z, y).
Axes of the slice: x: 2, y: 2, z: 4, core: 2. Of those that a mesh axis runs over, the one named last changes fastest.
Arguments:
- points: bfloat16 [131072, 128], P(('leaf', 'sub')), may hold values from -5 to 5
- charges: bfloat16 [131072, 64], P(('leaf', 'sub')), may hold values from -0.796875 to 0.796875
- near_leaves: int32 [256, 12], P(('leaf', 'sub')), may hold values from 0 to 255, as said below
- leaf_interpolant: bfloat16 [256, 512, 256], P(('leaf', 'sub')), may hold values from -0.25 to 0.25
- skel_leaf: int32 [256, 256], P(('leaf', 'sub')), may hold values from 0 to 511, as said below
- interp_mid: bfloat16 [32, 2048, 256], P(('leaf', 'sub')), may hold values from -0.375 to 0.375
- skel_mid: int32 [32, 256], P(('leaf', 'sub')), may hold values from 0 to 2047, as said below
- mid_partners: int32 [32, 4], P(('leaf', 'sub')), may hold values from 0 to 31, as said below
- interp_top: bfloat16 [4, 2048, 256], P('leaf', 'sub'), may hold values from -0.125 to 0.125
- skel_top: int32 [4, 256], P('leaf'), may hold values from 0 to 2047, as said below
Outputs:
- potential: float32 [131072, 64], P(('leaf', 'sub'))
Inputs may be any that keep to these rules, and one draw needn't show every extreme that they name: `near_leaves`: row l lists leaf l first, then 12 - 1 other different leaves of the same top node. Over the rows of one device's 8 leaves, at most 2 different leaves of any one other device are named. `skel_leaf`: different indices in a row. `skel_mid`: different indices in a row. `skel_top`: different indices in a row. `mid_partners`: different middle nodes of the same top node, never the node itself.
All inputs are finite; a program needn't handle non-finite values.
Results may differ from a plain program's by a relative error of at most 0.008.
Values may be sent and summed in bfloat16 or wider, within the bound.
No kernel may reach another device: no remote copies, remote signals or barrier semaphores. Data moves between devices by JAX's collectives and lax.ppermute only.
A program may use at most 128 MiB of HBM per device.

v0:
```python
import jax
import jax.numpy as jnp
from jax import lax
from jax.sharding import PartitionSpec as P

CAP = 2


kernel_rate = 0.25


def kernel_block(target, source):
    products = jnp.einsum("id,kjd->kij", target, source, preferred_element_type=jnp.float32)
    target_sq = jnp.sum(jnp.square(target.astype(jnp.float32)), axis=-1)
    source_sq = jnp.sum(jnp.square(source.astype(jnp.float32)), axis=-1)
    distance = target_sq[None, :, None] + source_sq[:, None, :] - 2.0 * products
    return jnp.exp(-kernel_rate * distance).astype(jnp.bfloat16)


def kernel_pair(target, target_sq, source):
    products = jnp.dot(target, source.T, preferred_element_type=jnp.float32)
    source_sq = jnp.sum(jnp.square(source.astype(jnp.float32)), axis=-1)
    distance = target_sq[:, None] + source_sq[None, :] - 2.0 * products
    return jnp.exp(-kernel_rate * distance).astype(jnp.bfloat16)


def slot_table(needed):
    slot_ranks = jnp.cumsum(needed.astype(jnp.int32), axis=1) - 1
    matches = needed[:, :, None] & (
        slot_ranks[:, :, None] == jnp.arange(CAP, dtype=jnp.int32)[None, None, :]
    )
    member_ids = jnp.arange(needed.shape[1], dtype=jnp.int32)
    chosen = jnp.sum(matches.astype(jnp.int32) * member_ids[None, :, None], axis=1)
    return (slot_ranks, chosen)


def body(
    points,
    charges,
    near_leaves,
    leaf_interpolant,
    skel_leaf,
    interp_mid,
    skel_mid,
    mid_partners,
    interp_top,
    skel_top,
):
    group_size = lax.axis_size("sub")
    self_index = lax.axis_index("sub")
    leaf_dev = leaf_interpolant.shape[0]
    leaf_size = leaf_interpolant.shape[1]
    coords = points.shape[1]
    rhs_count = charges.shape[1]
    near_count = near_leaves.shape[1]
    group_first = lax.axis_index("leaf") * group_size
    leaf_base = group_first * leaf_dev
    point_blocks = points.reshape(leaf_dev, leaf_size, coords)
    charge_blocks = charges.reshape(leaf_dev, leaf_size, rhs_count)
    local_ids = near_leaves - leaf_base
    owners = local_ids // leaf_dev
    members = local_ids % leaf_dev
    slots_all = jnp.arange(group_size * leaf_dev, dtype=jnp.int32)
    others = (jnp.arange(group_size, dtype=jnp.int32) != self_index)[:, None]
    wanted = (
        jnp.any(local_ids[:, :, None] == slots_all[None, None, :], axis=(0, 1)).reshape(
            group_size, leaf_dev
        )
        & others
    )
    slot_ranks, chosen = slot_table(wanted)
    listed = lax.all_gather(near_leaves, "sub", axis=0, tiled=True).reshape(group_size, -1)
    my_leaves = leaf_base + self_index * leaf_dev + jnp.arange(leaf_dev, dtype=jnp.int32)
    asked_for = jnp.any(listed[:, :, None] == my_leaves[None, None, :], axis=1) & others
    unused, handed = slot_table(asked_for)
    recv_points, recv_charges = (
        lax.all_to_all(point_blocks[handed], "sub", split_axis=0, concat_axis=0, tiled=True),
        lax.all_to_all(charge_blocks[handed], "sub", split_axis=0, concat_axis=0, tiled=True),
    )
    pool_points = jnp.concatenate(
        (point_blocks, recv_points.reshape(-1, leaf_size, coords)), axis=0
    )
    pool_charges = jnp.concatenate(
        (charge_blocks, recv_charges.reshape(-1, leaf_size, rhs_count)), axis=0
    )
    local_flag = owners == self_index
    slot_of = jnp.clip(slot_ranks[owners, members], 0, CAP - 1)
    pool_index = jnp.where(local_flag, members, leaf_dev + owners * CAP + slot_of)

    def near_leaf(leaf_index, totals):
        target = lax.dynamic_index_in_dim(point_blocks, leaf_index, 0, keepdims=False)
        target_sq = jnp.sum(jnp.square(target.astype(jnp.float32)), axis=-1)
        summed = jnp.zeros((leaf_size, rhs_count), jnp.float32)
        for entry in range(near_count):
            source_index = pool_index[leaf_index, entry]
            source = lax.dynamic_index_in_dim(pool_points, source_index, 0, keepdims=False)
            weights = lax.dynamic_index_in_dim(pool_charges, source_index, 0, keepdims=False)
            kernel = kernel_pair(target, target_sq, source)
            summed = summed + jnp.dot(kernel, weights, preferred_element_type=jnp.float32)
        return lax.dynamic_update_slice(totals, summed[None], (leaf_index, 0, 0))

    near_sum = lax.fori_loop(
        0, leaf_dev, near_leaf, jnp.zeros((leaf_dev, leaf_size, rhs_count), jnp.float32)
    )
    leaf_upward = jnp.einsum(
        "tmv,tmz->tvz", leaf_interpolant, charge_blocks, preferred_element_type=jnp.float32
    ).astype(jnp.bfloat16)
    leaf_skel = jnp.take_along_axis(point_blocks, skel_leaf[:, :, None], axis=1)
    mid_up = jnp.einsum(
        "qs,qr->sr",
        interp_mid[0],
        leaf_upward.reshape(-1, rhs_count),
        preferred_element_type=jnp.float32,
    ).astype(jnp.bfloat16)
    mid_points = leaf_skel.reshape(-1, coords)[skel_mid[0]]
    partners = mid_partners[0]
    skel_count = mid_points.shape[0]
    shard_points = lax.all_gather(mid_points[None], "sub", axis=0, tiled=True)
    shard_weights = lax.all_gather(mid_up[None], "sub", axis=0, tiled=True)
    node_ids = group_first + jnp.arange(shard_points.shape[0], dtype=jnp.int32)
    flags = jnp.sum((partners[:, None] == node_ids[None, :]).astype(jnp.float32), axis=0)
    kernel = kernel_block(mid_points, shard_points) * flags.astype(jnp.bfloat16)[:, None, None]
    mid_sum = jnp.einsum("kij,kjr->ir", kernel, shard_weights, preferred_element_type=jnp.float32)
    top_part = jnp.einsum("qs,qr->sr", interp_top[0], mid_up, preferred_element_type=jnp.float32)
    picked = skel_top[0] - self_index * skel_count
    inside = (picked >= 0) & (picked < skel_count)
    top_rows = jnp.where(
        inside[:, None], mid_points[jnp.clip(picked, 0, skel_count - 1)].astype(jnp.float32), 0.0
    )
    top_weight, top_points = lax.psum((top_part, top_rows), "sub")
    top_weight = top_weight.astype(jnp.bfloat16)
    top_points = top_points.astype(jnp.bfloat16)
    own_group = lax.axis_index("leaf")
    shard_points = lax.all_gather(top_points[None], "leaf", axis=0, tiled=True)
    shard_weights = lax.all_gather(top_weight[None], "leaf", axis=0, tiled=True)
    node_ids = jnp.arange(shard_points.shape[0], dtype=jnp.int32)
    flags = (node_ids != own_group).astype(jnp.bfloat16)
    kernel = kernel_block(top_points, shard_points) * flags[:, None, None]
    top_sum = jnp.einsum("kij,kjr->ir", kernel, shard_weights, preferred_element_type=jnp.float32)
    top_sum = top_sum.astype(jnp.bfloat16)
    mid_total = (
        mid_sum + jnp.dot(interp_top[0], top_sum, preferred_element_type=jnp.float32)
    ).astype(jnp.bfloat16)
    leaf_downward = (
        jnp.dot(interp_mid[0], mid_total, preferred_element_type=jnp.float32)
        .astype(jnp.bfloat16)
        .reshape(leaf_dev, -1, rhs_count)
    )
    distant_sum = jnp.einsum(
        "xiv,xvq->xiq", leaf_interpolant, leaf_downward, preferred_element_type=jnp.float32
    )
    return (near_sum + distant_sum).reshape(-1, rhs_count)


def solution(mesh):
    placed = (
        P(("leaf", "sub"), None),
        P(("leaf", "sub"), None),
        P(("leaf", "sub"), None),
        P(("leaf", "sub"), None, None),
        P(("leaf", "sub"), None),
        P(("leaf", "sub"), None, None),
        P(("leaf", "sub"), None),
        P(("leaf", "sub"), None),
        P("leaf", "sub", None),
        P("leaf", None),
    )
    return jax.shard_map(
        body, mesh=mesh, in_specs=placed, out_specs=P(("leaf", "sub"), None), check_vma=False
    )
```

profile of v0, /device:TPU:0, one launch (start us, length us, event | category | flops | bytes accessed | tf_op | source)
XLA Modules:
  0.0 667.1 jit_solution(15691092808204949463)
XLA Ops:
  0.0 32.7 %all_gather.15 = s32[64,12]{1,0:T(8,128)S(1)} all-gather(s32[8,12]{1,0:T(8,128)} %param.14), channel_id=1, replica_groups=mesh['leaf'=4,'sub'=8] {'sub'}, dimensions={0}, use_global_device_ids=true | all-gather | bytes 3456 | tf_op jit(solution)/shard_map/all_gather | solution.py:72
  39.4 2.8 copy.36
  42.1 5.5 all-to-all-start.1
  50.1 20.4 %gather_fusion.5 = bf16[2048,128]{1,0:T(8,128)(2,1)} fusion(bf16[8,512,128]{2,1,0:T(8,128)(2,1)S(1)} %bitcast.380, s32[2048]{0:T(1024)S(1)} %bitcast.378), kind=kCustom, calls=%fused_computation.5 | custom fusion | bytes 1064960 | tf_op jit(solution)/shard_map/jit(take_along_axis)/gather | solution.py:108
  73.8 6.0 all-to-all-start
  85.7 61.6 %all-reduce.2 = (bf16[256,128]{1,0:T(8,128)(2,1)}, bf16[256,64]{0,1:T(8,128)(2,1)S(1)}) all-reduce(f32[256,128]{1,0:T(8,128)S(1)} %convert_select_fusion, f32[256,64]{0,1:T(8,128)} %convolution_bitcast_fusion.2), channel_id=1, replica_groups=mesh['leaf'=4,'sub'=8] {'sub'}, use_global_device_ids=true, to_apply=%region_23.24 | all-reduce | flops 49152 | bytes 294912 | tf_op jit(solution)/shard_map/psum | solution.py:130
  147.3 5.8 all-gather.3
  153.1 6.0 all-gather.2
  160.3 33.0 %all-gather.1 = bf16[2048,64]{0,1:T(8,128)(2,1)} all-gather(bf16[256,64]{0,1:T(8,128)(2,1)S(1)} %bitcast.394), channel_id=3, replica_groups=mesh['leaf'=4,'sub'=8] {'sub'}, dimensions={0}, use_global_device_ids=true | all-gather | bytes 294912 | tf_op jit(solution)/shard_map/all_gather | solution.py:119
  196.3 31.4 %all-gather = bf16[2048,128]{1,0:T(8,128)(2,1)S(1)} all-gather(bf16[256,128]{1,0:T(8,128)(2,1)S(1)} %gather_fusion.3), channel_id=2, replica_groups=mesh['leaf'=4,'sub'=8] {'sub'}, dimensions={0}, use_global_device_ids=true | all-gather | bytes 589824 | tf_op jit(solution)/shard_map/all_gather | solution.py:118
  235.0 2.8 copy.37
  237.7 4.1 pad_maximum_fusion.1
  241.9 3.6 pad_maximum_fusion
  245.4 418.6 %while.13 = (s32[]{:T(128)}, f32[8,512,64]{1,2,0:T(8,128)}, bf16[8,512,128]{2,1,0:T(8,128)(2,1)S(1)}, s32[8,12]{1,0:T(8,128)S(1)}, bf16[24,512,128]{2,1,0:T(8,12...) while((s32[]{:T(128)}, f32[8,512,64]{1,2,0:T(8,128)}, ...), condition=%wide.region_19.20_spmd, body=%wide.region_5.19_spmd.sunk | while | flops 1226597888 | bytes 9532565 | solution.py:102
  268.4 2.4 multiply_reduce_fusion.18
  273.0 2.3 fusion.431
  277.5 2.3 fusion.433
  279.8 2.3 fusion.434
  284.3 2.3 fusion.436
  291.0 2.3 fusion.439
  295.5 2.3 fusion.441
  320.7 2.4 multiply_reduce_fusion.18
  325.3 2.3 fusion.431
  329.8 2.3 fusion.433
  332.1 2.3 fusion.434
  336.6 2.3 fusion.436
  343.3 2.3 fusion.439
  347.8 2.3 fusion.441
  373.0 2.4 multiply_reduce_fusion.18
  377.7 2.3 fusion.431
  382.2 2.3 fusion.433
  388.9 2.3 fusion.436
  395.7 2.3 fusion.439
  400.2 2.3 fusion.441
  425.4 2.4 multiply_reduce_fusion.18
  430.0 2.3 fusion.431
  434.5 2.3 fusion.433
  441.2 2.3 fusion.436
  448.0 2.3 fusion.439
  452.5 2.3 fusion.441
  477.7 2.4 multiply_reduce_fusion.18
  482.3 2.3 fusion.431
  486.8 2.3 fusion.433
  493.6 2.3 fusion.436
  500.3 2.3 fusion.439
  504.8 2.3 fusion.441
  530.0 2.4 multiply_reduce_fusion.18
  534.6 2.3 fusion.431
  539.1 2.3 fusion.433
  545.9 2.3 fusion.436
  552.7 2.3 fusion.439
  557.2 2.3 fusion.441
  582.3 2.4 multiply_reduce_fusion.18
  587.0 2.3 fusion.431
  591.5 2.3 fusion.433
  598.2 2.3 fusion.436
  605.0 2.3 fusion.439
  609.5 2.3 fusion.441
  634.7 2.4 multiply_reduce_fusion.18
  639.3 2.3 fusion.431
  643.8 2.3 fusion.433
  650.6 2.3 fusion.436
  657.3 2.3 fusion.439
  661.8 2.3 fusion.441
  (142 shorter events, 159.1 us)
Async XLA Ops:
  0.0 82.7 %copy-start = (bf16[8,512,256]{2,1,0:T(8,128)(2,1)S(1)}, bf16[8,512,256]{2,1,0:T(8,128)(2,1)}, u32[]{:S(2)}) copy-start(bf16[8,512,256]{2,1,0:T(8,128)(2,1)} %param.15) | copy-start | bytes 6291460
  36.2 1.0 copy-start.2
  39.4 8.3 %copy-start.6 = (s32[8,256]{1,0:T(8,128)S(1)}, s32[8,256]{1,0:T(8,128)}, u32[]{:S(2)}) copy-start(s32[8,256]{1,0:T(8,128)} %param.16) | copy-start | bytes 24580
  39.4 8.6 %copy-start.1 = (bf16[4096,128]{1,0:T(8,128)(2,1)S(1)}, bf16[4096,128]{1,0:T(8,128)(2,1)}, u32[]{:S(2)}) copy-start(bf16[4096,128]{1,0:T(8,128)(2,1)} %param.12) | copy-start | bytes 3145732
  42.1 31.6 %all-to-all-start.1 = ((bf16[8,2,512,64]{2,3,1,0:T(8,128)(2,1)}), bf16[8,2,512,64]{2,3,1,0:T(8,128)(2,1)}, u32[]{:S(2)}, u32[]{:S(2)}) async-start(bf16[8,2,512,64]{2,3,1,0:T(8,128)(2,1)} %bitcast.387), calls=%async_computation.1 | async-start | bytes 2097152 | tf_op jit(solution)/shard_map/all_to_all | solution.py:78
  70.5 1.0 copy-start.9
  70.5 1.1 copy-start.8
  73.8 168.1 %all-to-all-start = ((bf16[8,2,512,128]{3,2,1,0:T(8,128)(2,1)}), bf16[8,2,512,128]{3,2,1,0:T(8,128)(2,1)}, u32[]{:S(2)}, u32[]{:S(2)}) async-start(bf16[8,2,512,128]{3,2,1,0:T(8,128)(2,1)} %bitcast.386), calls=%async_computation | async-start | bytes 4194304 | tf_op jit(solution)/shard_map/all_to_all | solution.py:77
  81.7 3.2 copy-start.5
  82.6 2.0 copy-start.3
  82.7 77.0 %copy-start.10 = (s32[1,4]{1,0:T(1,128)S(1)}, s32[1,4]{1,0:T(1,128)}, u32[]{:S(2)}) copy-start(s32[1,4]{1,0:T(1,128)} %param.19) | copy-start | bytes 52
  227.7 0.8 copy-start.4
  228.9 2.0 copy-start.7
where the time goes:
time: 673 us; the launch traced here: 667 us
  matrix products  227 us (34%)
  loops' own time  178 us (26%)
  blocking collectives  171 us (25%)
  local copies, waits for them, and re-layouts  44.4 us (7%)
  other arithmetic  35.6 us (5%)
  starting transfers between devices  11.5 us (2%)
    dot_general x96, matrix products, near_leaf(): jnp.dot(kernel, weights, preferred_element_type=jnp.float32)  216 us
    another operation x1, loops' own time, body(): lax.fori_loop(0, leaf_dev, near_leaf, jnp.zeros((leaf_dev, leaf_size, rhs...  178 us
    psum x1, blocking collectives, body(): top_weight, top_points = lax.psum((top_part, top_rows), 'sub')  61.6 us
    all_gather x1, blocking collectives, body(): shard_weights = lax.all_gather(mid_up[None], 'sub', axis=0, tiled=True)  33 us
    all_gather x1, blocking collectives, body(): lax.all_gather(near_leaves, 'sub', axis=0, tiled=True)  32.7 us
    all_gather x1, blocking collectives, body(): shard_points = lax.all_gather(mid_points[None], 'sub', axis=0, tiled=True)  31.4 us
    gather x1, local copies, waits for them, and re-layouts, body(): leaf_skel = jnp.take_along_axis(point_blocks, skel_leaf[:, :, None], axis=1)  20.4 us
    reduce_sum x8, other arithmetic, kernel_pair(): source_sq = jnp.sum(jnp.square(source.astype(jnp.float32)), axis=-1)  19.4 us
  transfers between devices with their start and end apart: 2, of which 0 were waited for; matrix products, arithmetic and copies ran while one was open for 7% of the time, Pallas kernels for 0%

commit v1 on v0

v1 whole, which is shorter than its diff:
```python
import functools
import math

import jax
import jax.numpy as jnp
from jax import lax
from jax.experimental import pallas as pl
from jax.experimental.pallas import tpu as pltpu
from jax.sharding import PartitionSpec as P

CAP = 2
UNROLL = 4
LANES = 128
kernel_rate = 0.25
LOG2E = math.log2(math.e)
bf16 = jnp.bfloat16
f32 = jnp.float32
i32 = jnp.int32

ROWS_ROWS = (((1,), (1,)), ((), ()))


def dot(a, b):
    return jnp.dot(a, b, preferred_element_type=f32)


def dot_rows(a, b):
    return lax.dot_general(a, b, ROWS_ROWS, preferred_element_type=f32)


def squares(x):
    xf = x.astype(f32)
    sq = xf * xf
    high = sq.astype(bf16)
    low = (sq - high.astype(f32)).astype(bf16)
    return high, low


def source_term(x):
    high, low = squares(x)
    ones = jnp.ones((x.shape[1], LANES), bf16)
    return (dot(high, ones) + dot(low, ones)) * (-kernel_rate * LOG2E)


def target_term(x):
    high, low = squares(x)
    ones = jnp.ones((8, x.shape[1]), bf16)
    return (dot_rows(ones, high) + dot_rows(ones, low)) * (-kernel_rate * LOG2E)


def kernel_tile(source, source_sq, target, target_sq):
    products = dot_rows(source, target)
    columns = []
    for at in range(0, target.shape[0], LANES):
        exponent = products[:, at : at + LANES] * (2.0 * kernel_rate * LOG2E) + (
            source_sq + target_sq[0:1, at : at + LANES]
        )
        columns.append(jnp.exp2(exponent).astype(bf16))
    return jnp.concatenate(columns, axis=1)


def cost(flops, bytes_accessed, transcendentals=0):
    return pl.CostEstimate(
        flops=int(flops), bytes_accessed=int(bytes_accessed), transcendentals=int(transcendentals)
    )


def params():
    return pltpu.CompilerParams(vmem_limit_bytes=56 << 20)


def want_kernel(leaf_dev, group, where, near, chosen, pool):
    base, self_index = where[0], where[1]
    rows, near_count = near.shape
    width = max(LANES, group * leaf_dev)
    local = near[...] - base
    lane = lax.broadcasted_iota(i32, (rows, width), 1)
    member = lax.rem(lane, leaf_dev)
    owner = lax.div(lane, leaf_dev)
    named = jnp.zeros((rows, width), f32)
    for entry in range(near_count):
        named = jnp.maximum(named, (local[:, entry : entry + 1] == lane).astype(f32))
    wanted = jnp.max(named, axis=0, keepdims=True)
    wanted = jnp.where(owner == self_index, 0.0, jnp.broadcast_to(wanted, (rows, width)))
    row_id = lax.broadcasted_iota(i32, (width, width), 0)
    col_id = lax.broadcasted_iota(i32, (width, width), 1)
    before = (lax.div(row_id, leaf_dev) == lax.div(col_id, leaf_dev)) & (row_id < col_id)
    rank = dot(wanted.astype(bf16), before.astype(f32).astype(bf16))
    slot = lax.broadcasted_iota(i32, (rows, width), 0).astype(f32)
    picked = jnp.where((wanted > 0.0) & (rank == slot), member.astype(f32), 0.0)
    owner_row = lax.broadcasted_iota(i32, (group, width), 0)
    owner_of = lax.div(lax.broadcasted_iota(i32, (group, width), 1), leaf_dev)
    belongs = (owner_row == owner_of).astype(f32).astype(bf16)
    chosen[...] = dot_rows(belongs, picked.astype(bf16)).astype(i32)
    place = jnp.zeros((rows, LANES), i32)
    short_lane = lax.broadcasted_iota(i32, (rows, LANES), 1)
    for entry in range(near_count):
        ids = local[:, entry : entry + 1]
        at = jnp.sum(jnp.where(ids == lane, rank, 0.0), axis=1, keepdims=True).astype(i32)
        entry_owner = lax.div(ids, leaf_dev)
        index = jnp.where(
            entry_owner == self_index,
            lax.rem(ids, leaf_dev),
            leaf_dev + entry_owner * CAP + jnp.clip(at, 0, CAP - 1),
        )
        place = jnp.where(short_lane == entry, index, place)
    pool[...] = place


def want(near_leaves, where, leaf_dev, group):
    rows = near_leaves.shape[0]
    return pl.pallas_call(
        functools.partial(want_kernel, leaf_dev, group),
        out_shape=(
            jax.ShapeDtypeStruct((group, rows), i32),
            jax.ShapeDtypeStruct((rows, LANES), i32),
        ),
        grid_spec=pltpu.PrefetchScalarGridSpec(
            num_scalar_prefetch=1,
            grid=(1,),
            in_specs=[pl.BlockSpec(near_leaves.shape, lambda i, w: (0, 0))],
            out_specs=(
                pl.BlockSpec((group, rows), lambda i, w: (0, 0)),
                pl.BlockSpec((rows, LANES), lambda i, w: (0, 0)),
            ),
        ),
        compiler_params=params(),
        cost_estimate=cost(1e6, 1e5),
        name="want",
    )(where, near_leaves)


def pack_kernel(leaf_size, handed, points, charges, *outs):
    group = outs[0].shape[0]
    rhs = charges.shape[0]

    def one(peer, carry):
        for slot, out in enumerate(outs):
            leaf = handed[peer, slot]
            out[peer, :leaf_size, :] = points[leaf]
            for tile in range(leaf_size // LANES):
                at = pl.multiple_of(leaf * leaf_size + tile * LANES, LANES)
                row = leaf_size + tile * rhs
                out[peer, row : row + rhs, :] = charges[:, pl.ds(at, LANES)]
        return carry

    lax.fori_loop(0, group, one, 0)


def pack(handed, points, charges):
    leaf_dev, leaf_size, coords = points.shape
    group = handed.shape[0]
    rows = leaf_size + leaf_size // LANES * charges.shape[0]
    shape = (group, rows, coords)
    return pl.pallas_call(
        functools.partial(pack_kernel, leaf_size),
        out_shape=tuple(jax.ShapeDtypeStruct(shape, bf16) for _ in range(CAP)),
        grid_spec=pltpu.PrefetchScalarGridSpec(
            num_scalar_prefetch=1,
            grid=(1,),
            in_specs=[
                pl.BlockSpec(points.shape, lambda i, h: (0, 0, 0)),
                pl.BlockSpec(charges.shape, lambda i, h: (0, 0)),
            ],
            out_specs=tuple(pl.BlockSpec(shape, lambda i, h: (0, 0, 0)) for _ in range(CAP)),
        ),
        compiler_params=params(),
        cost_estimate=cost(1e5, 8e6),
        name="pack",
    )(handed, points, charges)


def run_pairs(pool, near_count, leaves, keep, tl, sl, prepared, acc):
    points_t, target_sq, points_s, source_sq, charge_of = prepared

    def scan(leaf, count):
        for entry in range(near_count):
            kept, source = keep(pool[leaf, entry])
            tl[count] = leaf
            sl[count] = source
            count = count + kept.astype(i32)
        return count

    count = lax.fori_loop(leaves[0], leaves[1], scan, jnp.int32(0))

    def one(at):
        target, source = tl[at], sl[at]
        tile = kernel_tile(
            points_s(source), source_sq[source], points_t[target], target_sq[target]
        )
        acc[target] += dot(charge_of(source), tile)

    def several(step, carry):
        for k in range(UNROLL):
            one(step * UNROLL + k)
        return carry

    def single(at, carry):
        one(at)
        return carry

    whole = lax.div(count, UNROLL)
    lax.fori_loop(0, whole, several, 0)
    lax.fori_loop(whole * UNROLL, count, single, 0)


def near_local_kernel(near_count, leaves, pool, points, charges, out, tl, sl, ssq, tsq, acc):
    leaf_dev, leaf_size, _ = points.shape

    def prepare(leaf, carry):
        x = points[leaf]
        ssq[leaf] = source_term(x)
        return carry

    def prepare_target(leaf, carry):
        tsq[leaf] = target_term(points[leaf])
        acc[leaf] = jnp.zeros(acc.shape[1:], f32)
        return carry

    lax.fori_loop(0, leaf_dev, prepare, 0)
    lax.fori_loop(leaves[0], leaves[1], prepare_target, 0)

    def charge_of(source):
        at = pl.multiple_of(source * leaf_size, leaf_size)
        return charges[:, pl.ds(at, leaf_size)]

    def keep(index):
        return index < leaf_dev, index

    prepared = (points, tsq, lambda s: points[s], ssq, charge_of)
    run_pairs(pool, near_count, leaves, keep, tl, sl, prepared, acc)
    for leaf in range(*leaves):
        at = (leaf - leaves[0]) * leaf_size
        out[:, at : at + leaf_size] = acc[leaf]


def near_local(pool, near_count, points, charges, leaves):
    leaf_dev, leaf_size, coords = points.shape
    rhs = charges.shape[0]
    span = leaves[1] - leaves[0]
    pairs = span * near_count / 2
    return pl.pallas_call(
        functools.partial(near_local_kernel, near_count, leaves),
        out_shape=jax.ShapeDtypeStruct((rhs, span * leaf_size), f32),
        grid_spec=pltpu.PrefetchScalarGridSpec(
            num_scalar_prefetch=1,
            grid=(1,),
            in_specs=[
                pl.BlockSpec(points.shape, lambda i, p: (0, 0, 0)),
                pl.BlockSpec(charges.shape, lambda i, p: (0, 0)),
            ],
            out_specs=pl.BlockSpec((rhs, span * leaf_size), lambda i, p: (0, 0)),
            scratch_shapes=[
                pltpu.SMEM((leaf_dev * near_count + 1,), i32),
                pltpu.SMEM((leaf_dev * near_count + 1,), i32),
                pltpu.VMEM((leaf_dev, leaf_size, LANES), f32),
                pltpu.VMEM((leaf_dev, 8, leaf_size), f32),
                pltpu.VMEM((leaf_dev, rhs, leaf_size), f32),
            ],
        ),
        compiler_params=params(),
        cost_estimate=cost(
            pairs * 2 * leaf_size * leaf_size * 4 * (coords + rhs), 3e6, pairs * leaf_size * leaf_size
        ),
        name="near_local",
    )(pool, points, charges)


def near_remote_kernel(near_count, slot, parts, pool, points, got, *refs):
    inits, (out, tl, sl, ssq, tsq, qs, acc) = refs[:parts], refs[parts:]
    leaf_dev, leaf_size, _ = points.shape
    group = got.shape[0]
    rhs = out.shape[0]

    def prepare(peer, carry):
        ssq[peer] = source_term(got[peer, :leaf_size, :])
        for tile in range(leaf_size // LANES):
            row = leaf_size + tile * rhs
            qs[peer, :, tile * LANES : (tile + 1) * LANES] = got[peer, row : row + rhs, :]
        return carry

    def prepare_target(leaf, carry):
        tsq[leaf] = target_term(points[leaf])
        acc[leaf] = jnp.zeros(acc.shape[1:], f32)
        return carry

    lax.fori_loop(0, group, prepare, 0)
    lax.fori_loop(0, leaf_dev, prepare_target, 0)

    def keep(index):
        remote = index - leaf_dev
        return (remote >= 0) & (lax.rem(remote, CAP) == slot), lax.div(remote, CAP)

    prepared = (points, tsq, lambda s: got[s, :leaf_size, :], ssq, lambda s: qs[s])
    run_pairs(pool, near_count, (0, leaf_dev), keep, tl, sl, prepared, acc)
    for leaf in range(leaf_dev):
        at = leaf * leaf_size
        total = acc[leaf]
        for init in inits:
            total = total + init[:, at : at + leaf_size]
        out[:, at : at + leaf_size] = total


def near_remote(pool, near_count, points, got, slot, inits):
    leaf_dev, leaf_size, coords = points.shape
    group = got.shape[0]
    rhs = inits[0].shape[0]
    pairs = leaf_dev * near_count / 4
    return pl.pallas_call(
        functools.partial(near_remote_kernel, near_count, slot, len(inits)),
        out_shape=jax.ShapeDtypeStruct((rhs, leaf_dev * leaf_size), f32),
        grid_spec=pltpu.PrefetchScalarGridSpec(
            num_scalar_prefetch=1,
            grid=(1,),
            in_specs=[
                pl.BlockSpec(points.shape, lambda i, p: (0, 0, 0)),
                pl.BlockSpec(got.shape, lambda i, p: (0, 0, 0)),
            ]
            + [pl.BlockSpec(init.shape, lambda i, p: (0, 0)) for init in inits],
            out_specs=pl.BlockSpec((rhs, leaf_dev * leaf_size), lambda i, p: (0, 0)),
            scratch_shapes=[
                pltpu.SMEM((leaf_dev * near_count + 1,), i32),
                pltpu.SMEM((leaf_dev * near_count + 1,), i32),
                pltpu.VMEM((group, leaf_size, LANES), f32),
                pltpu.VMEM((leaf_dev, 8, leaf_size), f32),
                pltpu.VMEM((group, rhs, leaf_size), bf16),
                pltpu.VMEM((leaf_dev, rhs, leaf_size), f32),
            ],
        ),
        compiler_params=params(),
        cost_estimate=cost(
            pairs * 2 * leaf_size * leaf_size * 4 * (coords + rhs), 5e6, pairs * leaf_size * leaf_size
        ),
        name="near_remote",
    )(pool, points, got, *inits)


def store_halves(out, row, value):
    for tile in range(value.shape[1] // LANES):
        out[row : row + value.shape[0], :] = value[:, tile * LANES : (tile + 1) * LANES]
        row += value.shape[0]
    return row


def load_halves(ref, row, rows, width):
    tiles = [ref[row + t * rows : row + (t + 1) * rows, :] for t in range(width // LANES)]
    return jnp.concatenate(tiles, axis=1)


def up_kernel(charges, leaf_interp, interp_mid, interp_top, mid_points, out, total):
    step = pl.program_id(0)

    @pl.when(step == 0)
    def _():
        total[...] = jnp.zeros_like(total)

    leaf_up = dot(charges[...], leaf_interp[0]).astype(bf16)
    total[...] += dot(leaf_up, interp_mid[...])

    @pl.when(step == pl.num_programs(0) - 1)
    def _():
        mid_up = total[...].astype(bf16)
        top = dot(mid_up, interp_top[...])
        high = top.astype(bf16)
        low = (top - high.astype(f32)).astype(bf16)
        skel = mid_points.shape[0]
        out[:skel, :] = mid_points[...]
        row = store_halves(out, skel, mid_up)
        row = store_halves(out, row, high)
        store_halves(out, row, low)


def up(charges, leaf_interp, interp_mid, interp_top, mid_points):
    leaf_dev, leaf_size, skel = leaf_interp.shape
    rhs = charges.shape[0]
    rows = skel + 3 * rhs * (skel // LANES)
    return pl.pallas_call(
        up_kernel,
        out_shape=jax.ShapeDtypeStruct((rows, LANES), bf16),
        grid=(leaf_dev,),
        in_specs=[
            pl.BlockSpec((rhs, leaf_size), lambda i: (0, i)),
            pl.BlockSpec((1, leaf_size, skel), lambda i: (i, 0, 0)),
            pl.BlockSpec((skel, skel), lambda i: (i, 0)),
            pl.BlockSpec(interp_top.shape, lambda i: (0, 0)),
            pl.BlockSpec(mid_points.shape, lambda i: (0, 0)),
        ],
        out_specs=pl.BlockSpec((rows, LANES), lambda i: (0, 0)),
        scratch_shapes=[pltpu.VMEM((rhs, skel), f32)],
        compiler_params=params(),
        cost_estimate=cost(3e8, 4e6),
        name="up",
    )(charges, leaf_interp, interp_mid, interp_top, mid_points)


def far_kernel(partners, mids, tops, interp_top, interp_mid, leaf_interp, out, total):
    step = pl.program_id(0)
    rhs, skel = total.shape

    @pl.when(step == 0)
    def _():
        def pair(source_ref, target, target_sq):
            source = source_ref[:skel, :]
            weight = load_halves(source_ref, skel, rhs, skel)
            tile = kernel_tile(source, source_term(source), target, target_sq)
            return dot(weight, tile)

        target = tops[0, :skel, :]
        target_sq = target_term(target)
        top_sum = jnp.zeros((rhs, skel), f32)
        for other in range(1, tops.shape[0]):
            top_sum = top_sum + pair(tops.at[other], target, target_sq)
        target = mids[0, :skel, :]
        target_sq = target_term(target)
        mid_sum = jnp.zeros((rhs, skel), f32)
        for at in range(partners.shape[0]):
            mid_sum = mid_sum + pair(mids.at[partners[at]], target, target_sq)
        total[...] = (mid_sum + dot_rows(top_sum.astype(bf16), interp_top[...])).astype(bf16)

    leaf_down = dot_rows(total[...], interp_mid[...]).astype(bf16)
    out[...] = dot_rows(leaf_down, leaf_interp[0])


def far(partners, mids, tops, interp_top, interp_mid, leaf_interp):
    leaf_dev, leaf_size, skel = leaf_interp.shape
    rhs = (mids.shape[1] - skel) // (3 * (skel // LANES))
    return pl.pallas_call(
        far_kernel,
        out_shape=jax.ShapeDtypeStruct((rhs, leaf_dev * leaf_size), f32),
        grid_spec=pltpu.PrefetchScalarGridSpec(
            num_scalar_prefetch=1,
            grid=(leaf_dev,),
            in_specs=[
                pl.BlockSpec(mids.shape, lambda i, p: (0, 0, 0)),
                pl.BlockSpec(tops.shape, lambda i, p: (0, 0, 0)),
                pl.BlockSpec(interp_top.shape, lambda i, p: (0, 0)),
                pl.BlockSpec((skel, skel), lambda i, p: (i, 0)),
                pl.BlockSpec((1, leaf_size, skel), lambda i, p: (i, 0, 0)),
            ],
            out_specs=pl.BlockSpec((rhs, leaf_size), lambda i, p: (0, i)),
            scratch_shapes=[pltpu.VMEM((rhs, skel), bf16)],
        ),
        compiler_params=params(),
        cost_estimate=cost(1e9, 6e6, 5e5),
        name="far",
    )(partners, mids, tops, interp_top, interp_mid, leaf_interp)


def share(value, axis, size):
    gathered = value[None]
    bit = size // 2
    while bit:
        swap = [(i, i ^ bit) for i in range(size)]
        other = lax.ppermute(gathered, axis, swap)
        gathered = jnp.stack((gathered, other), axis=1).reshape((-1,) + value.shape)
        bit //= 2
    return gathered


def body(
    points,
    charges,
    near_leaves,
    leaf_interpolant,
    skel_leaf,
    interp_mid,
    skel_mid,
    mid_partners,
    interp_top,
    skel_top,
):
    group = lax.axis_size("sub")
    groups = lax.axis_size("leaf")
    self_index = lax.axis_index("sub")
    leaf_dev, leaf_size, skel = leaf_interpolant.shape
    coords = points.shape[1]
    rhs = charges.shape[1]
    near_count = near_leaves.shape[1]
    group_first = lax.axis_index("leaf") * group
    blocks = points.reshape(leaf_dev, leaf_size, coords)
    charges_t = charges.T

    where = jnp.stack((group_first * leaf_dev, self_index)).astype(i32)
    chosen, pool = want(near_leaves, where, leaf_dev, group)
    handed = lax.all_to_all(chosen, "sub", split_axis=0, concat_axis=0, tiled=True)

    leaf_of = skel_mid[0] // skel
    rows = skel_leaf.reshape(-1)[skel_mid[0]] + leaf_of * leaf_size
    mid_points = points[rows]
    message = up(charges_t, leaf_interpolant, interp_mid[0], interp_top[0], mid_points)

    asked = pack(handed, blocks, charges_t)
    got = [lax.all_to_all(a, "sub", split_axis=0, concat_axis=0, tiled=True) for a in asked]

    half = leaf_dev // 2
    near_parts = [
        near_local(pool, near_count, blocks, charges_t, span)
        for span in ((0, half), (half, leaf_dev))
    ]

    mids = share(message, "sub", group)
    per = rhs * (skel // LANES)
    picked = skel_top[0]
    place = jnp.bitwise_xor(picked // skel, self_index) * mids.shape[1] + picked % skel
    top_points = mids.reshape(-1, LANES)[place]
    parts = mids[:, skel + per :, :].astype(f32)
    top_weight = jnp.sum(parts[:, :per, :] + parts[:, per:, :], axis=0).astype(bf16)
    tops = share(jnp.concatenate((top_points, top_weight), axis=0), "leaf", groups)

    partners = jnp.bitwise_xor(mid_partners[0] - group_first, self_index)
    distant = far(partners, mids, tops, interp_top[0], interp_mid[0], leaf_interpolant)
    near = jnp.concatenate(near_parts, axis=1)
    near = near_remote(pool, near_count, blocks, got[0], 0, (near,))
    return near_remote(pool, near_count, blocks, got[1], 1, (near, distant)).T


def solution(mesh):
    placed = (
        P(("leaf", "sub"), None),
        P(("leaf", "sub"), None),
        P(("leaf", "sub"), None),
        P(("leaf", "sub"), None, None),
        P(("leaf", "sub"), None),
        P(("leaf", "sub"), None, None),
        P(("leaf", "sub"), None),
        P(("leaf", "sub"), None),
        P("leaf", "sub", None),
        P("leaf", None),
    )
    return jax.shard_map(
        body, mesh=mesh, in_specs=placed, out_specs=P(("leaf", "sub"), None), check_vma=False
    )
```

time: 673 us -> 160 us (0.24)
  matrix products: 227 us -> 0 us
  loops' own time: 178 us -> 0 us
  blocking collectives: 171 us -> 13.7 us
  Pallas kernels: 0 us -> 85.1 us
  local copies, waits for them, and re-layouts: 44.4 us -> 6.21 us
  waiting for transfers between devices: 0.01 us -> 32.6 us
  other arithmetic: 35.6 us -> 3.62 us
    dot_general x103 -> x0, matrix products: 227 us -> none  [the longest x96 216 us: near_leaf(): jnp.dot(kernel, weights, preferred_element_type=jnp.float32)]
    another operation x1 -> x0, loops' own time: 178 us -> none  [body(): lax.fori_loop(0, leaf_dev, near_leaf, jnp.zeros((leaf_dev, leaf_size, rhs...]
    all_gather x5 -> x0, blocking collectives: 109 us -> none  [the longest x1 33 us: body(): shard_weights = lax.all_gather(mid_up[None], 'sub', axis=0, tiled=True)]
    pallas_call x0 -> x8, Pallas kernels: none -> 85.1 us  [the longest x2 34.1 us: near_remote(): pl.pallas_call(functools.partial(near_remote_kernel, near_count, slot, le...]
    psum x1 -> x0, blocking collectives: 61.6 us -> none  [body(): top_weight, top_points = lax.psum((top_part, top_rows), 'sub')]
    ppermute x0 -> x5, waiting for transfers between devices: none -> 32.6 us  [share(): other = lax.ppermute(gathered, axis, swap)]
    gather x7 -> x3, local copies, waits for them, and re-layouts: 31.2 us -> 4.03 us  [the longest x1 1.72 us: body(): rows = skel_leaf.reshape(-1)[skel_mid[0]] + leaf_of * leaf_size]
    reduce_sum x14 -> x1, other arithmetic: 23.5 us -> 0.05 us  [body(): jnp.sum(parts[:, :per, :] + parts[:, per:, :], axis=0).astype(bf16)]
  transfers between devices with their start and end apart: 2 -> 7, of which waited for: 0 -> 3; matrix products, arithmetic and copies ran while one was open for 7% -> 5% of each run, Pallas kernels for 0% -> 39%
where the time goes in v1:
time: 160 us; the launch traced here: 158 us
  Pallas kernels  85.1 us (53%)
  waiting for transfers between devices  32.6 us (20%)
  starting transfers between devices  16.7 us (10%)
  blocking collectives  13.7 us (9%)
  local copies, waits for them, and re-layouts  6.21 us (4%)
  other arithmetic  3.62 us (2%)
    pallas_call x2, Pallas kernels, near_remote(): pl.pallas_call(functools.partial(near_remote_kernel, near_count, slot, le...  34.1 us
    ppermute x5, waiting for transfers between devices, share(): other = lax.ppermute(gathered, axis, swap)  32.6 us
    pallas_call x2, Pallas kernels, near_local(): pl.pallas_call(functools.partial(near_local_kernel, near_count, leaves),...  27.9 us
    all_to_all x1, blocking collectives, body(): lax.all_to_all(chosen, 'sub', split_axis=0, concat_axis=0, tiled=True)  13.7 us
    pallas_call x1, Pallas kernels, far(): pl.pallas_call(far_kernel, out_shape=jax.ShapeDtypeStruct((rhs, leaf_dev...  9.91 us
    all_to_all x2, starting transfers between devices, body(): lax.all_to_all(a, 'sub', split_axis=0, concat_axis=0, tiled=True)  9.8 us
    ppermute x5, starting transfers between devices, share(): other = lax.ppermute(gathered, axis, swap)  6.89 us
    pallas_call x1, Pallas kernels, up(): pl.pallas_call(up_kernel, out_shape=jax.ShapeDtypeStruct((rows, LANES), b...  6.75 us
  transfers between devices with their start and end apart: 7, of which 3 were waited for; matrix products, arithmetic and copies ran while one was open for 5% of the time, Pallas kernels for 39%

profile of v1, /device:TPU:0, one launch (start us, length us, event | category | flops | bytes accessed | tf_op | source)
XLA Modules:
  0.0 158.1 jit_solution(2957433200660141171)
XLA Ops:
  0.0 0.6 pad_add_fusion.where
  0.6 2.3 %want.1 = (s32[8,8]{1,0:T(8,128)}, s32[8,128]{1,0:T(8,128)}) custom-call(s32[2]{0:T(128)} %pad_add_fusion.where, s32[8,12]{1,0:T(8,128)} %near.1), custom_call_target="tpu_custom_call" | custom-call | flops 1000000 | bytes 100000 | tf_op jit(solution)/shard_map/want/pallas_call | solution.py:112
  3.0 13.7 %all_to_all.21 = s32[8,1,8]{2,1,0:T(1,128)} all-to-all(s32[8,1,8]{2,1,0:T(1,128)} %bitcast.101), channel_id=1, replica_groups=mesh['leaf'=4,'sub'=8] {'sub'}, dimensions={0} | all-to-all | bytes 512 | tf_op jit(solution)/shard_map/all_to_all | solution.py:485
  16.6 4.1 %pack.1 = (bf16[8,768,128]{2,1,0:T(8,128)(2,1)}, bf16[8,768,128]{2,1,0:T(8,128)(2,1)}) custom-call(s32[8,8]{1,0:T(8,128)} %bitcast.96, bf16[8,512,128]{2,1,0:T(8,128)(2,1)} %bitcast.77, bf16[64,4096]{1,0:T(8,128)(2,1)} %bitcast.82), custom_call_target="tpu_custom_call" | custom-call | flops 100000 | bytes 8000000 | tf_op jit(solution)/shard_map/pack/pallas_call | solution.py:155
  20.8 0.0 copy-start.6
  20.8 0.0 copy-start.5
  20.8 4.4 %all-to-all-start.2 = ((bf16[8,768,128]{2,1,0:T(8,128)(2,1)}), bf16[8,768,128]{2,1,0:T(8,128)(2,1)}, u32[]{:S(2)}, u32[]{:S(2)}) async-start(bf16[8,768,128]{2,1,0:T(8,128)(2,1)} %get-tuple-element.12), calls=%async_computation.2 | async-start | bytes 3145728 | tf_op jit(solution)/shard_map/all_to_all | solution.py:493
  25.2 0.0 copy-done.6
  25.2 0.0 copy-start.1
  25.2 0.0 copy-done.5
  25.3 1.7 %gather_fusion = s32[256]{0:T(256)S(1)} fusion(s32[2048]{0:T(1024)S(1)} %bitcast.69, s32[1024]{0:T(1024)S(1)} %pad_clamp_fusion.2), kind=kCustom, calls=%fused_computation | custom fusion | bytes 3072 | tf_op jit(solution)/shard_map/gather | solution.py:488
  27.0 0.0 copy-done.1
  27.0 1.5 gather_fusion.1
  28.5 6.8 %up.1 = bf16[640,128]{1,0:T(8,128)(2,1)} custom-call(bf16[64,4096]{1,0:T(8,128)(2,1)} %bitcast.83, bf16[8,512,256]{2,1,0:T(8,128)(2,1)} %leaf_interp.3, bf16[2048,256]{1,0:T(8,128)(2,1)} %bitcast.73, bf16[256,256]{1,0:T(8,128)(2,1)} %bitcast.90, bf16[256,128]{1,0:T(8,128)(2,1)} %gather_fusion.1), custom_call_target="tpu_custom_call" | custom-call | flops 300000000 | bytes 4000000 | tf_op jit(solution)/shard_map/up/pallas_call | solution.py:377
  35.3 2.8 %collective-permute-start = (bf16[1,640,128]{2,1,0:T(8,128)(2,1)}, bf16[1,640,128]{2,1,0:T(8,128)(2,1)S(1)}, u32[]{:S(2)}, u32[]{:S(2)}) collective-permute-start(bf16[1,640,128]{2,1,0:T(8,128)(2,1)} %bitcast.88), channel_id=1, source_target_pairs={{0,4},{1,5},{2,6},{3,7},{4,0},{5,1},{6,2},{7,3},{8,12},{9,13},{10,... | collective-permute-start | bytes 491528 | tf_op jit(solution)/shard_map/ppermute | solution.py:454
  38.0 30.2 %collective-permute-done = bf16[1,640,128]{2,1,0:T(8,128)(2,1)S(1)} collective-permute-done((bf16[1,640,128]{2,1,0:T(8,128)(2,1)}, bf16[1,640,128]{2,1,0:T(8,128)(2,1)S(1)}, u32[]{:S(2)}, u32[]{:S(2)}) %collective-permute-start) | collective-permute-done | bytes 163872 | tf_op jit(solution)/shard_map/ppermute | solution.py:454
  68.2 1.0 fusion.2
  69.2 0.1 collective-permute-start.1
  69.2 13.9 %near_local.3 = f32[64,2048]{1,0:T(8,128)} custom-call(s32[8,128]{1,0:T(8,128)} %get-tuple-element.9.pool, bf16[8,512,128]{2,1,0:T(8,128)(2,1)} %bitcast.78, bf16[64,4096]{1,0:T(8,128)(2,1)} %bitcast.84), custom_call_target="tpu_custom_call" | custom-call | flops 9663676416 | bytes 3000000 | tf_op jit(solution)/shard_map/near_local/pallas_call | solution.py:242
  83.2 0.0 collective-permute-done.1
  83.2 0.1 pad_maximum_fusion.2
  83.3 0.5 collective-permute-start.2
  83.8 14.0 %near_local.2 = f32[64,2048]{1,0:T(8,128)} custom-call(s32[8,128]{1,0:T(8,128)} %get-tuple-element.9.pool, bf16[8,512,128]{2,1,0:T(8,128)(2,1)} %bitcast.79, bf16[64,4096]{1,0:T(8,128)(2,1)} %bitcast.85), custom_call_target="tpu_custom_call" | custom-call | flops 9663676416 | bytes 3000000 | tf_op jit(solution)/shard_map/near_local/pallas_call | solution.py:242
  97.8 0.0 all-to-all-done.2.got
  97.8 0.0 copy-start.7
  97.8 5.4 %all-to-all-start.1 = ((bf16[8,768,128]{2,1,0:T(8,128)(2,1)}), bf16[8,768,128]{2,1,0:T(8,128)(2,1)S(1)}, u32[]{:S(2)}, u32[]{:S(2)}) async-start(bf16[8,768,128]{2,1,0:T(8,128)(2,1)} %get-tuple-element.11), calls=%async_computation.1 | async-start | bytes 3145728 | tf_op jit(solution)/shard_map/all_to_all | solution.py:493
  103.2 0.0 copy-done.7
  103.3 0.0 collective-permute-done.2
  103.3 0.1 pad_maximum_fusion
  103.4 0.1 copy.20
  103.5 0.0 copy-start
  103.5 0.9 gather_fusion.2
  104.4 0.0 copy-start.3
  104.4 0.0 copy-start.4
  104.4 0.1 slice_convert_fusion
  104.5 0.1 fusion
  104.5 0.0 copy-done
  104.6 0.0 copy-start.8
  104.6 3.4 %collective-permute-start.3 = (bf16[1,384,128]{2,1,0:T(8,128)(2,1)S(1)}, bf16[1,384,128]{2,1,0:T(8,128)(2,1)S(1)}, u32[]{:S(2)}, u32[]{:S(2)}) collective-permute-start(bf16[1,384,128]{2,1,0:T(8,128)(2,1)S(1)} %get-tuple-element.18), channel_id=1, source_target_pairs={{0,16},{8,24},{16,0},{24,8},{1,17},{9,25},{17,1},{25,9},{2,18},{10... | collective-permute-start | bytes 294920 | tf_op jit(solution)/shard_map/ppermute | solution.py:454
  108.0 0.0 copy-done.3
  108.0 0.0 copy-done.4
  108.0 1.0 pad_maximum_fusion.1.refs_0_
  109.1 1.5 collective-permute-done.3
  110.6 0.1 collective-permute-start.4
  110.7 0.0 copy-done.8
  110.7 0.5 xor_bitcast_fusion.partners
  111.3 0.9 collective-permute-done.4
  112.2 0.8 copy.22
  113.0 9.9 %far.1.refs_1_ = f32[64,4096]{1,0:T(8,128)} custom-call(s32[4]{0:T(128)} %xor_bitcast_fusion.partners, bf16[8,640,128]{2,1,0:T(8,128)(2,1)} %bitcast.72, bf16[4,384,128]{2,1,0:T(8,128)(2,1)} %bitcast.86, bf16[256,256]{1,0:T(8,128)(2,1)} %bitcast.91, bf16[2048,256]{1,0:T(8,128)(2,1)} %bitcast.74, bf16[8,512,256]{2,1,0:T(8,128)(2,1)} %leaf_interp.3), custom_call_target="tpu_custom_call" | custom-call | flops 1000000000 | bytes 6000000 | tf_op jit(solution)/shard_map/far/pallas_call | solution.py:427
  122.9 17.4 %near_remote.2.refs_0_ = f32[64,4096]{1,0:T(8,128)} custom-call(s32[8,128]{1,0:T(8,128)} %get-tuple-element.9.pool, bf16[8,512,128]{2,1,0:T(8,128)(2,1)} %bitcast.80, bf16[8,768,128]{2,1,0:T(8,128)(2,1)} %all-to-all-done.2.got, f32[64,4096]{1,0:T(8,128)} %pad_maximum_fusion.1.refs_0_), custom_call_target="tpu_custom_call" | custom-call | flops 9663676416 | bytes 5000000 | tf_op jit(solution)/shard_map/near_remote/pallas_call | solution.py:309
  140.3 0.0 all-to-all-done.1.got
  140.3 0.0 copy-start.2
  140.3 1.2 copy-done.2
  141.4 16.7 %near_remote.3 = f32[64,4096]{1,0:T(8,128)} custom-call(s32[8,128]{1,0:T(8,128)} %get-tuple-element.9.pool, bf16[8,512,128]{2,1,0:T(8,128)(2,1)} %bitcast.81, bf16[8,768,128]{2,1,0:T(8,128)(2,1)} %copy-done.2, f32[64,4096]{1,0:T(8,128)} %near_remote.2.refs_0_, f32[64,4096]{1,0:T(8,128)} %far.1.refs_1_), custom_call_target="tpu_custom_call" | custom-call | flops 9663676416 | bytes 5000000 | tf_op jit(solution)/shard_map/near_remote/pallas_call | solution.py:309
  (11 shorter events, 0.2 us)
Async XLA Ops:
  20.8 4.4 %copy-start.6 = (s32[1,256]{1,0:T(1,128)S(1)}, s32[1,256]{1,0:T(1,128)}, u32[]{:S(2)}) copy-start(s32[1,256]{1,0:T(1,128)} %param.16) | copy-start | bytes 3076
  20.8 4.5 %copy-start.5 = (s32[8,256]{1,0:T(8,128)S(1)}, s32[8,256]{1,0:T(8,128)}, u32[]{:S(2)}) copy-start(s32[8,256]{1,0:T(8,128)} %param.14) | copy-start | bytes 24580
  20.8 77.1 %all-to-all-start.2 = ((bf16[8,768,128]{2,1,0:T(8,128)(2,1)}), bf16[8,768,128]{2,1,0:T(8,128)(2,1)}, u32[]{:S(2)}, u32[]{:S(2)}) async-start(bf16[8,768,128]{2,1,0:T(8,128)(2,1)} %get-tuple-element.12), calls=%async_computation.2 | async-start | bytes 3145728 | tf_op jit(solution)/shard_map/all_to_all | solution.py:493
  25.2 1.8 %copy-start.1 = (bf16[4096,128]{1,0:T(8,128)(2,1)S(1)}, bf16[4096,128]{1,0:T(8,128)(2,1)}, u32[]{:S(2)}) copy-start(bf16[4096,128]{1,0:T(8,128)(2,1)} %param.10) | copy-start | bytes 3145732
  35.3 32.9 %collective-permute-start = (bf16[1,640,128]{2,1,0:T(8,128)(2,1)}, bf16[1,640,128]{2,1,0:T(8,128)(2,1)S(1)}, u32[]{:S(2)}, u32[]{:S(2)}) collective-permute-start(bf16[1,640,128]{2,1,0:T(8,128)(2,1)} %bitcast.88), channel_id=1, source_target_pairs={{0,4},{1,5},{2,6},{3,7},{4,0},{5,1},{6,2},{7,3},{8,12},{9,13},{10,... | collective-permute-start | bytes 491528 | tf_op jit(solution)/shard_map/ppermute | solution.py:454
  69.2 14.0 %collective-permute-start.1 = (bf16[2,640,128]{2,1,0:T(8,128)(2,1)S(1)}, bf16[2,640,128]{2,1,0:T(8,128)(2,1)S(1)}, u32[]{:S(2)}, u32[]{:S(2)}) collective-permute-start(bf16[2,640,128]{2,1,0:T(8,128)(2,1)S(1)} %get-tuple-element.14), channel_id=1, source_target_pairs={{0,2},{1,3},{2,0},{3,1},{4,6},{5,7},{6,4},{7,5},{8,10},{9,11},{10,... | collective-permute-start | bytes 983048 | tf_op jit(solution)/shard_map/ppermute | solution.py:454
  83.3 20.0 %collective-permute-start.2 = (bf16[4,640,128]{2,1,0:T(8,128)(2,1)S(1)}, bf16[4,640,128]{2,1,0:T(8,128)(2,1)S(1)}, u32[]{:S(2)}, u32[]{:S(2)}) collective-permute-start(bf16[4,640,128]{2,1,0:T(8,128)(2,1)S(1)} %bitcast.75), channel_id=1, source_target_pairs={{0,1},{1,0},{2,3},{3,2},{4,5},{5,4},{6,7},{7,6},{8,9},{9,8},{10,11... | collective-permute-start | bytes 1966088 | tf_op jit(solution)/shard_map/ppermute | solution.py:454
  97.8 5.4 %copy-start.7 = (s32[1,256]{1,0:T(1,128)S(1)}, s32[1,256]{1,0:T(1,128)}, u32[]{:S(2)}) copy-start(s32[1,256]{1,0:T(1,128)} %param.19) | copy-start | bytes 3076
  97.8 42.4 %all-to-all-start.1 = ((bf16[8,768,128]{2,1,0:T(8,128)(2,1)}), bf16[8,768,128]{2,1,0:T(8,128)(2,1)S(1)}, u32[]{:S(2)}, u32[]{:S(2)}) async-start(bf16[8,768,128]{2,1,0:T(8,128)(2,1)} %get-tuple-element.11), calls=%async_computation.1 | async-start | bytes 3145728 | tf_op jit(solution)/shard_map/all_to_all | solution.py:493
  103.5 1.1 copy-start
  104.4 3.7 %copy-start.3 = (f32[64,2048]{1,0:T(8,128)S(1)}, f32[64,2048]{1,0:T(8,128)}, u32[]{:S(2)}) copy-start(f32[64,2048]{1,0:T(8,128)} %near_local.3) | copy-start | bytes 1572868
  104.4 3.7 %copy-start.4 = (f32[64,2048]{1,0:T(8,128)S(1)}, f32[64,2048]{1,0:T(8,128)}, u32[]{:S(2)}) copy-start(f32[64,2048]{1,0:T(8,128)} %near_local.2) | copy-start | bytes 1572868
  104.6 6.1 %copy-start.8 = (s32[1,4]{1,0:T(1,128)S(1)}, s32[1,4]{1,0:T(1,128)}, u32[]{:S(2)}) copy-start(s32[1,4]{1,0:T(1,128)} %param.17) | copy-start | bytes 52
  104.6 6.0 %collective-permute-start.3 = (bf16[1,384,128]{2,1,0:T(8,128)(2,1)S(1)}, bf16[1,384,128]{2,1,0:T(8,128)(2,1)S(1)}, u32[]{:S(2)}, u32[]{:S(2)}) collective-permute-start(bf16[1,384,128]{2,1,0:T(8,128)(2,1)S(1)} %get-tuple-element.18), channel_id=1, source_target_pairs={{0,16},{8,24},{16,0},{24,8},{1,17},{9,25},{17,1},{25,9},{2,18},{10... | collective-permute-start | bytes 294920 | tf_op jit(solution)/shard_map/ppermute | solution.py:454
  110.6 1.5 collective-permute-start.4
  140.3 1.2 copy-start.2

commit v2 on v1

v2 whole, which is shorter than its diff:
```python
import functools
import math

import jax
import jax.numpy as jnp
from jax import lax
from jax.experimental import pallas as pl
from jax.experimental.pallas import tpu as pltpu
from jax.sharding import PartitionSpec as P


CAP = 2
UNROLL = 4
LANES = 128
kernel_rate = 0.25
LOG2E = math.log2(math.e)
bf16 = jnp.bfloat16
f32 = jnp.float32
i32 = jnp.int32

ROWS_ROWS = (((1,), (1,)), ((), ()))


def dot(a, b):
    return jnp.dot(a, b, preferred_element_type=f32)


def dot_rows(a, b):
    return lax.dot_general(a, b, ROWS_ROWS, preferred_element_type=f32)


def squares(x):
    xf = x.astype(f32)
    sq = xf * xf
    high = sq.astype(bf16)
    low = (sq - high.astype(f32)).astype(bf16)
    return high, low


def source_term(x):
    high, low = squares(x)
    ones = jnp.ones((x.shape[1], LANES), bf16)
    return (dot(high, ones) + dot(low, ones)) * (-kernel_rate * LOG2E)


def target_term(x):
    high, low = squares(x)
    ones = jnp.ones((8, x.shape[1]), bf16)
    return (dot_rows(ones, high) + dot_rows(ones, low)) * (-kernel_rate * LOG2E)


def kernel_tile(source, source_sq, target, target_sq):
    products = dot_rows(source, target)
    columns = []
    for at in range(0, target.shape[0], LANES):
        exponent = products[:, at : at + LANES] * (2.0 * kernel_rate * LOG2E) + (
            source_sq + target_sq[0:1, at : at + LANES]
        )
        columns.append(jnp.exp2(exponent).astype(bf16))
    return jnp.concatenate(columns, axis=1)


def cost(flops, bytes_accessed, transcendentals=0):
    return pl.CostEstimate(
        flops=int(flops), bytes_accessed=int(bytes_accessed), transcendentals=int(transcendentals)
    )


def room(shapes):
    total = 0
    for shape in shapes:
        count = shape.dtype.itemsize * math.prod(shape.shape[:-1])
        total += count * -(-shape.shape[-1] // LANES) * LANES
    return total


def call(kernel, out_shape, in_specs, estimate, operands, scratch=(), own=0):
    outs = out_shape if isinstance(out_shape, (tuple, list)) else [out_shape]
    grant = room(operands) + room(outs) + own + (2 << 20)
    return pl.pallas_call(
        kernel,
        out_shape=out_shape,
        in_specs=in_specs,
        out_specs=[vmem()] * len(outs) if outs is out_shape else vmem(),
        scratch_shapes=list(scratch),
        compiler_params=pltpu.CompilerParams(vmem_limit_bytes=grant),
        cost_estimate=estimate,
    )(*operands)


def vmem():
    return pl.BlockSpec(memory_space=pltpu.VMEM)


def smem():
    return pl.BlockSpec(memory_space=pltpu.SMEM)


def want_kernel(leaf_dev, group, where, near, chosen, pool):
    base, self_index = where[0], where[1]
    rows, near_count = near.shape
    width = max(LANES, group * leaf_dev)
    local = near[...] - base
    lane = lax.broadcasted_iota(i32, (rows, width), 1)
    member = lax.rem(lane, leaf_dev)
    owner = lax.div(lane, leaf_dev)
    named = jnp.zeros((rows, width), f32)
    for entry in range(near_count):
        named = jnp.maximum(named, (local[:, entry : entry + 1] == lane).astype(f32))
    wanted = jnp.max(named, axis=0, keepdims=True)
    wanted = jnp.where(owner == self_index, 0.0, jnp.broadcast_to(wanted, (rows, width)))
    row_id = lax.broadcasted_iota(i32, (width, width), 0)
    col_id = lax.broadcasted_iota(i32, (width, width), 1)
    before = (lax.div(row_id, leaf_dev) == lax.div(col_id, leaf_dev)) & (row_id < col_id)
    rank = dot(wanted.astype(bf16), before.astype(f32).astype(bf16))
    slot = lax.broadcasted_iota(i32, (rows, width), 0).astype(f32)
    picked = jnp.where((wanted > 0.0) & (rank == slot), member.astype(f32), 0.0)
    owner_row = lax.broadcasted_iota(i32, (group, width), 0)
    owner_of = lax.div(lax.broadcasted_iota(i32, (group, width), 1), leaf_dev)
    belongs = (owner_row == owner_of).astype(f32).astype(bf16)
    chosen[...] = dot_rows(belongs, picked.astype(bf16)).astype(i32)
    place = jnp.zeros((rows, LANES), i32)
    short_lane = lax.broadcasted_iota(i32, (rows, LANES), 1)
    for entry in range(near_count):
        ids = local[:, entry : entry + 1]
        at = jnp.sum(jnp.where(ids == lane, rank, 0.0), axis=1, keepdims=True).astype(i32)
        distance = jnp.bitwise_xor(lax.div(ids, leaf_dev), self_index)
        index = jnp.where(
            distance == 0,
            lax.rem(ids, leaf_dev),
            leaf_dev + distance * CAP + jnp.clip(at, 0, CAP - 1),
        )
        place = jnp.where(short_lane == entry, index, place)
    pool[...] = place


def want(near_leaves, where, leaf_dev, group):
    rows = near_leaves.shape[0]
    return call(
        functools.partial(want_kernel, leaf_dev, group),
        [jax.ShapeDtypeStruct((group, rows), i32), jax.ShapeDtypeStruct((rows, LANES), i32)],
        [smem(), vmem()],
        cost(1e6, 1e5),
        (where, near_leaves),
    )


def pack_kernel(leaf_size, where, handed, points, charges, *outs):
    self_index = where[1]
    rhs = charges.shape[0]
    for at, out in enumerate(outs):
        peer = jnp.bitwise_xor(self_index, at + 1)
        for slot in range(CAP):
            leaf = handed[peer, slot]
            out[slot, :leaf_size, :] = points[leaf]
            for tile in range(leaf_size // LANES):
                lane = pl.multiple_of(leaf * leaf_size + tile * LANES, LANES)
                row = leaf_size + tile * rhs
                out[slot, row : row + rhs, :] = charges[:, pl.ds(lane, LANES)]


def pack(where, handed, points, charges):
    _, leaf_size, coords = points.shape
    group = handed.shape[0]
    rows = leaf_size + leaf_size // LANES * charges.shape[0]
    return call(
        functools.partial(pack_kernel, leaf_size),
        [jax.ShapeDtypeStruct((CAP, rows, coords), bf16) for _ in range(group - 1)],
        [smem(), smem(), vmem(), vmem()],
        cost(1e5, 8e6),
        (where, handed, points, charges),
    )


def run_pairs(pool, near_count, leaves, keep, tl, sl, tile_of, charge_of, acc):
    def scan(leaf, count):
        for entry in range(near_count):
            kept, source = keep(pool[leaf, entry])
            tl[count] = leaf
            sl[count] = source
            count = count + kept.astype(i32)
        return count

    count = lax.fori_loop(leaves[0], leaves[1], scan, jnp.int32(0))

    def one(at):
        target, source = tl[at], sl[at]
        acc[target] += dot(charge_of(source), tile_of(target, source))

    def several(step, carry):
        for k in range(UNROLL):
            one(step * UNROLL + k)
        return carry

    def single(at, carry):
        one(at)
        return carry

    whole = lax.div(count, UNROLL)
    lax.fori_loop(0, whole, several, 0)
    lax.fori_loop(whole * UNROLL, count, single, 0)


def near_cost(pairs, leaf_size, coords, rhs):
    return cost(
        pairs * 2 * leaf_size * leaf_size * 4 * (coords + rhs), 3e6, pairs * leaf_size * leaf_size
    )


def near_local_kernel(near_count, leaves, pool, points, charges, *refs):
    if leaves[0] == 0:
        out, tsq, tl, sl, ssq, acc = refs
    else:
        tsq, out, tl, sl, ssq, acc = refs
    leaf_dev, leaf_size, _ = points.shape

    def prepare(leaf, carry):
        ssq[leaf] = source_term(points[leaf])
        if leaves[0] == 0:
            tsq[leaf] = target_term(points[leaf])
        return carry

    lax.fori_loop(0, leaf_dev, prepare, 0)
    for leaf in range(*leaves):
        acc[leaf] = jnp.zeros(acc.shape[1:], f32)

    def charge_of(source):
        at = pl.multiple_of(source * leaf_size, leaf_size)
        return charges[:, pl.ds(at, leaf_size)]

    def tile_of(target, source):
        return kernel_tile(points[source], ssq[source], points[target], tsq[target])

    def keep(index):
        return index < leaf_dev, index

    run_pairs(pool, near_count, leaves, keep, tl, sl, tile_of, charge_of, acc)
    for leaf in range(*leaves):
        at = (leaf - leaves[0]) * leaf_size
        out[:, at : at + leaf_size] = acc[leaf]


def near_local(pool, near_count, points, charges, leaves, *tsq):
    leaf_dev, leaf_size, coords = points.shape
    rhs = charges.shape[0]
    span = leaves[1] - leaves[0]
    result = jax.ShapeDtypeStruct((rhs, span * leaf_size), f32)
    terms = jax.ShapeDtypeStruct((leaf_dev, 8, leaf_size), f32)
    return call(
        functools.partial(near_local_kernel, near_count, leaves),
        result if tsq else [result, terms],
        [smem(), vmem(), vmem()] + [vmem()] * len(tsq),
        near_cost(span * near_count / 2, leaf_size, coords, rhs),
        (pool, points, charges) + tsq,
        scratch=[
            pltpu.SMEM((leaf_dev * near_count + 1,), i32),
            pltpu.SMEM((leaf_dev * near_count + 1,), i32),
            pltpu.VMEM((leaf_dev, leaf_size, LANES), f32),
            pltpu.VMEM((leaf_dev, rhs, leaf_size), f32),
        ],
        own=leaf_dev * leaf_size * (rhs + LANES) * 4 + (1 << 20),
    )


def near_remote_kernel(near_count, first, parts, extra, pool, points, tsq, *refs):
    got, inits, refs = refs[:parts], refs[parts : parts + extra], refs[parts + extra :]
    out, tl, sl, pts, ssq, qs, acc = refs
    leaf_dev, leaf_size, _ = points.shape
    rhs = out.shape[0]

    for part, message in enumerate(got):
        def prepare(slot, carry, part=part, message=message):
            place = part * CAP + slot
            x = message[slot, :leaf_size, :]
            pts[place] = x
            ssq[place] = source_term(x)
            for tile in range(leaf_size // LANES):
                row = leaf_size + tile * rhs
                qs[place, :, tile * LANES : (tile + 1) * LANES] = message[slot, row : row + rhs, :]
            return carry

        lax.fori_loop(0, CAP, prepare, 0)

    width = 0
    for init in inits:
        span = init.shape[1] // leaf_size
        for leaf in range(span):
            value = init[:, leaf * leaf_size : (leaf + 1) * leaf_size]
            target = (width + leaf) % leaf_dev
            if width + leaf < leaf_dev:
                acc[target] = value
            else:
                acc[target] += value
        width += span

    low = leaf_dev + first * CAP

    def keep(index):
        return (index >= low) & (index < low + parts * CAP), index - low

    def tile_of(target, source):
        return kernel_tile(pts[source], ssq[source], points[target], tsq[target])

    run_pairs(
        pool, near_count, (0, leaf_dev), keep, tl, sl, tile_of, lambda s: qs[s], acc
    )
    for leaf in range(leaf_dev):
        out[:, leaf * leaf_size : (leaf + 1) * leaf_size] = acc[leaf]


def near_remote(pool, near_count, points, tsq, first, got, inits):
    leaf_dev, leaf_size, coords = points.shape
    rhs = inits[0].shape[0]
    places = len(got) * CAP
    return call(
        functools.partial(near_remote_kernel, near_count, first, len(got), len(inits)),
        jax.ShapeDtypeStruct((rhs, leaf_dev * leaf_size), f32),
        [smem(), vmem(), vmem()] + [vmem()] * (len(got) + len(inits)),
        near_cost(len(got) * leaf_dev, leaf_size, coords, rhs),
        (pool, points, tsq, *got, *inits),
        scratch=[
            pltpu.SMEM((leaf_dev * near_count + 1,), i32),
            pltpu.SMEM((leaf_dev * near_count + 1,), i32),
            pltpu.VMEM((places, leaf_size, coords), bf16),
            pltpu.VMEM((places, leaf_size, LANES), f32),
            pltpu.VMEM((places, rhs, leaf_size), bf16),
            pltpu.VMEM((leaf_dev, rhs, leaf_size), f32),
        ],
        own=(leaf_dev * rhs * 4 + places * (coords * 2 + LANES * 4 + rhs * 2)) * leaf_size
        + (2 << 20),
    )


def store_halves(out, row, value):
    for tile in range(value.shape[1] // LANES):
        out[row : row + value.shape[0], :] = value[:, tile * LANES : (tile + 1) * LANES]
        row += value.shape[0]
    return row


def load_halves(ref, row, rows, width):
    tiles = [ref[row + t * rows : row + (t + 1) * rows, :] for t in range(width // LANES)]
    return jnp.concatenate(tiles, axis=1)


def up_kernel(charges, leaf_interp, interp_mid, interp_top, mid_points, out):
    leaf_dev, leaf_size, skel = leaf_interp.shape
    total = jnp.zeros((charges.shape[0], skel), f32)
    for leaf in range(leaf_dev):
        block = charges[:, leaf * leaf_size : (leaf + 1) * leaf_size]
        leaf_up = dot(block, leaf_interp[leaf]).astype(bf16)
        total = total + dot(leaf_up, interp_mid[leaf * skel : (leaf + 1) * skel, :])
    mid_up = total.astype(bf16)
    top = dot(mid_up, interp_top[...])
    out[:skel, :] = mid_points[...]
    row = store_halves(out, skel, mid_up)
    store_halves(out, row, top.astype(bf16))


def up(charges, leaf_interp, interp_mid, interp_top, mid_points):
    _, _, skel = leaf_interp.shape
    rhs = charges.shape[0]
    rows = skel + 2 * rhs * (skel // LANES)
    return call(
        up_kernel,
        jax.ShapeDtypeStruct((rows, LANES), bf16),
        [vmem()] * 5,
        cost(3e8, 4e6),
        (charges, leaf_interp, interp_mid, interp_top, mid_points),
    )


def far_kernel(partners, mids, tops, interp_top, interp_mid, leaf_interp, out):
    leaf_dev, leaf_size, skel = leaf_interp.shape
    rhs = out.shape[0]

    def pair(source_ref, target, target_sq):
        source = source_ref[:skel, :]
        weight = load_halves(source_ref, skel, rhs, skel)
        tile = kernel_tile(source, source_term(source), target, target_sq)
        return dot(weight, tile)

    target = tops[0, :skel, :]
    target_sq = target_term(target)
    top_sum = jnp.zeros((rhs, skel), f32)
    for other in range(1, tops.shape[0]):
        top_sum = top_sum + pair(tops.at[other], target, target_sq)
    target = mids[0, :skel, :]
    target_sq = target_term(target)
    mid_sum = jnp.zeros((rhs, skel), f32)
    for at in range(partners.shape[0]):
        mid_sum = mid_sum + pair(mids.at[partners[at]], target, target_sq)
    total = (mid_sum + dot_rows(top_sum.astype(bf16), interp_top[...])).astype(bf16)
    for leaf in range(leaf_dev):
        block = interp_mid[leaf * skel : (leaf + 1) * skel, :]
        leaf_down = dot_rows(total, block).astype(bf16)
        out[:, leaf * leaf_size : (leaf + 1) * leaf_size] = dot_rows(leaf_down, leaf_interp[leaf])


def far(partners, mids, tops, interp_top, interp_mid, leaf_interp):
    leaf_dev, leaf_size, skel = leaf_interp.shape
    rhs = (mids.shape[1] - skel) // (2 * (skel // LANES))
    return call(
        far_kernel,
        jax.ShapeDtypeStruct((rhs, leaf_dev * leaf_size), f32),
        [smem()] + [vmem()] * 5,
        cost(1e9, 6e6, 5e5),
        (partners, mids, tops, interp_top, interp_mid, leaf_interp),
        own=1 << 20,
    )


def swapped(value, axis, size, distance):
    return lax.ppermute(value, axis, [(i, i ^ distance) for i in range(size)])


def share_halves(value, axis, size):
    half = size // 2
    pair = jnp.stack((value, swapped(value, axis, size, half)))
    others = [swapped(pair, axis, size, d) for d in range(1, half)]
    return jnp.concatenate([pair] + others, axis=0)


def place(distance, size):
    half = size // 2
    return distance % half * 2 + distance // half


def share(value, axis, size):
    gathered = value[None]
    while gathered.shape[0] < size:
        at = gathered.shape[0]
        other = swapped(gathered, axis, size, at)
        gathered = jnp.concatenate((gathered, other), axis=0)
    return gathered


def near_spans(group):
    half = group // 2
    spans = [(half, half + half // 2), (1, half)]
    spans += [(half + half // 2, half + half * 3 // 4), (half + half * 3 // 4, group)]
    return [span for span in spans if span[1] > span[0]]


def body(
    points,
    charges,
    near_leaves,
    leaf_interpolant,
    skel_leaf,
    interp_mid,
    skel_mid,
    mid_partners,
    interp_top,
    skel_top,
):
    group = lax.axis_size("sub")
    groups = lax.axis_size("leaf")
    self_index = lax.axis_index("sub")
    leaf_dev, leaf_size, skel = leaf_interpolant.shape
    coords = points.shape[1]
    rhs = charges.shape[1]
    near_count = near_leaves.shape[1]
    group_first = lax.axis_index("leaf") * group
    blocks = points.reshape(leaf_dev, leaf_size, coords)
    charges_t = charges.T

    where = jnp.stack((group_first * leaf_dev, self_index)).astype(i32)
    chosen, pool = want(near_leaves, where, leaf_dev, group)
    handed = lax.all_to_all(chosen, "sub", split_axis=0, concat_axis=0, tiled=True)

    leaf_of = skel_mid[0] // skel
    rows = skel_leaf.reshape(-1)[skel_mid[0]] + leaf_of * leaf_size
    mid_points = points[rows]
    message = up(charges_t, leaf_interpolant, interp_mid[0], interp_top[0], mid_points)

    asked = pack(where, handed, blocks, charges_t)
    got = []
    for distance, one in enumerate(asked, 1):
        got.append(swapped(one, "sub", group, distance))

    half = leaf_dev // 2
    first, tsq = near_local(pool, near_count, blocks, charges_t, (0, half))
    second = near_local(pool, near_count, blocks, charges_t, (half, leaf_dev), tsq)
    sums = [first, second]

    mids = share_halves(message, "sub", group)
    per = rhs * (skel // LANES)
    picked = skel_top[0]
    node = place(jnp.bitwise_xor(picked // skel, self_index), group)
    top_points = mids.reshape(-1, LANES)[node * mids.shape[1] + picked % skel]
    top_weight = jnp.sum(mids[:, skel + per :, :].astype(f32), axis=0).astype(bf16)
    tops = share(jnp.concatenate((top_points, top_weight), axis=0), "leaf", groups)

    partners = place(jnp.bitwise_xor(mid_partners[0] - group_first, self_index), group)
    distant = far(partners, mids, tops, interp_top[0], interp_mid[0], leaf_interpolant)
    spans = near_spans(group)
    for at, span in enumerate(spans):
        if at == len(spans) - 1:
            sums.append(distant)
        part = got[span[0] - 1 : span[1] - 1]
        sums = [near_remote(pool, near_count, blocks, tsq, span[0], part, sums)]
    return sums[0].T


def solution(mesh):
    placed = (
        P(("leaf", "sub"), None),
        P(("leaf", "sub"), None),
        P(("leaf", "sub"), None),
        P(("leaf", "sub"), None, None),
        P(("leaf", "sub"), None),
        P(("leaf", "sub"), None, None),
        P(("leaf", "sub"), None),
        P(("leaf", "sub"), None),
        P("leaf", "sub", None),
        P("leaf", None),
    )
    return jax.shard_map(
        body, mesh=mesh, in_specs=placed, out_specs=P(("leaf", "sub"), None), check_vma=False
    )
```

time: 160 us -> 176 us (1.10)
  the two profiles are of different devices: /device:TPU:0 before, /device:TPU:9 now
where the time goes in v2:
time: 176 us
  waiting for transfers between devices  60.8 us (35%)
  Pallas kernels  60.2 us (34%)
  starting transfers between devices  31 us (18%)
  local copies, waits for them, and re-layouts  18.8 us (11%)
  other arithmetic  4.44 us (3%)
    ppermute x13, waiting for transfers between devices, swapped(): return lax.ppermute(value, axis, [(i, i ^ distance) for i in range(size)])  60.8 us
    pallas_call x10, Pallas kernels, call(): pl.pallas_call(kernel, out_shape=out_shape, in_specs=in_specs, out_specs=...  60.2 us
    ppermute x13, starting transfers between devices, swapped(): return lax.ppermute(value, axis, [(i, i ^ distance) for i in range(size)])  25.3 us
    unnamed x45, local copies, waits for them, and re-layouts  13.3 us
    all_to_all x1, starting transfers between devices, body(): lax.all_to_all(chosen, 'sub', split_axis=0, concat_axis=0, tiled=True)  5.72 us
  transfers between devices with their start and end apart: 14, of which 5 were waited for; matrix products, arithmetic and copies ran while one was open for 7% of the time, Pallas kernels for 29%

profile of v2, /device:TPU:9, one launch (start us, length us, event | category | flops | bytes accessed | tf_op | source)
XLA Modules:
  0.0 175.5 jit_solution(4946482653567467259)
XLA Ops:
  0.0 0.1 pad_add_fusion.where
  0.1 0.8 copy-done.9
  0.8 1.5 shard_map.100
  2.3 5.7 %all-to-all-start = ((s32[8,1,8]{2,1,0:T(1,128)}), s32[8,1,8]{2,1,0:T(1,128)S(1)}, u32[]{:S(2)}, u32[]{:S(2)}) async-start(s32[8,1,8]{2,1,0:T(1,128)} %bitcast.5), calls=%async_computation | async-start | bytes 8192 | tf_op jit(solution)/shard_map/all_to_all | solution.py:470
  8.0 0.7 copy.12
  8.7 0.7 compare_select_fusion.5
  9.4 1.7 gather_fusion
  11.1 0.7 compare_select_fusion.1
  11.8 2.1 %gather_fusion.1 = bf16[256,128]{1,0:T(8,128)(2,1)S(1)} fusion(bf16[4096,128]{1,0:T(8,128)(2,1)} %param.10, s32[1024]{0:T(1024)S(1)} %pad_clamp_fusion.1), kind=kCustom, calls=%fused_computation.1 | custom fusion | bytes 132096 | tf_op jit(solution)/shard_map/gather | solution.py:474
  13.9 0.0 copy-start
  14.0 1.6 copy-done
  15.5 1.0 copy-done.4
  16.6 0.9 copy-done.7
  17.5 0.9 shard_map.107
  18.4 2.2 %collective-permute-start.7 = (bf16[512,128]{1,0:T(8,128)(2,1)S(1)}, bf16[512,128]{1,0:T(8,128)(2,1)S(1)}, u32[]{:S(2)}, u32[]{:S(2)}) collective-permute-start(bf16[512,128]{1,0:T(8,128)(2,1)S(1)} %shard_map.107), channel_id=1, source_target_pairs={{0,4},{1,5},{2,6},{3,7},{4,0},{5,1},{6,2},{7,3},{8,12},{9,13},{10,... | collective-permute-start | bytes 393224 | tf_op jit(solution)/shard_map/ppermute | solution.py:414
  20.6 10.9 %shard_map.101 = (f32[64,2048]{1,0:T(8,128)S(1)}, f32[8,8,512]{2,1,0:T(8,128)S(1)}) custom-call(s32[8,128]{1,0:T(8,128)S(1)} %get-tuple-element.16.pool, bf16[8,512,128]{2,1,0:T(8,128)(2,1)S(1)} %bitcast.66, bf16[64,4096]{1,0:T(8,128)(2,1)S(1)} %bitcast.74), custom_call_target="tpu_custom_call" | custom-call | flops 9663676416 | bytes 3000000 | tf_op jit(solution)/shard_map/pallas_call | solution.py:80
  31.5 0.0 copy-start.14
  31.5 0.8 copy-done.14
  32.3 11.0 %shard_map.103.refs_3_ = f32[64,2048]{1,0:T(8,128)S(1)} custom-call(s32[8,128]{1,0:T(8,128)S(1)} %get-tuple-element.16.pool, bf16[8,512,128]{2,1,0:T(8,128)(2,1)S(1)} %bitcast.67, bf16[64,4096]{1,0:T(8,128)(2,1)S(1)} %bitcast.75, f32[8,8,512]{2,1,0:T(8,128)S(1)} %get-tuple-element.17.refs_0_.tsq), custom_call_target="tpu_custom_call" | custom-call | flops 9663676416 | bytes 3000000 | tf_op jit(solution)/shard_map/pallas_call | solution.py:80
  43.4 0.8 copy-done.16
  44.2 0.7 fusion.4.partners
  44.9 0.0 collective-permute-done.7
  44.9 0.7 pad_maximum_fusion.1
  45.6 1.2 collective-permute-start.8
  46.9 0.6 pad_clamp_fusion
  47.5 0.0 all-to-all-done
  47.5 1.0 copy-done.6
  48.5 2.2 %shard_map.102 = (bf16[2,768,128]{2,1,0:T(8,128)(2,1)}, bf16[2,768,128]{2,1,0:T(8,128)(2,1)S(1)}, bf16[2,768,128]{2,1,0:T(8,128)(2,1)S(1)}, bf16[2,768,128]{2,1,...) custom-call(s32[2]{0:T(128)S(1)} %pad_add_fusion.where, ...), custom_call_target="tpu_custom_call" | custom-call | flops 100000 | bytes 8000000 | tf_op jit(solution)/shard_map/pallas_call | solution.py:80
  50.7 0.8 copy-done.10
  51.4 1.8 %collective-permute-start = (bf16[2,768,128]{2,1,0:T(8,128)(2,1)}, bf16[2,768,128]{2,1,0:T(8,128)(2,1)}, u32[]{:S(2)}, u32[]{:S(2)}) collective-permute-start(bf16[2,768,128]{2,1,0:T(8,128)(2,1)} %get-tuple-element.19), channel_id=1, source_target_pairs={{0,7},{1,6},{2,5},{3,4},{4,3},{5,2},{6,1},{7,0},{8,15},{9,14},{10,... | collective-permute-start | bytes 1179656 | tf_op jit(solution)/shard_map/ppermute | solution.py:414
  53.2 0.0 collective-permute-start.1
  53.2 2.6 %collective-permute-start.9 = (bf16[2,512,128]{2,1,0:T(8,128)(2,1)}, bf16[2,512,128]{2,1,0:T(8,128)(2,1)S(1)}, u32[]{:S(2)}, u32[]{:S(2)}) collective-permute-start(bf16[2,512,128]{2,1,0:T(8,128)(2,1)} %pad_maximum_fusion.1), channel_id=1, source_target_pairs={{0,2},{1,3},{2,0},{3,1},{4,6},{5,7},{6,4},{7,5},{8,10},{9,11},{10,... | collective-permute-start | bytes 786440 | tf_op jit(solution)/shard_map/ppermute | solution.py:414
  55.8 0.0 collective-permute-start.10
  55.9 0.9 constant_dynamic-update-slice_fusion.3
  56.8 0.0 collective-permute-done.8
  56.8 3.0 %collective-permute-start.5 = (bf16[2,768,128]{2,1,0:T(8,128)(2,1)}, bf16[2,768,128]{2,1,0:T(8,128)(2,1)}, u32[]{:S(2)}, u32[]{:S(2)}) collective-permute-start(bf16[2,768,128]{2,1,0:T(8,128)(2,1)} %get-tuple-element.24), channel_id=1, source_target_pairs={{0,4},{1,5},{2,6},{3,7},{4,0},{5,1},{6,2},{7,3},{8,12},{9,13},{10,... | collective-permute-start | bytes 1179656 | tf_op jit(solution)/shard_map/ppermute | solution.py:414
  59.8 1.0 constant_dynamic-update-slice_fusion.2
  60.8 16.9 %collective-permute-done.9 = bf16[2,512,128]{2,1,0:T(8,128)(2,1)S(1)} collective-permute-done((bf16[2,512,128]{2,1,0:T(8,128)(2,1)}, bf16[2,512,128]{2,1,0:T(8,128)(2,1)S(1)}, u32[]{:S(2)}, u32[]{:S(2)}) %collective-permute-start.9) | collective-permute-done | bytes 262176 | tf_op jit(solution)/shard_map/ppermute | solution.py:414
  77.7 3.6 %collective-permute-start.6 = (bf16[2,768,128]{2,1,0:T(8,128)(2,1)}, bf16[2,768,128]{2,1,0:T(8,128)(2,1)}, u32[]{:S(2)}, u32[]{:S(2)}) collective-permute-start(bf16[2,768,128]{2,1,0:T(8,128)(2,1)} %get-tuple-element.25), channel_id=1, source_target_pairs={{0,5},{1,4},{2,7},{3,6},{4,1},{5,0},{6,3},{7,2},{8,13},{9,12},{10,... | collective-permute-start | bytes 1179656 | tf_op jit(solution)/shard_map/ppermute | solution.py:414
  81.3 2.4 %collective-permute-done.10 = bf16[2,512,128]{2,1,0:T(8,128)(2,1)S(1)} collective-permute-done((bf16[2,512,128]{2,1,0:T(8,128)(2,1)}, bf16[2,512,128]{2,1,0:T(8,128)(2,1)S(1)}, u32[]{:S(2)}, u32[]{:S(2)}) %collective-permute-start.10) | collective-permute-done | bytes 262176 | tf_op jit(solution)/shard_map/ppermute | solution.py:414
  83.7 0.0 collective-permute-start.2
  83.7 1.6 gather_fusion.2
  85.4 0.8 maximum_bitcast_fusion
  86.2 28.6 %collective-permute-done.5.refs_0_ = bf16[2,768,128]{2,1,0:T(8,128)(2,1)} collective-permute-done((bf16[2,768,128]{2,1,0:T(8,128)(2,1)}, bf16[2,768,128]{2,1,0:T(8,128)(2,1)}, u32[]{:S(2)}, u32[]{:S(2)}) %collective-permute-start.5) | collective-permute-done | bytes 393248 | tf_op jit(solution)/shard_map/ppermute | solution.py:414
  114.8 0.0 collective-permute-start.3
  114.8 8.5 %collective-permute-done.6.refs_1_ = bf16[2,768,128]{2,1,0:T(8,128)(2,1)} collective-permute-done((bf16[2,768,128]{2,1,0:T(8,128)(2,1)}, bf16[2,768,128]{2,1,0:T(8,128)(2,1)}, u32[]{:S(2)}, u32[]{:S(2)}) %collective-permute-start.6) | collective-permute-done | bytes 393248 | tf_op jit(solution)/shard_map/ppermute | solution.py:414
  123.3 0.9 copy-done.12
  124.2 1.0 copy-done.15
  125.2 1.0 copy-done.17
  126.2 2.6 %shard_map.104.refs_3_ = f32[64,4096]{1,0:T(8,128)S(1)} custom-call(s32[8,128]{1,0:T(8,128)S(1)} %get-tuple-element.16.pool, bf16[8,512,128]{2,1,0:T(8,128)(2,1)S(1)} %bitcast.69, f32[8,8,512]{2,1,0:T(8,128)S(1)} %copy-done.12, bf16[2,768,128]{2,1,0:T(8,128)(2,1)} %collective-permute-done.5.refs_0_, bf16[2,768,128]{2,1,0:T(8,128)(2,1)} %collective-permute-done.6.refs_1_, ...), custom_call_target="tpu_custom_call" | custom-call | flops 6442450944 | bytes 3000000 | tf_op jit(solution)/shard_map/pallas_call | solution.py:80
  128.8 0.0 collective-permute-done.2.refs_0_
  128.8 10.8 %collective-permute-start.11 = (bf16[1,384,128]{2,1,0:T(8,128)(2,1)S(1)}, bf16[1,384,128]{2,1,0:T(8,128)(2,1)S(1)}, u32[]{:S(2)}, u32[]{:S(2)}) collective-permute-start(bf16[1,384,128]{2,1,0:T(8,128)(2,1)S(1)} %maximum_bitcast_fusion), channel_id=1, source_target_pairs={{0,8},{8,0},{16,24},{24,16},{1,9},{9,1},{17,25},{25,17},{2,10},{10... | collective-permute-start | bytes 294920 | tf_op jit(solution)/shard_map/ppermute | solution.py:414
  139.7 0.0 collective-permute-done.3.refs_1_
  139.7 0.0 collective-permute-done.4.refs_2_
  139.7 17.1 %shard_map.105.refs_1_ = f32[64,4096]{1,0:T(8,128)S(1)} custom-call(s32[8,128]{1,0:T(8,128)S(1)} %get-tuple-element.16.pool, bf16[8,512,128]{2,1,0:T(8,128)(2,1)S(1)} %bitcast.70, f32[8,8,512]{2,1,0:T(8,128)S(1)} %copy-done.12, bf16[2,768,128]{2,1,0:T(8,128)(2,1)} %collective-permute-done.2.refs_0_, bf16[2,768,128]{2,1,0:T(8,128)(2,1)S(1)} %collective-permute-done.3.refs_1_, ...), custom_call_target="tpu_custom_call" | custom-call | flops 9663676416 | bytes 3000000 | tf_op jit(solution)/shard_map/pallas_call | solution.py:80
  156.8 0.0 collective-permute-done.11
  156.9 0.0 copy-start.8
  156.9 0.1 collective-permute-start.12
  157.0 0.0 collective-permute-done.1.refs_0_
  157.0 0.0 copy-start.1
  157.0 2.3 %shard_map.106.refs_1_ = f32[64,4096]{1,0:T(8,128)S(1)} custom-call(s32[8,128]{1,0:T(8,128)S(1)} %get-tuple-element.16.pool, bf16[8,512,128]{2,1,0:T(8,128)(2,1)S(1)} %bitcast.71, f32[8,8,512]{2,1,0:T(8,128)S(1)} %copy-done.13, bf16[2,768,128]{2,1,0:T(8,128)(2,1)} %collective-permute-done.1.refs_0_, f32[64,4096]{1,0:T(8,128)S(1)} %shard_map.105.refs_1_), custom_call_target="tpu_custom_call" | custom-call | flops 3221225472 | bytes 3000000 | tf_op jit(solution)/shard_map/pallas_call | solution.py:80
  159.3 4.4 %collective-permute-done.12 = bf16[2,384,128]{2,1,0:T(8,128)(2,1)S(1)} collective-permute-done((bf16[2,384,128]{2,1,0:T(8,128)(2,1)S(1)}, bf16[2,384,128]{2,1,0:T(8,128)(2,1)S(1)}, u32[]{:S(2)}, u32[]{:S(2)}) %collective-permute-start.12) | collective-permute-done | bytes 196640 | tf_op jit(solution)/shard_map/ppermute | solution.py:414
  163.8 3.8 %shard_map.108.refs_2_ = f32[64,4096]{1,0:T(8,128)S(1)} custom-call(s32[4]{0:T(128)S(1)} %fusion.4.partners, bf16[8,512,128]{2,1,0:T(8,128)(2,1)S(1)} %constant_dynamic-update-slice_fusion.mids, bf16[4,384,128]{2,1,0:T(8,128)(2,1)S(1)} %pad_maximum_fusion.tops, bf16[256,256]{1,0:T(8,128)(2,1)S(1)} %bitcast.79, bf16[2048,256]{1,0:T(8,128)(2,1)S(1)} %bitcast.64, ...), custom_call_target="tpu_custom_call" | custom-call | flops 1000000000 | bytes 6000000 | tf_op jit(solution)/shard_map/pallas_call | solution.py:80
  167.6 8.0 %shard_map.109 = f32[64,4096]{1,0:T(8,128)} custom-call(s32[8,128]{1,0:T(8,128)S(1)} %get-tuple-element.16.pool, bf16[8,512,128]{2,1,0:T(8,128)(2,1)S(1)} %bitcast.72, f32[8,8,512]{2,1,0:T(8,128)S(1)} %copy-done.13, bf16[2,768,128]{2,1,0:T(8,128)(2,1)} %collective-permute-done.refs_0_, f32[64,4096]{1,0:T(8,128)S(1)} %shard_map.106.refs_1_, ...), custom_call_target="tpu_custom_call" | custom-call | flops 3221225472 | bytes 3000000 | tf_op jit(solution)/shard_map/pallas_call | solution.py:80
  (36 shorter events, 0.3 us)
Async XLA Ops:
  0.0 13.9 %copy-start.2 = (bf16[1,2048,256]{2,1,0:T(8,128)(2,1)S(1)}, bf16[1,2048,256]{2,1,0:T(8,128)(2,1)}, u32[]{:S(2)}) copy-start(bf16[1,2048,256]{2,1,0:T(8,128)(2,1)} %param.15) | copy-start | bytes 3145732
  0.1 0.8 copy-start.9
  2.3 45.2 %all-to-all-start = ((s32[8,1,8]{2,1,0:T(1,128)}), s32[8,1,8]{2,1,0:T(1,128)S(1)}, u32[]{:S(2)}, u32[]{:S(2)}) async-start(s32[8,1,8]{2,1,0:T(1,128)} %bitcast.5), calls=%async_computation | async-start | bytes 8192 | tf_op jit(solution)/shard_map/all_to_all | solution.py:470
  13.9 1.6 copy-start
  15.5 1.0 copy-start.4
  16.6 0.9 copy-start.7
  17.5 3.1 %copy-start.3 = (bf16[4096,128]{1,0:T(8,128)(2,1)S(1)}, bf16[4096,128]{1,0:T(8,128)(2,1)}, u32[]{:S(2)}) copy-start(bf16[4096,128]{1,0:T(8,128)(2,1)} %param.10) | copy-start | bytes 3145732
  17.5 3.1 %copy-start.5 = (bf16[4096,64]{0,1:T(8,128)(2,1)S(1)}, bf16[4096,64]{0,1:T(8,128)(2,1)}, u32[]{:S(2)}) copy-start(bf16[4096,64]{0,1:T(8,128)(2,1)} %param.11) | copy-start | bytes 1572868
  18.4 26.5 %collective-permute-start.7 = (bf16[512,128]{1,0:T(8,128)(2,1)S(1)}, bf16[512,128]{1,0:T(8,128)(2,1)S(1)}, u32[]{:S(2)}, u32[]{:S(2)}) collective-permute-start(bf16[512,128]{1,0:T(8,128)(2,1)S(1)} %shard_map.107), channel_id=1, source_target_pairs={{0,4},{1,5},{2,6},{3,7},{4,0},{5,1},{6,2},{7,3},{8,12},{9,13},{10,... | collective-permute-start | bytes 393224 | tf_op jit(solution)/shard_map/ppermute | solution.py:414
  31.5 0.8 copy-start.14
  32.3 11.0 %copy-start.11 = (f32[8,8,512]{2,1,0:T(8,128)}, f32[8,8,512]{2,1,0:T(8,128)S(1)}, u32[]{:S(2)}) copy-start(f32[8,8,512]{2,1,0:T(8,128)S(1)} %get-tuple-element.17.refs_0_.tsq) | copy-start | bytes 393220
  32.3 11.8 %copy-start.19 = (s32[1,256]{1,0:T(1,128)S(1)}, s32[1,256]{1,0:T(1,128)}, u32[]{:S(2)}) copy-start(s32[1,256]{1,0:T(1,128)} %param.19) | copy-start | bytes 3076
  43.4 0.8 copy-start.16
  44.9 2.6 %copy-start.18 = (bf16[512,128]{1,0:T(8,128)(2,1)}, bf16[512,128]{1,0:T(8,128)(2,1)S(1)}, u32[]{:S(2)}) copy-start(bf16[512,128]{1,0:T(8,128)(2,1)S(1)} %collective-permute-done.7) | copy-start | bytes 393220
  45.6 11.2 %collective-permute-start.8 = (bf16[2,512,128]{2,1,0:T(8,128)(2,1)}, bf16[2,512,128]{2,1,0:T(8,128)(2,1)}, u32[]{:S(2)}, u32[]{:S(2)}) collective-permute-start(bf16[2,512,128]{2,1,0:T(8,128)(2,1)} %pad_maximum_fusion.1), channel_id=1, source_target_pairs={{0,1},{1,0},{2,3},{3,2},{4,5},{5,4},{6,7},{7,6},{8,9},{9,8},{10,11... | collective-permute-start | bytes 786440 | tf_op jit(solution)/shard_map/ppermute | solution.py:414
  47.5 1.0 copy-start.6
  50.7 0.8 copy-start.10
  51.4 116.1 %collective-permute-start = (bf16[2,768,128]{2,1,0:T(8,128)(2,1)}, bf16[2,768,128]{2,1,0:T(8,128)(2,1)}, u32[]{:S(2)}, u32[]{:S(2)}) collective-permute-start(bf16[2,768,128]{2,1,0:T(8,128)(2,1)} %get-tuple-element.19), channel_id=1, source_target_pairs={{0,7},{1,6},{2,5},{3,4},{4,3},{5,2},{6,1},{7,0},{8,15},{9,14},{10,... | collective-permute-start | bytes 1179656 | tf_op jit(solution)/shard_map/ppermute | solution.py:414
  53.2 103.7 %collective-permute-start.1 = (bf16[2,768,128]{2,1,0:T(8,128)(2,1)}, bf16[2,768,128]{2,1,0:T(8,128)(2,1)}, u32[]{:S(2)}, u32[]{:S(2)}) collective-permute-start(bf16[2,768,128]{2,1,0:T(8,128)(2,1)} %get-tuple-element.20), channel_id=1, source_target_pairs={{0,6},{1,7},{2,4},{3,5},{4,2},{5,3},{6,0},{7,1},{8,14},{9,15},{10,... | collective-permute-start | bytes 1179656 | tf_op jit(solution)/shard_map/ppermute | solution.py:414
  53.2 24.4 %collective-permute-start.9 = (bf16[2,512,128]{2,1,0:T(8,128)(2,1)}, bf16[2,512,128]{2,1,0:T(8,128)(2,1)S(1)}, u32[]{:S(2)}, u32[]{:S(2)}) collective-permute-start(bf16[2,512,128]{2,1,0:T(8,128)(2,1)} %pad_maximum_fusion.1), channel_id=1, source_target_pairs={{0,2},{1,3},{2,0},{3,1},{4,6},{5,7},{6,4},{7,5},{8,10},{9,11},{10,... | collective-permute-start | bytes 786440 | tf_op jit(solution)/shard_map/ppermute | solution.py:414
  55.8 27.8 %collective-permute-start.10 = (bf16[2,512,128]{2,1,0:T(8,128)(2,1)}, bf16[2,512,128]{2,1,0:T(8,128)(2,1)S(1)}, u32[]{:S(2)}, u32[]{:S(2)}) collective-permute-start(bf16[2,512,128]{2,1,0:T(8,128)(2,1)} %pad_maximum_fusion.1), channel_id=1, source_target_pairs={{0,3},{1,2},{2,1},{3,0},{4,7},{5,6},{6,5},{7,4},{8,11},{9,10},{10,... | collective-permute-start | bytes 786440 | tf_op jit(solution)/shard_map/ppermute | solution.py:414
  56.8 58.0 %collective-permute-start.5 = (bf16[2,768,128]{2,1,0:T(8,128)(2,1)}, bf16[2,768,128]{2,1,0:T(8,128)(2,1)}, u32[]{:S(2)}, u32[]{:S(2)}) collective-permute-start(bf16[2,768,128]{2,1,0:T(8,128)(2,1)} %get-tuple-element.24), channel_id=1, source_target_pairs={{0,4},{1,5},{2,6},{3,7},{4,0},{5,1},{6,2},{7,3},{8,12},{9,13},{10,... | collective-permute-start | bytes 1179656 | tf_op jit(solution)/shard_map/ppermute | solution.py:414
  77.7 45.6 %collective-permute-start.6 = (bf16[2,768,128]{2,1,0:T(8,128)(2,1)}, bf16[2,768,128]{2,1,0:T(8,128)(2,1)}, u32[]{:S(2)}, u32[]{:S(2)}) collective-permute-start(bf16[2,768,128]{2,1,0:T(8,128)(2,1)} %get-tuple-element.25), channel_id=1, source_target_pairs={{0,5},{1,4},{2,7},{3,6},{4,1},{5,0},{6,3},{7,2},{8,13},{9,12},{10,... | collective-permute-start | bytes 1179656 | tf_op jit(solution)/shard_map/ppermute | solution.py:414
  83.7 45.1 %collective-permute-start.2 = (bf16[2,768,128]{2,1,0:T(8,128)(2,1)}, bf16[2,768,128]{2,1,0:T(8,128)(2,1)}, u32[]{:S(2)}, u32[]{:S(2)}) collective-permute-start(bf16[2,768,128]{2,1,0:T(8,128)(2,1)} %get-tuple-element.21), channel_id=1, source_target_pairs={{0,1},{1,0},{2,3},{3,2},{4,5},{5,4},{6,7},{7,6},{8,9},{9,8},{10,11... | collective-permute-start | bytes 1179656 | tf_op jit(solution)/shard_map/ppermute | solution.py:414
  114.8 24.9 %collective-permute-start.3 = (bf16[2,768,128]{2,1,0:T(8,128)(2,1)}, bf16[2,768,128]{2,1,0:T(8,128)(2,1)S(1)}, u32[]{:S(2)}, u32[]{:S(2)}) collective-permute-start(bf16[2,768,128]{2,1,0:T(8,128)(2,1)} %copy-done.10), channel_id=1, source_target_pairs={{0,2},{1,3},{2,0},{3,1},{4,6},{5,7},{6,4},{7,5},{8,10},{9,11},{10,... | collective-permute-start | bytes 1179656 | tf_op jit(solution)/shard_map/ppermute | solution.py:414
  123.2 16.4 %collective-permute-start.4 = (bf16[2,768,128]{2,1,0:T(8,128)(2,1)S(1)}, bf16[2,768,128]{2,1,0:T(8,128)(2,1)S(1)}, u32[]{:S(2)}, u32[]{:S(2)}) collective-permute-start(bf16[2,768,128]{2,1,0:T(8,128)(2,1)S(1)} %get-tuple-element.23), channel_id=1, source_target_pairs={{0,3},{1,2},{2,1},{3,0},{4,7},{5,6},{6,5},{7,4},{8,11},{9,10},{10,... | collective-permute-start | bytes 1179656 | tf_op jit(solution)/shard_map/ppermute | solution.py:414
  123.3 0.9 copy-start.12
  124.2 1.0 copy-start.15
  125.2 1.0 copy-start.17
  128.8 28.2 %copy-start.13 = (f32[8,8,512]{2,1,0:T(8,128)S(1)}, f32[8,8,512]{2,1,0:T(8,128)}, u32[]{:S(2)}) copy-start(f32[8,8,512]{2,1,0:T(8,128)} %copy-done.11) | copy-start | bytes 393220
  128.8 28.0 %collective-permute-start.11 = (bf16[1,384,128]{2,1,0:T(8,128)(2,1)S(1)}, bf16[1,384,128]{2,1,0:T(8,128)(2,1)S(1)}, u32[]{:S(2)}, u32[]{:S(2)}) collective-permute-start(bf16[1,384,128]{2,1,0:T(8,128)(2,1)S(1)} %maximum_bitcast_fusion), channel_id=1, source_target_pairs={{0,8},{8,0},{16,24},{24,16},{1,9},{9,1},{17,25},{25,17},{2,10},{10... | collective-permute-start | bytes 294920 | tf_op jit(solution)/shard_map/ppermute | solution.py:414
  156.9 6.9 %copy-start.8 = (bf16[1,256,256]{2,1,0:T(8,128)(2,1)S(1)}, bf16[1,256,256]{2,1,0:T(8,128)(2,1)}, u32[]{:S(2)}) copy-start(bf16[1,256,256]{2,1,0:T(8,128)(2,1)} %param.18) | copy-start | bytes 393220
  156.9 6.8 %collective-permute-start.12 = (bf16[2,384,128]{2,1,0:T(8,128)(2,1)S(1)}, bf16[2,384,128]{2,1,0:T(8,128)(2,1)S(1)}, u32[]{:S(2)}, u32[]{:S(2)}) collective-permute-start(bf16[2,384,128]{2,1,0:T(8,128)(2,1)S(1)} %pad_maximum_fusion.2), channel_id=1, source_target_pairs={{0,16},{8,24},{16,0},{24,8},{1,17},{9,25},{17,1},{25,9},{2,18},{10... | collective-permute-start | bytes 589832 | tf_op jit(solution)/shard_map/ppermute | solution.py:414
  157.0 6.8 %copy-start.1 = (bf16[8,512,256]{2,1,0:T(8,128)(2,1)S(1)}, bf16[8,512,256]{2,1,0:T(8,128)(2,1)}, u32[]{:S(2)}) copy-start(bf16[8,512,256]{2,1,0:T(8,128)(2,1)} %leaf_interp.3) | copy-start | bytes 6291460

commit v3 on v2

--- a/solution.py
+++ b/solution.py
@@ -13,6 +13,7 @@
 UNROLL = 4
 LANES = 128
 kernel_rate = 0.25
+VMEM_BYTES = 67043328
 LOG2E = math.log2(math.e)
 bf16 = jnp.bfloat16
 f32 = jnp.float32
@@ -74,15 +75,28 @@
     return total
 
 
-def call(kernel, out_shape, in_specs, estimate, operands, scratch=(), own=0):
-    outs = out_shape if isinstance(out_shape, (tuple, list)) else [out_shape]
-    grant = room(operands) + room(outs) + own + (2 << 20)
+def in_hbm():
+    return pl.BlockSpec(memory_space=pltpu.HBM)
+
+
+def copy_in(source, target, sem):
+    made = pltpu.make_async_copy(source, target, sem)
+    made.start()
+    return made
+
+
+def call(kernel, out_shape, in_specs, estimate, operands, scratch=(), own=0, outs=None, alias=None):
+    several = isinstance(out_shape, (tuple, list))
+    shapes = out_shape if several else [out_shape]
+    specs = outs or [vmem()] * len(shapes)
+    grant = room(operands) + room(shapes) + own + (2 << 20) if own is not None else VMEM_BYTES
     return pl.pallas_call(
         kernel,
         out_shape=out_shape,
         in_specs=in_specs,
-        out_specs=[vmem()] * len(outs) if outs is out_shape else vmem(),
+        out_specs=specs if several else specs[0],
         scratch_shapes=list(scratch),
+        input_output_aliases=alias or {},
         compiler_params=pltpu.CompilerParams(vmem_limit_bytes=grant),
         cost_estimate=estimate,
     )(*operands)
@@ -142,37 +156,70 @@
         [smem(), vmem()],
         cost(1e6, 1e5),
         (where, near_leaves),
-    )
-
-
-def pack_kernel(leaf_size, where, handed, points, charges, *outs):
+        own=None,
+    )
+
+
+def pack_kernel(leaf_size, distances, where, handed, points, charges, *refs):
+    outs, (x, q, sem_x, sem_q, sem_out) = refs[: len(distances)], refs[len(distances) :]
     self_index = where[1]
     rhs = charges.shape[0]
-    for at, out in enumerate(outs):
-        peer = jnp.bitwise_xor(self_index, at + 1)
+    taken, given = [], []
+    for at, distance in enumerate(distances):
+        peer = jnp.bitwise_xor(self_index, distance)
         for slot in range(CAP):
             leaf = handed[peer, slot]
-            out[slot, :leaf_size, :] = points[leaf]
+            lanes = pl.ds(pl.multiple_of(leaf * leaf_size, leaf_size), leaf_size)
+            put = at * CAP + slot
+            taken.append(
+                (
+                    copy_in(points.at[leaf], x.at[put], sem_x.at[put]),
+                    copy_in(charges.at[:, lanes], q.at[put], sem_q.at[put]),
+                )
+            )
+    for at, out in enumerate(outs):
+        for slot in range(CAP):
+            put = at * CAP + slot
+            taken[put][0].wait()
+            given.append(copy_in(x.at[put], out.at[slot, :leaf_size, :], sem_out.at[put, 0]))
+            taken[put][1].wait()
             for tile in range(leaf_size // LANES):
-                lane = pl.multiple_of(leaf * leaf_size + tile * LANES, LANES)
-                row = leaf_size + tile * rhs
-                out[slot, row : row + rhs, :] = charges[:, pl.ds(lane, LANES)]
-
-
-def pack(where, handed, points, charges):
+                rows = pl.ds(leaf_size + tile * rhs, rhs)
+                lanes = pl.ds(tile * LANES, LANES)
+                given.append(
+                    copy_in(
+                        q.at[put, :, lanes], out.at[slot, rows, :], sem_out.at[put, 1 + tile]
+                    )
+                )
+    for one in given:
+        one.wait()
+
+
+def pack(where, handed, points, charges, distances):
     _, leaf_size, coords = points.shape
-    group = handed.shape[0]
-    rows = leaf_size + leaf_size // LANES * charges.shape[0]
+    rhs = charges.shape[0]
+    rows = leaf_size + leaf_size // LANES * rhs
+    places = len(distances) * CAP
+    sem = pltpu.SemaphoreType.DMA
     return call(
-        functools.partial(pack_kernel, leaf_size),
-        [jax.ShapeDtypeStruct((CAP, rows, coords), bf16) for _ in range(group - 1)],
-        [smem(), smem(), vmem(), vmem()],
-        cost(1e5, 8e6),
+        functools.partial(pack_kernel, leaf_size, distances),
+        [jax.ShapeDtypeStruct((CAP, rows, coords), bf16) for _ in distances],
+        [smem(), smem(), in_hbm(), in_hbm()],
+        cost(1e5, 2 * places * rows * coords * 2),
         (where, handed, points, charges),
-    )
-
-
-def run_pairs(pool, near_count, leaves, keep, tl, sl, tile_of, charge_of, acc):
+        scratch=[
+            pltpu.VMEM((places, leaf_size, coords), bf16),
+            pltpu.VMEM((places, rhs, leaf_size), bf16),
+            sem((places,)),
+            sem((places,)),
+            sem((places, 1 + leaf_size // LANES)),
+        ],
+        own=None,
+        outs=[in_hbm()] * len(distances),
+    )
+
+
+def run_pairs(pool, near_count, leaves, keep, tl, sl, tile_of, charge_of, acc, base):
     def scan(leaf, count):
         for entry in range(near_count):
             kept, source = keep(pool[leaf, entry])
@@ -185,7 +232,7 @@
 
     def one(at):
         target, source = tl[at], sl[at]
-        acc[target] += dot(charge_of(source), tile_of(target, source))
+        acc[target - base] += dot(charge_of(source), tile_of(target, source))
 
     def several(step, carry):
         for k in range(UNROLL):
@@ -209,89 +256,106 @@
 
 def near_local_kernel(near_count, leaves, pool, points, charges, *refs):
     if leaves[0] == 0:
-        out, tsq, tl, sl, ssq, acc = refs
+        out, tsq, tl, sl, x, q, ssq, acc, sem_x, sem_q, sem_out = refs
     else:
-        tsq, out, tl, sl, ssq, acc = refs
+        tsq, out, tl, sl, x, q, ssq, acc, sem_x, sem_q, sem_out = refs
     leaf_dev, leaf_size, _ = points.shape
-
-    def prepare(leaf, carry):
-        ssq[leaf] = source_term(points[leaf])
+    q_copy = copy_in(charges, q, sem_q)
+    x_copies = [copy_in(points.at[m], x.at[m], sem_x.at[m]) for m in range(leaf_dev)]
+    acc[...] = jnp.zeros_like(acc)
+    for leaf, waited in enumerate(x_copies):
+        waited.wait()
+        ssq[leaf] = source_term(x[leaf])
         if leaves[0] == 0:
-            tsq[leaf] = target_term(points[leaf])
-        return carry
-
-    lax.fori_loop(0, leaf_dev, prepare, 0)
-    for leaf in range(*leaves):
-        acc[leaf] = jnp.zeros(acc.shape[1:], f32)
+            tsq[leaf] = target_term(x[leaf])
+    q_copy.wait()
 
     def charge_of(source):
         at = pl.multiple_of(source * leaf_size, leaf_size)
-        return charges[:, pl.ds(at, leaf_size)]
+        return q[:, pl.ds(at, leaf_size)]
 
     def tile_of(target, source):
-        return kernel_tile(points[source], ssq[source], points[target], tsq[target])
+        return kernel_tile(x[source], ssq[source], x[target], tsq[target])
 
     def keep(index):
         return index < leaf_dev, index
 
-    run_pairs(pool, near_count, leaves, keep, tl, sl, tile_of, charge_of, acc)
-    for leaf in range(*leaves):
-        at = (leaf - leaves[0]) * leaf_size
-        out[:, at : at + leaf_size] = acc[leaf]
+    run_pairs(pool, near_count, leaves, keep, tl, sl, tile_of, charge_of, acc, leaves[0])
+    copy_in(acc, out, sem_out).wait()
 
 
 def near_local(pool, near_count, points, charges, leaves, *tsq):
     leaf_dev, leaf_size, coords = points.shape
     rhs = charges.shape[0]
     span = leaves[1] - leaves[0]
-    result = jax.ShapeDtypeStruct((rhs, span * leaf_size), f32)
+    result = jax.ShapeDtypeStruct((span, rhs, leaf_size), f32)
     terms = jax.ShapeDtypeStruct((leaf_dev, 8, leaf_size), f32)
     return call(
         functools.partial(near_local_kernel, near_count, leaves),
         result if tsq else [result, terms],
-        [smem(), vmem(), vmem()] + [vmem()] * len(tsq),
+        [smem(), in_hbm(), in_hbm()] + [vmem()] * len(tsq),
         near_cost(span * near_count / 2, leaf_size, coords, rhs),
         (pool, points, charges) + tsq,
         scratch=[
             pltpu.SMEM((leaf_dev * near_count + 1,), i32),
             pltpu.SMEM((leaf_dev * near_count + 1,), i32),
+            pltpu.VMEM(points.shape, bf16),
+            pltpu.VMEM(charges.shape, bf16),
             pltpu.VMEM((leaf_dev, leaf_size, LANES), f32),
-            pltpu.VMEM((leaf_dev, rhs, leaf_size), f32),
+            pltpu.VMEM((span, rhs, leaf_size), f32),
+            pltpu.SemaphoreType.DMA((leaf_dev,)),
+            pltpu.SemaphoreType.DMA,
+            pltpu.SemaphoreType.DMA,
         ],
-        own=leaf_dev * leaf_size * (rhs + LANES) * 4 + (1 << 20),
-    )
-
-
-def near_remote_kernel(near_count, first, parts, extra, pool, points, tsq, *refs):
-    got, inits, refs = refs[:parts], refs[parts : parts + extra], refs[parts + extra :]
-    out, tl, sl, pts, ssq, qs, acc = refs
+        own=None,
+        outs=[in_hbm()] if tsq else [in_hbm(), vmem()],
+    )
+
+
+def near_remote_kernel(near_count, first, parts, stage, pool, points, tsq, *refs):
+    got, refs = refs[:parts], refs[parts:]
+    taken = {"first": 2, "middle": 1, "last": 2}[stage]
+    inits, refs = refs[:taken], refs[taken:]
+    out, tl, sl, x, pts, ssq, qs = refs[:7]
+    sem_got, sem_x, sem_acc = refs[-3:]
+    acc = refs[7] if stage == "last" else out
     leaf_dev, leaf_size, _ = points.shape
-    rhs = out.shape[0]
-
+    rhs = acc.shape[1]
+    tiles = leaf_size // LANES
+
+    moves = []
     for part, message in enumerate(got):
-        def prepare(slot, carry, part=part, message=message):
-            place = part * CAP + slot
-            x = message[slot, :leaf_size, :]
-            pts[place] = x
-            ssq[place] = source_term(x)
-            for tile in range(leaf_size // LANES):
-                row = leaf_size + tile * rhs
-                qs[place, :, tile * LANES : (tile + 1) * LANES] = message[slot, row : row + rhs, :]
-            return carry
-
-        lax.fori_loop(0, CAP, prepare, 0)
-
-    width = 0
-    for init in inits:
-        span = init.shape[1] // leaf_size
-        for leaf in range(span):
-            value = init[:, leaf * leaf_size : (leaf + 1) * leaf_size]
-            target = (width + leaf) % leaf_dev
-            if width + leaf < leaf_dev:
-                acc[target] = value
-            else:
-                acc[target] += value
-        width += span
+        for slot in range(CAP):
+            at = part * CAP + slot
+            one = [copy_in(message.at[slot, :leaf_size, :], pts.at[at], sem_got.at[at, 0])]
+            for tile in range(tiles):
+                rows = pl.ds(leaf_size + tile * rhs, rhs)
+                lanes = pl.ds(tile * LANES, LANES)
+                one.append(
+                    copy_in(
+                        message.at[slot, rows, :], qs.at[at, :, lanes], sem_got.at[at, 1 + tile]
+                    )
+                )
+            moves.append(one)
+    x_copy = copy_in(points, x, sem_x)
+    acc_copies = []
+    if stage == "first":
+        base = 0
+        for at, init in enumerate(inits):
+            rows = pl.ds(base, init.shape[0])
+            acc_copies.append(copy_in(init, acc.at[rows], sem_acc.at[at]))
+            base += init.shape[0]
+    if stage == "last":
+        for leaf in range(leaf_dev):
+            acc[leaf] = inits[0][leaf] + inits[1][leaf]
+    for at, one in enumerate(moves):
+        one[0].wait()
+        ssq[at] = source_term(pts[at])
+        for move in one[1:]:
+            move.wait()
+    x_copy.wait()
+    for move in acc_copies:
+        move.wait()
 
     low = leaf_dev + first * CAP
 
@@ -299,35 +363,47 @@
         return (index >= low) & (index < low + parts * CAP), index - low
 
     def tile_of(target, source):
-        return kernel_tile(pts[source], ssq[source], points[target], tsq[target])
-
-    run_pairs(
-        pool, near_count, (0, leaf_dev), keep, tl, sl, tile_of, lambda s: qs[s], acc
-    )
-    for leaf in range(leaf_dev):
-        out[:, leaf * leaf_size : (leaf + 1) * leaf_size] = acc[leaf]
-
-
-def near_remote(pool, near_count, points, tsq, first, got, inits):
+        return kernel_tile(pts[source], ssq[source], x[target], tsq[target])
+
+    run_pairs(pool, near_count, (0, leaf_dev), keep, tl, sl, tile_of, lambda s: qs[s], acc, 0)
+    if stage == "last":
+        for leaf in range(leaf_dev):
+            out[:, leaf * leaf_size : (leaf + 1) * leaf_size] = acc[leaf]
+
+
+def near_remote(pool, near_count, points, tsq, first, got, inits, stage):
     leaf_dev, leaf_size, coords = points.shape
-    rhs = inits[0].shape[0]
+    rhs = inits[0].shape[1]
     places = len(got) * CAP
+    sums = (leaf_dev, rhs, leaf_size)
+    last = stage == "last"
+    scratch = [
+        pltpu.SMEM((leaf_dev * near_count + 1,), i32),
+        pltpu.SMEM((leaf_dev * near_count + 1,), i32),
+        pltpu.VMEM(points.shape, bf16),
+        pltpu.VMEM((places, leaf_size, coords), bf16),
+        pltpu.VMEM((places, leaf_size, LANES), f32),
+        pltpu.VMEM((places, rhs, leaf_size), bf16),
+    ]
+    if last:
+        scratch.append(pltpu.VMEM(sums, f32))
+    scratch += [
+        pltpu.SemaphoreType.DMA((places, 1 + leaf_size // LANES)),
+        pltpu.SemaphoreType.DMA,
+        pltpu.SemaphoreType.DMA((2,)),
+    ]
+    spec = in_hbm() if stage == "first" else vmem()
+    shape = (rhs, leaf_dev * leaf_size) if last else sums
     return call(
-        functools.partial(near_remote_kernel, near_count, first, len(got), len(inits)),
-        jax.ShapeDtypeStruct((rhs, leaf_dev * leaf_size), f32),
-        [smem(), vmem(), vmem()] + [vmem()] * (len(got) + len(inits)),
+        functools.partial(near_remote_kernel, near_count, first, len(got), stage),
+        jax.ShapeDtypeStruct(shape, f32),
+        [smem(), in_hbm(), vmem()] + [in_hbm()] * len(got) + [spec] * len(inits),
         near_cost(len(got) * leaf_dev, leaf_size, coords, rhs),
         (pool, points, tsq, *got, *inits),
-        scratch=[
-            pltpu.SMEM((leaf_dev * near_count + 1,), i32),
-            pltpu.SMEM((leaf_dev * near_count + 1,), i32),
-            pltpu.VMEM((places, leaf_size, coords), bf16),
-            pltpu.VMEM((places, leaf_size, LANES), f32),
-            pltpu.VMEM((places, rhs, leaf_size), bf16),
-            pltpu.VMEM((leaf_dev, rhs, leaf_size), f32),
-        ],
+        scratch=scratch,
         own=(leaf_dev * rhs * 4 + places * (coords * 2 + LANES * 4 + rhs * 2)) * leaf_size
         + (2 << 20),
+        alias={3 + len(got): 0} if stage == "middle" else None,
     )
 
 
@@ -343,36 +419,76 @@
     return jnp.concatenate(tiles, axis=1)
 
 
-def up_kernel(charges, leaf_interp, interp_mid, interp_top, mid_points, out):
+def skeleton_rows(skel_leaf, skel_mid, leaf_size):
+    leaf_dev, skel = skel_leaf.shape
+    column = lax.rem(skel_mid, skel)
+    leaf = lax.div(skel_mid, skel)
+    hit = lax.broadcasted_iota(i32, (skel, skel), 0) == column
+    table = jnp.concatenate((lax.div(skel_leaf, 16), lax.rem(skel_leaf, 16)), axis=0)
+    found = dot(table.astype(f32).astype(bf16), hit.astype(f32).astype(bf16))
+    index = (found[:leaf_dev] * 16.0 + found[leaf_dev:]).astype(i32)
+    row = lax.broadcasted_iota(i32, (leaf_dev, skel), 0)
+    return jnp.sum(jnp.where(row == leaf, index + row * leaf_size, 0), axis=0, keepdims=True)
+
+
+def up_kernel(*refs):
+    points, charges, leaf_interp, interp_mid, interp_top, skel_leaf, skel_mid, out = refs[:8]
+    x, q, leaf_w, mid_w, top_w, sem_x, sem_l, sem_m, sem_q, sem_t = refs[8:]
     leaf_dev, leaf_size, skel = leaf_interp.shape
-    total = jnp.zeros((charges.shape[0], skel), f32)
-    for leaf in range(leaf_dev):
-        block = charges[:, leaf * leaf_size : (leaf + 1) * leaf_size]
-        leaf_up = dot(block, leaf_interp[leaf]).astype(bf16)
-        total = total + dot(leaf_up, interp_mid[leaf * skel : (leaf + 1) * skel, :])
+    leaves = range(leaf_dev)
+    x_copies = [copy_in(points.at[m], x.at[m], sem_x.at[m]) for m in leaves]
+    q_copy = copy_in(charges, q, sem_q)
+    l_copies, m_copies = [], []
+    for m in leaves:
+        rows = pl.ds(m * skel, skel)
+        l_copies.append(copy_in(leaf_interp.at[m], leaf_w.at[m], sem_l.at[m]))
+        m_copies.append(copy_in(interp_mid.at[rows], mid_w.at[rows], sem_m.at[m]))
+    t_copy = copy_in(interp_top, top_w, sem_t)
+
+    rows = skeleton_rows(skel_leaf[...], skel_mid[...], leaf_size)
+    at = lax.broadcasted_iota(i32, (leaf_size, skel), 0)
+    columns = (((0,), (0,)), ((), ()))
+    picked = jnp.zeros((skel, x.shape[2]), f32)
+    for m in leaves:
+        one_hot = (at == rows - m * leaf_size).astype(f32).astype(bf16)
+        x_copies[m].wait()
+        picked = picked + lax.dot_general(one_hot, x[m], columns, preferred_element_type=f32)
+    out[:skel, :] = picked.astype(bf16)
+    total = jnp.zeros((q.shape[0], skel), f32)
+    q_copy.wait()
+    for m in leaves:
+        l_copies[m].wait()
+        leaf_up = dot(q[:, m * leaf_size : (m + 1) * leaf_size], leaf_w[m]).astype(bf16)
+        m_copies[m].wait()
+        total = total + dot(leaf_up, mid_w[m * skel : (m + 1) * skel, :])
     mid_up = total.astype(bf16)
-    top = dot(mid_up, interp_top[...])
-    out[:skel, :] = mid_points[...]
+    t_copy.wait()
+    top = dot(mid_up, top_w[...])
     row = store_halves(out, skel, mid_up)
     store_halves(out, row, top.astype(bf16))
 
 
-def up(charges, leaf_interp, interp_mid, interp_top, mid_points):
-    _, _, skel = leaf_interp.shape
+def up(points, charges, leaf_interp, interp_mid, interp_top, skel_leaf, skel_mid):
+    leaf_dev, _, skel = leaf_interp.shape
     rhs = charges.shape[0]
     rows = skel + 2 * rhs * (skel // LANES)
+    sem = pltpu.SemaphoreType.DMA
+    whole = (points, charges, leaf_interp, interp_mid, interp_top)
     return call(
         up_kernel,
         jax.ShapeDtypeStruct((rows, LANES), bf16),
-        [vmem()] * 5,
-        cost(3e8, 4e6),
-        (charges, leaf_interp, interp_mid, interp_top, mid_points),
+        [in_hbm()] * 5 + [vmem()] * 2,
+        cost(3e9, 5e6),
+        whole + (skel_leaf, skel_mid),
+        scratch=[pltpu.VMEM(a.shape, bf16) for a in whole]
+        + [sem((leaf_dev,)), sem((leaf_dev,)), sem((leaf_dev,)), sem, sem],
+        own=None,
     )
 
 
 def far_kernel(partners, mids, tops, interp_top, interp_mid, leaf_interp, out):
-    leaf_dev, leaf_size, skel = leaf_interp.shape
-    rhs = out.shape[0]
+    leaf_dev, _, skel = leaf_interp.shape
+    rhs = out.shape[1]
 
     def pair(source_ref, target, target_sq):
         source = source_ref[:skel, :]
@@ -391,10 +507,9 @@
     for at in range(partners.shape[0]):
         mid_sum = mid_sum + pair(mids.at[partners[at]], target, target_sq)
     total = (mid_sum + dot_rows(top_sum.astype(bf16), interp_top[...])).astype(bf16)
-    for leaf in range(leaf_dev):
-        block = interp_mid[leaf * skel : (leaf + 1) * skel, :]
-        leaf_down = dot_rows(total, block).astype(bf16)
-        out[:, leaf * leaf_size : (leaf + 1) * leaf_size] = dot_rows(leaf_down, leaf_interp[leaf])
+    for m in range(leaf_dev):
+        leaf_down = dot_rows(total, interp_mid[m * skel : (m + 1) * skel, :]).astype(bf16)
+        out[m] = dot_rows(leaf_down, leaf_interp[m])
 
 
 def far(partners, mids, tops, interp_top, interp_mid, leaf_interp):
@@ -402,7 +517,7 @@
     rhs = (mids.shape[1] - skel) // (2 * (skel // LANES))
     return call(
         far_kernel,
-        jax.ShapeDtypeStruct((rhs, leaf_dev * leaf_size), f32),
+        jax.ShapeDtypeStruct((leaf_dev, rhs, leaf_size), f32),
         [smem()] + [vmem()] * 5,
         cost(1e9, 6e6, 5e5),
         (partners, mids, tops, interp_top, interp_mid, leaf_interp),
@@ -433,6 +548,12 @@
         other = swapped(gathered, axis, size, at)
         gathered = jnp.concatenate((gathered, other), axis=0)
     return gathered
+
+
+def across(group):
+    half = group // 2
+    cuts = [half, half + max(half // 4, 1), half + half // 2, half + half * 3 // 4, group]
+    return [list(range(*cut)) for cut in zip(cuts, cuts[1:])]
 
 
 def near_spans(group):
@@ -469,15 +590,16 @@
     chosen, pool = want(near_leaves, where, leaf_dev, group)
     handed = lax.all_to_all(chosen, "sub", split_axis=0, concat_axis=0, tiled=True)
 
-    leaf_of = skel_mid[0] // skel
-    rows = skel_leaf.reshape(-1)[skel_mid[0]] + leaf_of * leaf_size
-    mid_points = points[rows]
-    message = up(charges_t, leaf_interpolant, interp_mid[0], interp_top[0], mid_points)
-
-    asked = pack(where, handed, blocks, charges_t)
-    got = []
-    for distance, one in enumerate(asked, 1):
-        got.append(swapped(one, "sub", group, distance))
+    message = up(
+        blocks, charges_t, leaf_interpolant, interp_mid[0], interp_top[0], skel_leaf, skel_mid
+    )
+
+    early = across(group)[0]
+    got = {}
+    for distances in (early, [d for d in range(1, group) if d not in early]):
+        asked = pack(where, handed, blocks, charges_t, distances)
+        for distance, one in zip(distances, asked):
+            got[distance] = swapped(one, "sub", group, distance)
 
     half = leaf_dev // 2
     first, tsq = near_local(pool, near_count, blocks, charges_t, (0, half))
@@ -496,10 +618,12 @@
     distant = far(partners, mids, tops, interp_top[0], interp_mid[0], leaf_interpolant)
     spans = near_spans(group)
     for at, span in enumerate(spans):
+        stage = "first" if at == 0 else "middle"
         if at == len(spans) - 1:
+            stage = "last"
             sums.append(distant)
-        part = got[span[0] - 1 : span[1] - 1]
-        sums = [near_remote(pool, near_count, blocks, tsq, span[0], part, sums)]
+        part = [got[distance] for distance in range(*span)]
+        sums = [near_remote(pool, near_count, blocks, tsq, span[0], part, sums, stage)]
     return sums[0].T
 
 

time: 176 us -> 184 us (1.045)
  Pallas kernels: 60.2 us -> 78.6 us
  local copies, waits for them, and re-layouts: 18.8 us -> 10.6 us
  waiting for transfers between devices: 60.8 us -> 55.4 us
    pallas_call x10 -> x11, Pallas kernels: 60.2 us -> 78.6 us  [call(): pl.pallas_call(kernel, out_shape=out_shape, in_specs=in_specs, out_specs=...]
    unnamed x45 -> x24, local copies, waits for them, and re-layouts: 13.3 us -> 7.68 us
    ppermute x13, waiting for transfers between devices: 60.8 us -> 55.4 us  [swapped(): return lax.ppermute(value, axis, [(i, i ^ distance) for i in range(size)])]
    gather x2 -> x0, local copies, waits for them, and re-layouts: 3.81 us -> none  [the longest x1 2.09 us: body(): mid_points = points[rows]]
  transfers between devices with their start and end apart: 14 -> 14, of which waited for: 5 -> 5; matrix products, arithmetic and copies ran while one was open for 7% -> 7% of each run, Pallas kernels for 29% -> 38%
where the time goes in v3:
time: 184 us; the launch traced here: 183 us
  Pallas kernels  78.6 us (43%)
  waiting for transfers between devices  55.4 us (30%)
  starting transfers between devices  32 us (17%)
  local copies, waits for them, and re-layouts  10.6 us (6%)
  other arithmetic  5.84 us (3%)
    pallas_call x11, Pallas kernels, call(): pl.pallas_call(kernel, out_shape=out_shape, in_specs=in_specs, out_specs=...  78.6 us
    ppermute x13, waiting for transfers between devices, swapped(): return lax.ppermute(value, axis, [(i, i ^ distance) for i in range(size)])  55.4 us
    ppermute x13, starting transfers between devices, swapped(): return lax.ppermute(value, axis, [(i, i ^ distance) for i in range(size)])  26.2 us
    unnamed x24, local copies, waits for them, and re-layouts  7.68 us
    all_to_all x1, starting transfers between devices, body(): lax.all_to_all(chosen, 'sub', split_axis=0, concat_axis=0, tiled=True)  5.72 us
  transfers between devices with their start and end apart: 14, of which 5 were waited for; matrix products, arithmetic and copies ran while one was open for 7% of the time, Pallas kernels for 38%

profile of v3, /device:TPU:9, one launch (start us, length us, event | category | flops | bytes accessed | tf_op | source)
XLA Modules:
  0.0 182.8 jit_solution(2290413995344029030)
XLA Ops:
  0.0 0.6 pad_add_fusion.where
  0.6 1.7 shard_map.100
  2.3 5.7 %all-to-all-start = ((s32[8,1,8]{2,1,0:T(1,128)}), s32[8,1,8]{2,1,0:T(1,128)}, u32[]{:S(2)}, u32[]{:S(2)}) async-start(s32[8,1,8]{2,1,0:T(1,128)} %bitcast.68), calls=%async_computation | async-start | bytes 8192 | tf_op jit(solution)/shard_map/all_to_all | solution.py:591
  8.0 7.3 %shard_map.108 = bf16[512,128]{1,0:T(8,128)(2,1)} custom-call(bf16[8,512,128]{2,1,0:T(8,128)(2,1)} %bitcast.47, bf16[64,4096]{1,0:T(8,128)(2,1)} %bitcast.61, bf16[8,512,256]{2,1,0:T(8,128)(2,1)} %leaf_interp.1, bf16[2048,256]{1,0:T(8,128)(2,1)} %bitcast.57, bf16[256,256]{1,0:T(8,128)(2,1)} %bitcast.59, s32[8,256]{1,0:T(8,128)} %refs_5_.1, s32[1,256]{1,0:T(1,128)} %refs_6_.1), custom_call_target="tpu_custom_call" | custom-call | flops 3000000000 | bytes 5000000 | tf_op jit(solution)/shard_map/pallas_call | solution.py:93
  15.3 2.1 %collective-permute-start.7 = (bf16[512,128]{1,0:T(8,128)(2,1)}, bf16[512,128]{1,0:T(8,128)(2,1)}, u32[]{:S(2)}, u32[]{:S(2)}) collective-permute-start(bf16[512,128]{1,0:T(8,128)(2,1)} %shard_map.108), channel_id=1, source_target_pairs={{0,4},{1,5},{2,6},{3,7},{4,0},{5,1},{6,2},{7,3},{8,12},{9,13},{10,... | collective-permute-start | bytes 393224 | tf_op jit(solution)/shard_map/ppermute | solution.py:529
  17.5 1.6 constant_dynamic-update-slice_fusion.4
  19.1 13.4 %shard_map.101 = (f32[4,64,512]{2,1,0:T(8,128)}, f32[8,8,512]{2,1,0:T(8,128)}) custom-call(s32[8,128]{1,0:T(8,128)} %get-tuple-element.15.pool, bf16[8,512,128]{2,1,0:T(8,128)(2,1)} %bitcast.48, bf16[64,4096]{1,0:T(8,128)(2,1)} %bitcast.62), custom_call_target="tpu_custom_call" | custom-call | flops 9663676416 | bytes 3000000 | tf_op jit(solution)/shard_map/pallas_call | solution.py:93
  32.5 13.4 %shard_map.104.refs_3_ = f32[4,64,512]{2,1,0:T(8,128)} custom-call(s32[8,128]{1,0:T(8,128)} %get-tuple-element.15.pool, bf16[8,512,128]{2,1,0:T(8,128)(2,1)} %bitcast.49, bf16[64,4096]{1,0:T(8,128)(2,1)} %bitcast.63, f32[8,8,512]{2,1,0:T(8,128)} %get-tuple-element.16.refs_0_.tsq), custom_call_target="tpu_custom_call" | custom-call | flops 9663676416 | bytes 3000000 | tf_op jit(solution)/shard_map/pallas_call | solution.py:93
  46.0 0.7 compare_select_fusion
  46.7 1.2 fusion.4.partners
  47.8 0.0 collective-permute-done.7
  47.8 1.7 pad_maximum_fusion.1
  49.5 1.3 collective-permute-start.8
  50.8 0.6 pad_clamp_fusion
  51.4 0.0 all-to-all-done
  51.4 4.8 %shard_map.102 = (bf16[2,768,128]{2,1,0:T(8,128)(2,1)}, bf16[2,768,128]{2,1,0:T(8,128)(2,1)}, bf16[2,768,128]{2,1,0:T(8,128)(2,1)}, bf16[2,768,128]{2,1,0:T(8,12...) custom-call(s32[2]{0:T(128)} %pad_add_fusion.where, s32[8,8]{1,0:T(8,128)} %bitcast.6.handed, ...), custom_call_target="tpu_custom_call" | custom-call | flops 100000 | bytes 4718592 | tf_op jit(solution)/shard_map/pallas_call | solution.py:93
  56.2 2.5 %shard_map.103 = bf16[2,768,128]{2,1,0:T(8,128)(2,1)} custom-call(s32[2]{0:T(128)} %pad_add_fusion.where, s32[8,8]{1,0:T(8,128)} %bitcast.6.handed, bf16[8,512,128]{2,1,0:T(8,128)(2,1)} %bitcast.51, bf16[64,4096]{1,0:T(8,128)(2,1)} %bitcast.65), custom_call_target="tpu_custom_call" | custom-call | flops 100000 | bytes 786432 | tf_op jit(solution)/shard_map/pallas_call | solution.py:93
  58.8 0.0 copy-start
  58.8 0.0 copy-start.6
  58.8 0.0 copy-start.7
  58.8 1.5 collective-permute-start
  60.3 0.2 collective-permute-start.1
  60.5 2.5 %collective-permute-start.9 = (bf16[2,512,128]{2,1,0:T(8,128)(2,1)}, bf16[2,512,128]{2,1,0:T(8,128)(2,1)S(1)}, u32[]{:S(2)}, u32[]{:S(2)}) collective-permute-start(bf16[2,512,128]{2,1,0:T(8,128)(2,1)} %pad_maximum_fusion.1), channel_id=1, source_target_pairs={{0,2},{1,3},{2,0},{3,1},{4,6},{5,7},{6,4},{7,5},{8,10},{9,11},{10,... | collective-permute-start | bytes 786440 | tf_op jit(solution)/shard_map/ppermute | solution.py:529
  63.0 0.0 collective-permute-start.10
  63.0 1.6 constant_dynamic-update-slice_fusion.3
  64.5 0.0 collective-permute-done.8
  64.5 2.7 %collective-permute-start.5 = (bf16[2,768,128]{2,1,0:T(8,128)(2,1)}, bf16[2,768,128]{2,1,0:T(8,128)(2,1)S(1)}, u32[]{:S(2)}, u32[]{:S(2)}) collective-permute-start(bf16[2,768,128]{2,1,0:T(8,128)(2,1)} %shard_map.103), channel_id=1, source_target_pairs={{0,4},{1,5},{2,6},{3,7},{4,0},{5,1},{6,2},{7,3},{8,12},{9,13},{10,... | collective-permute-start | bytes 1179656 | tf_op jit(solution)/shard_map/ppermute | solution.py:529
  67.3 1.7 constant_dynamic-update-slice_fusion.2
  68.9 15.8 %collective-permute-done.9 = bf16[2,512,128]{2,1,0:T(8,128)(2,1)S(1)} collective-permute-done((bf16[2,512,128]{2,1,0:T(8,128)(2,1)}, bf16[2,512,128]{2,1,0:T(8,128)(2,1)S(1)}, u32[]{:S(2)}, u32[]{:S(2)}) %collective-permute-start.9) | collective-permute-done | bytes 262176 | tf_op jit(solution)/shard_map/ppermute | solution.py:529
  84.8 3.4 %collective-permute-start.6 = (bf16[2,768,128]{2,1,0:T(8,128)(2,1)}, bf16[2,768,128]{2,1,0:T(8,128)(2,1)S(1)}, u32[]{:S(2)}, u32[]{:S(2)}) collective-permute-start(bf16[2,768,128]{2,1,0:T(8,128)(2,1)} %get-tuple-element.23), channel_id=1, source_target_pairs={{0,5},{1,4},{2,7},{3,6},{4,1},{5,0},{6,3},{7,2},{8,13},{9,12},{10,... | collective-permute-start | bytes 1179656 | tf_op jit(solution)/shard_map/ppermute | solution.py:529
  88.2 0.7 constant_dynamic-update-slice_fusion.1
  88.9 1.6 collective-permute-done.10
  90.5 0.8 collective-permute-start.2
  91.3 0.7 constant_dynamic-update-slice_fusion.mids
  92.0 2.2 %gather_fusion = bf16[256,128]{1,0:T(8,128)(2,1)S(1)} fusion(bf16[4096,128]{1,0:T(8,128)(2,1)} %bitcast.56, s32[1024]{0:T(1024)} %pad_clamp_fusion), kind=kCustom, calls=%fused_computation | custom fusion | bytes 132096 | tf_op jit(solution)/shard_map/gather | solution.py:613
  94.3 1.0 slice_reduce_fusion
  95.3 25.8 %collective-permute-done.5.refs_0_ = bf16[2,768,128]{2,1,0:T(8,128)(2,1)S(1)} collective-permute-done((bf16[2,768,128]{2,1,0:T(8,128)(2,1)}, bf16[2,768,128]{2,1,0:T(8,128)(2,1)S(1)}, u32[]{:S(2)}, u32[]{:S(2)}) %collective-permute-start.5) | collective-permute-done | bytes 393248 | tf_op jit(solution)/shard_map/ppermute | solution.py:529
  121.1 0.0 collective-permute-start.3
  121.1 8.5 %collective-permute-done.6.refs_1_ = bf16[2,768,128]{2,1,0:T(8,128)(2,1)S(1)} collective-permute-done((bf16[2,768,128]{2,1,0:T(8,128)(2,1)}, bf16[2,768,128]{2,1,0:T(8,128)(2,1)S(1)}, u32[]{:S(2)}, u32[]{:S(2)}) %collective-permute-start.6) | collective-permute-done | bytes 393248 | tf_op jit(solution)/shard_map/ppermute | solution.py:529
  129.5 0.7 collective-permute-start.4
  130.2 0.0 copy-done
  130.2 0.0 copy-done.6
  130.2 0.0 copy-done.7
  130.2 1.0 copy-done.8
  131.3 1.0 copy-done.9
  132.3 3.3 %shard_map.105.refs_3_ = f32[8,64,512]{2,1,0:T(8,128)S(1)} custom-call(s32[8,128]{1,0:T(8,128)S(1)} %copy-done.6, bf16[8,512,128]{2,1,0:T(8,128)(2,1)S(1)} %bitcast.52, f32[8,8,512]{2,1,0:T(8,128)S(1)} %copy-done.7, bf16[2,768,128]{2,1,0:T(8,128)(2,1)S(1)} %collective-permute-done.5.refs_0_, bf16[2,768,128]{2,1,0:T(8,128)(2,1)S(1)} %collective-permute-done.6.refs_1_, ...), custom_call_target="tpu_custom_call" | custom-call | flops 6442450944 | bytes 3000000 | tf_op jit(solution)/shard_map/pallas_call | solution.py:93
  135.7 0.0 collective-permute-done.2.refs_0_
  135.7 11.0 %collective-permute-start.11 = (bf16[1,384,128]{2,1,0:T(8,128)(2,1)S(1)}, bf16[1,384,128]{2,1,0:T(8,128)(2,1)S(1)}, u32[]{:S(2)}, u32[]{:S(2)}) collective-permute-start(bf16[1,384,128]{2,1,0:T(8,128)(2,1)S(1)} %maximum_bitcast_fusion), channel_id=1, source_target_pairs={{0,8},{8,0},{16,24},{24,16},{1,9},{9,1},{17,25},{25,17},{2,10},{10... | collective-permute-start | bytes 294920 | tf_op jit(solution)/shard_map/ppermute | solution.py:529
  146.7 0.0 collective-permute-done.3.refs_1_
  146.7 0.0 collective-permute-done.4.refs_2_
  146.7 18.2 %shard_map.106.refs_1_ = f32[8,64,512]{2,1,0:T(8,128)S(1)} custom-call(s32[8,128]{1,0:T(8,128)S(1)} %copy-done.6, bf16[8,512,128]{2,1,0:T(8,128)(2,1)S(1)} %bitcast.53, f32[8,8,512]{2,1,0:T(8,128)S(1)} %copy-done.7, bf16[2,768,128]{2,1,0:T(8,128)(2,1)S(1)} %collective-permute-done.2.refs_0_, ...), custom_call_target="tpu_custom_call", output_to_operand_aliasing={{}: (6, {})} | custom-call | flops 9663676416 | bytes 3000000 | tf_op jit(solution)/shard_map/pallas_call | solution.py:93
  164.8 0.0 collective-permute-done.11
  164.9 0.0 copy-start.1
  164.9 0.0 copy-start.3
  164.9 0.0 copy-start.4
  164.9 0.0 copy-start.5
  164.9 0.1 collective-permute-start.12
  165.0 0.0 collective-permute-done.1.refs_0_
  165.0 0.0 copy-start.2
  165.0 2.1 %shard_map.107.refs_1_ = f32[8,64,512]{2,1,0:T(8,128)S(1)} custom-call(s32[8,128]{1,0:T(8,128)S(1)} %copy-done.6, bf16[8,512,128]{2,1,0:T(8,128)(2,1)S(1)} %bitcast.54, f32[8,8,512]{2,1,0:T(8,128)S(1)} %copy-done.7, bf16[2,768,128]{2,1,0:T(8,128)(2,1)S(1)} %collective-permute-done.1.refs_0_, ...), custom_call_target="tpu_custom_call", output_to_operand_aliasing={{}: (4, {})} | custom-call | flops 3221225472 | bytes 3000000 | tf_op jit(solution)/shard_map/pallas_call | solution.py:93
  167.1 3.6 %collective-permute-done.12 = bf16[2,384,128]{2,1,0:T(8,128)(2,1)S(1)} collective-permute-done((bf16[2,384,128]{2,1,0:T(8,128)(2,1)S(1)}, bf16[2,384,128]{2,1,0:T(8,128)(2,1)S(1)}, u32[]{:S(2)}, u32[]{:S(2)}) %collective-permute-start.12) | collective-permute-done | bytes 196640 | tf_op jit(solution)/shard_map/ppermute | solution.py:529
  170.8 3.8 %shard_map.109.refs_2_ = f32[8,64,512]{2,1,0:T(8,128)S(1)} custom-call(s32[4]{0:T(128)S(1)} %copy-done.5, bf16[8,512,128]{2,1,0:T(8,128)(2,1)S(1)} %copy-done.1, bf16[4,384,128]{2,1,0:T(8,128)(2,1)S(1)} %pad_maximum_fusion.tops, bf16[256,256]{1,0:T(8,128)(2,1)S(1)} %bitcast.60, bf16[2048,256]{1,0:T(8,128)(2,1)S(1)} %bitcast.58, ...), custom_call_target="tpu_custom_call" | custom-call | flops 1000000000 | bytes 6000000 | tf_op jit(solution)/shard_map/pallas_call | solution.py:93
  174.6 0.0 collective-permute-done.refs_0_
  174.6 8.1 %shard_map.110 = f32[64,4096]{1,0:T(8,128)} custom-call(s32[8,128]{1,0:T(8,128)S(1)} %copy-done.6, bf16[8,512,128]{2,1,0:T(8,128)(2,1)S(1)} %bitcast.55, f32[8,8,512]{2,1,0:T(8,128)S(1)} %copy-done.7, bf16[2,768,128]{2,1,0:T(8,128)(2,1)S(1)} %collective-permute-done.refs_0_, f32[8,64,512]{2,1,0:T(8,128)S(1)} %shard_map.107.refs_1_, ...), custom_call_target="tpu_custom_call" | custom-call | flops 3221225472 | bytes 3000000 | tf_op jit(solution)/shard_map/pallas_call | solution.py:93
  (10 shorter events, 0.1 us)
Async XLA Ops:
  2.3 49.1 %all-to-all-start = ((s32[8,1,8]{2,1,0:T(1,128)}), s32[8,1,8]{2,1,0:T(1,128)}, u32[]{:S(2)}, u32[]{:S(2)}) async-start(s32[8,1,8]{2,1,0:T(1,128)} %bitcast.68), calls=%async_computation | async-start | bytes 8192 | tf_op jit(solution)/shard_map/all_to_all | solution.py:591
  15.3 32.5 %collective-permute-start.7 = (bf16[512,128]{1,0:T(8,128)(2,1)}, bf16[512,128]{1,0:T(8,128)(2,1)}, u32[]{:S(2)}, u32[]{:S(2)}) collective-permute-start(bf16[512,128]{1,0:T(8,128)(2,1)} %shard_map.108), channel_id=1, source_target_pairs={{0,4},{1,5},{2,6},{3,7},{4,0},{5,1},{6,2},{7,3},{8,12},{9,13},{10,... | collective-permute-start | bytes 393224 | tf_op jit(solution)/shard_map/ppermute | solution.py:529
  49.5 15.0 %collective-permute-start.8 = (bf16[2,512,128]{2,1,0:T(8,128)(2,1)}, bf16[2,512,128]{2,1,0:T(8,128)(2,1)}, u32[]{:S(2)}, u32[]{:S(2)}) collective-permute-start(bf16[2,512,128]{2,1,0:T(8,128)(2,1)} %pad_maximum_fusion.1), channel_id=1, source_target_pairs={{0,1},{1,0},{2,3},{3,2},{4,5},{5,4},{6,7},{7,6},{8,9},{9,8},{10,11... | collective-permute-start | bytes 786440 | tf_op jit(solution)/shard_map/ppermute | solution.py:529
  58.8 71.5 %copy-start = (bf16[4096,128]{1,0:T(8,128)(2,1)S(1)}, bf16[4096,128]{1,0:T(8,128)(2,1)}, u32[]{:S(2)}) copy-start(bf16[4096,128]{1,0:T(8,128)(2,1)} %param.10) | copy-start | bytes 3145732
  58.8 71.5 %copy-start.6 = (s32[8,128]{1,0:T(8,128)S(1)}, s32[8,128]{1,0:T(8,128)}, u32[]{:S(2)}) copy-start(s32[8,128]{1,0:T(8,128)} %get-tuple-element.15.pool) | copy-start | bytes 12292
  58.8 71.5 %copy-start.7 = (f32[8,8,512]{2,1,0:T(8,128)S(1)}, f32[8,8,512]{2,1,0:T(8,128)}, u32[]{:S(2)}) copy-start(f32[8,8,512]{2,1,0:T(8,128)} %get-tuple-element.16.refs_0_.tsq) | copy-start | bytes 393220
  58.8 115.8 %collective-permute-start = (bf16[2,768,128]{2,1,0:T(8,128)(2,1)}, bf16[2,768,128]{2,1,0:T(8,128)(2,1)S(1)}, u32[]{:S(2)}, u32[]{:S(2)}) collective-permute-start(bf16[2,768,128]{2,1,0:T(8,128)(2,1)} %get-tuple-element.18), channel_id=1, source_target_pairs={{0,7},{1,6},{2,5},{3,4},{4,3},{5,2},{6,1},{7,0},{8,15},{9,14},{10,... | collective-permute-start | bytes 1179656 | tf_op jit(solution)/shard_map/ppermute | solution.py:529
  60.3 104.7 %collective-permute-start.1 = (bf16[2,768,128]{2,1,0:T(8,128)(2,1)}, bf16[2,768,128]{2,1,0:T(8,128)(2,1)S(1)}, u32[]{:S(2)}, u32[]{:S(2)}) collective-permute-start(bf16[2,768,128]{2,1,0:T(8,128)(2,1)} %get-tuple-element.19), channel_id=1, source_target_pairs={{0,6},{1,7},{2,4},{3,5},{4,2},{5,3},{6,0},{7,1},{8,14},{9,15},{10,... | collective-permute-start | bytes 1179656 | tf_op jit(solution)/shard_map/ppermute | solution.py:529
  60.5 24.3 %collective-permute-start.9 = (bf16[2,512,128]{2,1,0:T(8,128)(2,1)}, bf16[2,512,128]{2,1,0:T(8,128)(2,1)S(1)}, u32[]{:S(2)}, u32[]{:S(2)}) collective-permute-start(bf16[2,512,128]{2,1,0:T(8,128)(2,1)} %pad_maximum_fusion.1), channel_id=1, source_target_pairs={{0,2},{1,3},{2,0},{3,1},{4,6},{5,7},{6,4},{7,5},{8,10},{9,11},{10,... | collective-permute-start | bytes 786440 | tf_op jit(solution)/shard_map/ppermute | solution.py:529
  63.0 27.6 %collective-permute-start.10 = (bf16[2,512,128]{2,1,0:T(8,128)(2,1)}, bf16[2,512,128]{2,1,0:T(8,128)(2,1)S(1)}, u32[]{:S(2)}, u32[]{:S(2)}) collective-permute-start(bf16[2,512,128]{2,1,0:T(8,128)(2,1)} %pad_maximum_fusion.1), channel_id=1, source_target_pairs={{0,3},{1,2},{2,1},{3,0},{4,7},{5,6},{6,5},{7,4},{8,11},{9,10},{10,... | collective-permute-start | bytes 786440 | tf_op jit(solution)/shard_map/ppermute | solution.py:529
  64.5 56.5 %collective-permute-start.5 = (bf16[2,768,128]{2,1,0:T(8,128)(2,1)}, bf16[2,768,128]{2,1,0:T(8,128)(2,1)S(1)}, u32[]{:S(2)}, u32[]{:S(2)}) collective-permute-start(bf16[2,768,128]{2,1,0:T(8,128)(2,1)} %shard_map.103), channel_id=1, source_target_pairs={{0,4},{1,5},{2,6},{3,7},{4,0},{5,1},{6,2},{7,3},{8,12},{9,13},{10,... | collective-permute-start | bytes 1179656 | tf_op jit(solution)/shard_map/ppermute | solution.py:529
  84.8 44.7 %collective-permute-start.6 = (bf16[2,768,128]{2,1,0:T(8,128)(2,1)}, bf16[2,768,128]{2,1,0:T(8,128)(2,1)S(1)}, u32[]{:S(2)}, u32[]{:S(2)}) collective-permute-start(bf16[2,768,128]{2,1,0:T(8,128)(2,1)} %get-tuple-element.23), channel_id=1, source_target_pairs={{0,5},{1,4},{2,7},{3,6},{4,1},{5,0},{6,3},{7,2},{8,13},{9,12},{10,... | collective-permute-start | bytes 1179656 | tf_op jit(solution)/shard_map/ppermute | solution.py:529
  90.5 45.1 %collective-permute-start.2 = (bf16[2,768,128]{2,1,0:T(8,128)(2,1)}, bf16[2,768,128]{2,1,0:T(8,128)(2,1)S(1)}, u32[]{:S(2)}, u32[]{:S(2)}) collective-permute-start(bf16[2,768,128]{2,1,0:T(8,128)(2,1)} %get-tuple-element.20), channel_id=1, source_target_pairs={{0,1},{1,0},{2,3},{3,2},{4,5},{5,4},{6,7},{7,6},{8,9},{9,8},{10,11... | collective-permute-start | bytes 1179656 | tf_op jit(solution)/shard_map/ppermute | solution.py:529
  121.1 25.6 %collective-permute-start.3 = (bf16[2,768,128]{2,1,0:T(8,128)(2,1)}, bf16[2,768,128]{2,1,0:T(8,128)(2,1)S(1)}, u32[]{:S(2)}, u32[]{:S(2)}) collective-permute-start(bf16[2,768,128]{2,1,0:T(8,128)(2,1)} %get-tuple-element.21), channel_id=1, source_target_pairs={{0,2},{1,3},{2,0},{3,1},{4,6},{5,7},{6,4},{7,5},{8,10},{9,11},{10,... | collective-permute-start | bytes 1179656 | tf_op jit(solution)/shard_map/ppermute | solution.py:529
  129.5 17.1 %collective-permute-start.4 = (bf16[2,768,128]{2,1,0:T(8,128)(2,1)}, bf16[2,768,128]{2,1,0:T(8,128)(2,1)S(1)}, u32[]{:S(2)}, u32[]{:S(2)}) collective-permute-start(bf16[2,768,128]{2,1,0:T(8,128)(2,1)} %get-tuple-element.22), channel_id=1, source_target_pairs={{0,3},{1,2},{2,1},{3,0},{4,7},{5,6},{6,5},{7,4},{8,11},{9,10},{10,... | collective-permute-start | bytes 1179656 | tf_op jit(solution)/shard_map/ppermute | solution.py:529
  130.2 1.0 copy-start.8
  131.3 1.0 copy-start.9
  135.7 29.2 %collective-permute-start.11 = (bf16[1,384,128]{2,1,0:T(8,128)(2,1)S(1)}, bf16[1,384,128]{2,1,0:T(8,128)(2,1)S(1)}, u32[]{:S(2)}, u32[]{:S(2)}) collective-permute-start(bf16[1,384,128]{2,1,0:T(8,128)(2,1)S(1)} %maximum_bitcast_fusion), channel_id=1, source_target_pairs={{0,8},{8,0},{16,24},{24,16},{1,9},{9,1},{17,25},{25,17},{2,10},{10... | collective-permute-start | bytes 294920 | tf_op jit(solution)/shard_map/ppermute | solution.py:529
  164.9 5.9 %copy-start.1 = (bf16[8,512,128]{2,1,0:T(8,128)(2,1)S(1)}, bf16[8,512,128]{2,1,0:T(8,128)(2,1)}, u32[]{:S(2)}) copy-start(bf16[8,512,128]{2,1,0:T(8,128)(2,1)} %constant_dynamic-update-slice_fusion.mids) | copy-start | bytes 3145732
  164.9 5.9 %copy-start.3 = (bf16[1,2048,256]{2,1,0:T(8,128)(2,1)S(1)}, bf16[1,2048,256]{2,1,0:T(8,128)(2,1)}, u32[]{:S(2)}) copy-start(bf16[1,2048,256]{2,1,0:T(8,128)(2,1)} %param.15) | copy-start | bytes 3145732
  164.9 5.9 %copy-start.4 = (bf16[1,256,256]{2,1,0:T(8,128)(2,1)S(1)}, bf16[1,256,256]{2,1,0:T(8,128)(2,1)}, u32[]{:S(2)}) copy-start(bf16[1,256,256]{2,1,0:T(8,128)(2,1)} %param.18) | copy-start | bytes 393220
  164.9 5.9 %copy-start.5 = (s32[4]{0:T(128)S(1)}, s32[4]{0:T(128)}, u32[]{:S(2)}) copy-start(s32[4]{0:T(128)} %fusion.4.partners) | copy-start | bytes 52
  164.9 5.8 %collective-permute-start.12 = (bf16[2,384,128]{2,1,0:T(8,128)(2,1)S(1)}, bf16[2,384,128]{2,1,0:T(8,128)(2,1)S(1)}, u32[]{:S(2)}, u32[]{:S(2)}) collective-permute-start(bf16[2,384,128]{2,1,0:T(8,128)(2,1)S(1)} %pad_maximum_fusion.2), channel_id=1, source_target_pairs={{0,16},{8,24},{16,0},{24,8},{1,17},{9,25},{17,1},{25,9},{2,18},{10... | collective-permute-start | bytes 589832 | tf_op jit(solution)/shard_map/ppermute | solution.py:529
  165.0 5.8 %copy-start.2 = (bf16[8,512,256]{2,1,0:T(8,128)(2,1)S(1)}, bf16[8,512,256]{2,1,0:T(8,128)(2,1)}, u32[]{:S(2)}) copy-start(bf16[8,512,256]{2,1,0:T(8,128)(2,1)} %leaf_interp.1) | copy-start | bytes 6291460

commit v4 on v3

--- a/solution.py
+++ b/solution.py
@@ -35,19 +35,17 @@
     sq = xf * xf
     high = sq.astype(bf16)
     low = (sq - high.astype(f32)).astype(bf16)
-    return high, low
+    return jnp.concatenate((high, low), axis=1)
 
 
 def source_term(x):
-    high, low = squares(x)
-    ones = jnp.ones((x.shape[1], LANES), bf16)
-    return (dot(high, ones) + dot(low, ones)) * (-kernel_rate * LOG2E)
+    ones = jnp.ones((2 * x.shape[1], LANES), bf16)
+    return dot(squares(x), ones) * (-kernel_rate * LOG2E)
 
 
 def target_term(x):
-    high, low = squares(x)
-    ones = jnp.ones((8, x.shape[1]), bf16)
-    return (dot_rows(ones, high) + dot_rows(ones, low)) * (-kernel_rate * LOG2E)
+    ones = jnp.ones((8, 2 * x.shape[1]), bf16)
+    return dot_rows(ones, squares(x)) * (-kernel_rate * LOG2E)
 
 
 def kernel_tile(source, source_sq, target, target_sq):
@@ -160,11 +158,14 @@
     )
 
 
-def pack_kernel(leaf_size, distances, where, handed, points, charges, *refs):
-    outs, (x, q, sem_x, sem_q, sem_out) = refs[: len(distances)], refs[len(distances) :]
+def pack_kernel(leaf_size, distances, count, where, handed, points, charges, *refs):
+    blocks, refs = refs[:count], refs[count:]
+    outs, (x, q, mid, sem_x, sem_q, sem_m, sem_out) = refs[: len(distances)], refs[len(distances) :]
     self_index = where[1]
     rhs = charges.shape[0]
+    rows = leaf_size + leaf_size // LANES * rhs
     taken, given = [], []
+    mid_copies = [copy_in(block, mid.at[at], sem_m.at[at]) for at, block in enumerate(blocks)]
     for at, distance in enumerate(distances):
         peer = jnp.bitwise_xor(self_index, distance)
         for slot in range(CAP):
@@ -177,42 +178,61 @@
                     copy_in(charges.at[:, lanes], q.at[put], sem_q.at[put]),
                 )
             )
+    for waited in mid_copies:
+        waited.wait()
+    tiles = leaf_size // LANES
     for at, out in enumerate(outs):
         for slot in range(CAP):
             put = at * CAP + slot
+            base = slot * rows
             taken[put][0].wait()
-            given.append(copy_in(x.at[put], out.at[slot, :leaf_size, :], sem_out.at[put, 0]))
+            given.append(
+                copy_in(x.at[put], out.at[base : base + leaf_size, :], sem_out.at[put, 0])
+            )
             taken[put][1].wait()
-            for tile in range(leaf_size // LANES):
-                rows = pl.ds(leaf_size + tile * rhs, rhs)
+            for tile in range(tiles):
+                row = base + leaf_size + tile * rhs
                 lanes = pl.ds(tile * LANES, LANES)
                 given.append(
                     copy_in(
-                        q.at[put, :, lanes], out.at[slot, rows, :], sem_out.at[put, 1 + tile]
+                        q.at[put, :, lanes], out.at[row : row + rhs, :], sem_out.at[put, 1 + tile]
                     )
                 )
+        for block in range(count):
+            row = CAP * rows + block * mid.shape[1]
+            given.append(
+                copy_in(
+                    mid.at[block],
+                    out.at[row : row + mid.shape[1], :],
+                    sem_out.at[at * CAP, 1 + tiles + block],
+                )
+            )
     for one in given:
         one.wait()
 
 
-def pack(where, handed, points, charges, distances):
+def pack(where, handed, points, charges, distances, *blocks):
     _, leaf_size, coords = points.shape
     rhs = charges.shape[0]
-    rows = leaf_size + leaf_size // LANES * rhs
+    rows = CAP * (leaf_size + leaf_size // LANES * rhs)
+    each = blocks[0].shape[0] if blocks else 16
+    rows += len(blocks) * each
     places = len(distances) * CAP
     sem = pltpu.SemaphoreType.DMA
     return call(
-        functools.partial(pack_kernel, leaf_size, distances),
-        [jax.ShapeDtypeStruct((CAP, rows, coords), bf16) for _ in distances],
-        [smem(), smem(), in_hbm(), in_hbm()],
-        cost(1e5, 2 * places * rows * coords * 2),
-        (where, handed, points, charges),
+        functools.partial(pack_kernel, leaf_size, distances, len(blocks)),
+        [jax.ShapeDtypeStruct((rows, coords), bf16) for _ in distances],
+        [smem(), smem()] + [in_hbm()] * (2 + len(blocks)),
+        cost(1e5, 2 * len(distances) * rows * coords * 2),
+        (where, handed, points, charges) + blocks,
         scratch=[
             pltpu.VMEM((places, leaf_size, coords), bf16),
             pltpu.VMEM((places, rhs, leaf_size), bf16),
+            pltpu.VMEM((max(len(blocks), 1), each, coords), bf16),
             sem((places,)),
             sem((places,)),
-            sem((places, 1 + leaf_size // LANES)),
+            sem((max(len(blocks), 1),)),
+            sem((places, 1 + leaf_size // LANES + len(blocks))),
         ],
         own=None,
         outs=[in_hbm()] * len(distances),
@@ -314,11 +334,9 @@
 
 def near_remote_kernel(near_count, first, parts, stage, pool, points, tsq, *refs):
     got, refs = refs[:parts], refs[parts:]
-    taken = {"first": 2, "middle": 1, "last": 2}[stage]
+    taken = 2 if stage == "first" else 1
     inits, refs = refs[:taken], refs[taken:]
-    out, tl, sl, x, pts, ssq, qs = refs[:7]
-    sem_got, sem_x, sem_acc = refs[-3:]
-    acc = refs[7] if stage == "last" else out
+    acc, tl, sl, x, pts, ssq, qs, sem_got, sem_x, sem_acc = refs
     leaf_dev, leaf_size, _ = points.shape
     rhs = acc.shape[1]
     tiles = leaf_size // LANES
@@ -327,13 +345,14 @@
     for part, message in enumerate(got):
         for slot in range(CAP):
             at = part * CAP + slot
-            one = [copy_in(message.at[slot, :leaf_size, :], pts.at[at], sem_got.at[at, 0])]
+            base = slot * (leaf_size + tiles * rhs)
+            one = [copy_in(message.at[base : base + leaf_size, :], pts.at[at], sem_got.at[at, 0])]
             for tile in range(tiles):
-                rows = pl.ds(leaf_size + tile * rhs, rhs)
+                row = base + leaf_size + tile * rhs
                 lanes = pl.ds(tile * LANES, LANES)
                 one.append(
                     copy_in(
-                        message.at[slot, rows, :], qs.at[at, :, lanes], sem_got.at[at, 1 + tile]
+                        message.at[row : row + rhs, :], qs.at[at, :, lanes], sem_got.at[at, 1 + tile]
                     )
                 )
             moves.append(one)
@@ -345,9 +364,6 @@
             rows = pl.ds(base, init.shape[0])
             acc_copies.append(copy_in(init, acc.at[rows], sem_acc.at[at]))
             base += init.shape[0]
-    if stage == "last":
-        for leaf in range(leaf_dev):
-            acc[leaf] = inits[0][leaf] + inits[1][leaf]
     for at, one in enumerate(moves):
         one[0].wait()
         ssq[at] = source_term(pts[at])
@@ -366,9 +382,6 @@
         return kernel_tile(pts[source], ssq[source], x[target], tsq[target])
 
     run_pairs(pool, near_count, (0, leaf_dev), keep, tl, sl, tile_of, lambda s: qs[s], acc, 0)
-    if stage == "last":
-        for leaf in range(leaf_dev):
-            out[:, leaf * leaf_size : (leaf + 1) * leaf_size] = acc[leaf]
 
 
 def near_remote(pool, near_count, points, tsq, first, got, inits, stage):
@@ -376,7 +389,6 @@
     rhs = inits[0].shape[1]
     places = len(got) * CAP
     sums = (leaf_dev, rhs, leaf_size)
-    last = stage == "last"
     scratch = [
         pltpu.SMEM((leaf_dev * near_count + 1,), i32),
         pltpu.SMEM((leaf_dev * near_count + 1,), i32),
@@ -384,19 +396,14 @@
         pltpu.VMEM((places, leaf_size, coords), bf16),
         pltpu.VMEM((places, leaf_size, LANES), f32),
         pltpu.VMEM((places, rhs, leaf_size), bf16),
-    ]
-    if last:
-        scratch.append(pltpu.VMEM(sums, f32))
-    scratch += [
         pltpu.SemaphoreType.DMA((places, 1 + leaf_size // LANES)),
         pltpu.SemaphoreType.DMA,
         pltpu.SemaphoreType.DMA((2,)),
     ]
     spec = in_hbm() if stage == "first" else vmem()
-    shape = (rhs, leaf_dev * leaf_size) if last else sums
     return call(
         functools.partial(near_remote_kernel, near_count, first, len(got), stage),
-        jax.ShapeDtypeStruct(shape, f32),
+        jax.ShapeDtypeStruct(sums, f32),
         [smem(), in_hbm(), vmem()] + [in_hbm()] * len(got) + [spec] * len(inits),
         near_cost(len(got) * leaf_dev, leaf_size, coords, rhs),
         (pool, points, tsq, *got, *inits),
@@ -486,9 +493,63 @@
     )
 
 
-def far_kernel(partners, mids, tops, interp_top, interp_mid, leaf_interp, out):
-    leaf_dev, _, skel = leaf_interp.shape
-    rhs = out.shape[1]
+def place(distance, size):
+    half = size // 2
+    return lax.rem(distance, half) * 2 + lax.div(distance, half)
+
+
+def top_kernel(near_rows, where, skel_top, own, across_own, *refs):
+    inner = len(refs) - 3
+    got, (mids, out, sem) = refs[:inner], refs[inner:]
+    size, rows, _ = mids.shape
+    skel = skel_top.shape[1]
+    copies = [copy_in(own, mids.at[0], sem.at[0]), copy_in(across_own, mids.at[1], sem.at[1])]
+    for at, message in enumerate(got, 1):
+        for side in range(2):
+            row = near_rows + side * rows
+            to = at * 2 + side
+            copies.append(copy_in(message.at[row : row + rows, :], mids.at[to], sem.at[to]))
+    picked = skel_top[...]
+    distance = jnp.bitwise_xor(lax.div(picked, skel), where[1])
+    index = place(distance, size) * skel + lax.rem(picked, skel)
+    at = lax.broadcasted_iota(i32, (skel, skel), 0)
+    columns = (((0,), (0,)), ((), ()))
+    points = jnp.zeros((skel, mids.shape[2]), f32)
+    first = skel + (rows - skel) // 2
+    weight = jnp.zeros((rows - first, mids.shape[2]), f32)
+    for p in range(size):
+        one_hot = (at == index - p * skel).astype(f32).astype(bf16)
+        copies[p].wait()
+        points = points + lax.dot_general(
+            one_hot, mids[p, :skel, :], columns, preferred_element_type=f32
+        )
+        weight = weight + mids[p, first:, :].astype(f32)
+    out[:skel, :] = points.astype(bf16)
+    out[skel:, :] = weight.astype(bf16)
+
+
+def top_prepare(near_rows, where, skel_top, own, across_own, got):
+    rows, coords = own.shape
+    skel = skel_top.shape[1]
+    size = 2 + 2 * len(got)
+    return call(
+        functools.partial(top_kernel, near_rows),
+        [
+            jax.ShapeDtypeStruct((size, rows, coords), bf16),
+            jax.ShapeDtypeStruct((skel + (rows - skel) // 2, coords), bf16),
+        ],
+        [smem(), vmem()] + [in_hbm()] * (2 + len(got)),
+        cost(1e9, 2e6),
+        (where, skel_top, own, across_own, *got),
+        scratch=[pltpu.SemaphoreType.DMA((size,))],
+        own=2 << 20,
+    )
+
+
+def far_kernel(where, partners, mids, acc, interp_top, interp_mid, leaf_interp, *refs):
+    tops, out = refs[:-1], refs[-1]
+    leaf_dev, leaf_size, skel = leaf_interp.shape
+    rhs = acc.shape[1]
 
     def pair(source_ref, target, target_sq):
         source = source_ref[:skel, :]
@@ -496,71 +557,45 @@
         tile = kernel_tile(source, source_term(source), target, target_sq)
         return dot(weight, tile)
 
-    target = tops[0, :skel, :]
+    target = tops[0][:skel, :]
     target_sq = target_term(target)
     top_sum = jnp.zeros((rhs, skel), f32)
-    for other in range(1, tops.shape[0]):
-        top_sum = top_sum + pair(tops.at[other], target, target_sq)
+    for other in tops[1:]:
+        top_sum = top_sum + pair(other, target, target_sq)
     target = mids[0, :skel, :]
     target_sq = target_term(target)
     mid_sum = jnp.zeros((rhs, skel), f32)
-    for at in range(partners.shape[0]):
-        mid_sum = mid_sum + pair(mids.at[partners[at]], target, target_sq)
+    for at in range(partners.shape[1]):
+        distance = jnp.bitwise_xor(partners[0, at] - where[2], where[1])
+        mid_sum = mid_sum + pair(mids.at[place(distance, mids.shape[0])], target, target_sq)
     total = (mid_sum + dot_rows(top_sum.astype(bf16), interp_top[...])).astype(bf16)
     for m in range(leaf_dev):
         leaf_down = dot_rows(total, interp_mid[m * skel : (m + 1) * skel, :]).astype(bf16)
-        out[m] = dot_rows(leaf_down, leaf_interp[m])
-
-
-def far(partners, mids, tops, interp_top, interp_mid, leaf_interp):
-    leaf_dev, leaf_size, skel = leaf_interp.shape
-    rhs = (mids.shape[1] - skel) // (2 * (skel // LANES))
+        distant = dot_rows(leaf_down, leaf_interp[m])
+        out[:, m * leaf_size : (m + 1) * leaf_size] = acc[m] + distant
+
+
+def far(where, partners, mids, acc, tops, interp_top, interp_mid, leaf_interp):
+    leaf_dev, leaf_size, _ = leaf_interp.shape
+    rhs = acc.shape[1]
     return call(
         far_kernel,
-        jax.ShapeDtypeStruct((leaf_dev, rhs, leaf_size), f32),
-        [smem()] + [vmem()] * 5,
+        jax.ShapeDtypeStruct((rhs, leaf_dev * leaf_size), f32),
+        [smem()] * 2 + [vmem()] * (5 + len(tops)),
         cost(1e9, 6e6, 5e5),
-        (partners, mids, tops, interp_top, interp_mid, leaf_interp),
+        (where, partners, mids, acc, interp_top, interp_mid, leaf_interp, *tops),
         own=1 << 20,
     )
 
 
 def swapped(value, axis, size, distance):
     return lax.ppermute(value, axis, [(i, i ^ distance) for i in range(size)])
-
-
-def share_halves(value, axis, size):
-    half = size // 2
-    pair = jnp.stack((value, swapped(value, axis, size, half)))
-    others = [swapped(pair, axis, size, d) for d in range(1, half)]
-    return jnp.concatenate([pair] + others, axis=0)
-
-
-def place(distance, size):
-    half = size // 2
-    return distance % half * 2 + distance // half
-
-
-def share(value, axis, size):
-    gathered = value[None]
-    while gathered.shape[0] < size:
-        at = gathered.shape[0]
-        other = swapped(gathered, axis, size, at)
-        gathered = jnp.concatenate((gathered, other), axis=0)
-    return gathered
 
 
 def across(group):
     half = group // 2
     cuts = [half, half + max(half // 4, 1), half + half // 2, half + half * 3 // 4, group]
     return [list(range(*cut)) for cut in zip(cuts, cuts[1:])]
-
-
-def near_spans(group):
-    half = group // 2
-    spans = [(half, half + half // 2), (1, half)]
-    spans += [(half + half // 2, half + half * 3 // 4), (half + half * 3 // 4, group)]
-    return [span for span in spans if span[1] > span[0]]
 
 
 def body(
@@ -578,7 +613,7 @@
     group = lax.axis_size("sub")
     groups = lax.axis_size("leaf")
     self_index = lax.axis_index("sub")
-    leaf_dev, leaf_size, skel = leaf_interpolant.shape
+    leaf_dev, leaf_size, _ = leaf_interpolant.shape
     coords = points.shape[1]
     rhs = charges.shape[1]
     near_count = near_leaves.shape[1]
@@ -586,45 +621,44 @@
     blocks = points.reshape(leaf_dev, leaf_size, coords)
     charges_t = charges.T
 
-    where = jnp.stack((group_first * leaf_dev, self_index)).astype(i32)
+    where = jnp.stack((group_first * leaf_dev, self_index, group_first)).astype(i32)
     chosen, pool = want(near_leaves, where, leaf_dev, group)
     handed = lax.all_to_all(chosen, "sub", split_axis=0, concat_axis=0, tiled=True)
 
     message = up(
         blocks, charges_t, leaf_interpolant, interp_mid[0], interp_top[0], skel_leaf, skel_mid
     )
-
-    early = across(group)[0]
+    across_message = swapped(message, "sub", group, group // 2)
+
+    first, second, third, last = across(group)
+    inner = list(range(1, group // 2))
     got = {}
-    for distances in (early, [d for d in range(1, group) if d not in early]):
-        asked = pack(where, handed, blocks, charges_t, distances)
+    for distances, carried in ((first, ()), (second + third + last, ()), (inner, (message, across_message))):
+        asked = pack(where, handed, blocks, charges_t, distances, *carried)
         for distance, one in zip(distances, asked):
             got[distance] = swapped(one, "sub", group, distance)
 
     half = leaf_dev // 2
-    first, tsq = near_local(pool, near_count, blocks, charges_t, (0, half))
-    second = near_local(pool, near_count, blocks, charges_t, (half, leaf_dev), tsq)
-    sums = [first, second]
-
-    mids = share_halves(message, "sub", group)
-    per = rhs * (skel // LANES)
-    picked = skel_top[0]
-    node = place(jnp.bitwise_xor(picked // skel, self_index), group)
-    top_points = mids.reshape(-1, LANES)[node * mids.shape[1] + picked % skel]
-    top_weight = jnp.sum(mids[:, skel + per :, :].astype(f32), axis=0).astype(bf16)
-    tops = share(jnp.concatenate((top_points, top_weight), axis=0), "leaf", groups)
-
-    partners = place(jnp.bitwise_xor(mid_partners[0] - group_first, self_index), group)
-    distant = far(partners, mids, tops, interp_top[0], interp_mid[0], leaf_interpolant)
-    spans = near_spans(group)
-    for at, span in enumerate(spans):
+    sum0, tsq = near_local(pool, near_count, blocks, charges_t, (0, half))
+    sum1 = near_local(pool, near_count, blocks, charges_t, (half, leaf_dev), tsq)
+    sums = [sum0, sum1]
+
+    near_rows = CAP * (leaf_size + leaf_size // LANES * rhs)
+    mids, top_own = top_prepare(
+        near_rows, where, skel_top, message, across_message, [got[d] for d in inner]
+    )
+    tops = [top_own]
+    for distance in range(1, groups):
+        tops.append(swapped(top_own, "leaf", groups, distance))
+
+    for at, span in enumerate((first + second, inner, third + last)):
         stage = "first" if at == 0 else "middle"
-        if at == len(spans) - 1:
-            stage = "last"
-            sums.append(distant)
-        part = [got[distance] for distance in range(*span)]
+        part = [got[distance] for distance in span]
         sums = [near_remote(pool, near_count, blocks, tsq, span[0], part, sums, stage)]
-    return sums[0].T
+    total = far(
+        where, mid_partners, mids, sums[0], tops, interp_top[0], interp_mid[0], leaf_interpolant
+    )
+    return total.T
 
 
 def solution(mesh):

time: 184 us -> 147 us (0.80)
  the two profiles are of different devices: /device:TPU:9 before, /device:TPU:2 now
where the time goes in v4:
time: 147 us; the launch traced here: 146 us
  Pallas kernels  83.2 us (57%)
  waiting for transfers between devices  35.8 us (24%)
  starting transfers between devices  21.2 us (14%)
  local copies, waits for them, and re-layouts  4.93 us (3%)
    pallas_call x12, Pallas kernels, call(): pl.pallas_call(kernel, out_shape=out_shape, in_specs=in_specs, out_specs=...  83.2 us
    ppermute x11, waiting for transfers between devices, swapped(): return lax.ppermute(value, axis, [(i, i ^ distance) for i in range(size)])  35.8 us
    ppermute x11, starting transfers between devices, swapped(): return lax.ppermute(value, axis, [(i, i ^ distance) for i in range(size)])  15.3 us
    all_to_all x1, starting transfers between devices, body(): lax.all_to_all(chosen, 'sub', split_axis=0, concat_axis=0, tiled=True)  5.83 us
    unnamed x30, local copies, waits for them, and re-layouts  4.93 us
  transfers between devices with their start and end apart: 12, of which 3 were waited for; matrix products, arithmetic and copies ran while one was open for 0% of the time, Pallas kernels for 53%

profile of v4, /device:TPU:2, one launch (start us, length us, event | category | flops | bytes accessed | tf_op | source)
XLA Modules:
  0.0 146.0 jit_solution(15759432052553800427)
XLA Ops:
  0.0 0.6 pad_add_fusion.where
  0.6 1.7 %shard_map.101 = (s32[8,8]{1,0:T(8,128)}, s32[8,128]{1,0:T(8,128)}) custom-call(s32[3]{0:T(128)} %pad_add_fusion.where, s32[8,12]{1,0:T(8,128)} %near.1), custom_call_target="tpu_custom_call" | custom-call | flops 1000000 | bytes 100000 | tf_op jit(solution)/shard_map/pallas_call | solution.py:91
  2.3 5.8 %all-to-all-start = ((s32[8,1,8]{2,1,0:T(1,128)}), s32[8,1,8]{2,1,0:T(1,128)}, u32[]{:S(2)}, u32[]{:S(2)}) async-start(s32[8,1,8]{2,1,0:T(1,128)} %bitcast.31), calls=%async_computation | async-start | bytes 8192 | tf_op jit(solution)/shard_map/all_to_all | solution.py:626
  8.1 7.3 %shard_map.100.refs_0_.own = bf16[512,128]{1,0:T(8,128)(2,1)} custom-call(bf16[8,512,128]{2,1,0:T(8,128)(2,1)} %bitcast.12, bf16[64,4096]{1,0:T(8,128)(2,1)} %bitcast.25, bf16[8,512,256]{2,1,0:T(8,128)(2,1)} %leaf_interp.1, bf16[2048,256]{1,0:T(8,128)(2,1)} %bitcast.21, bf16[256,256]{1,0:T(8,128)(2,1)} %bitcast.23, s32[8,256]{1,0:T(8,128)} %refs_5_.1, ...), custom_call_target="tpu_custom_call" | custom-call | flops 3000000000 | bytes 5000000 | tf_op jit(solution)/shard_map/pallas_call | solution.py:91
  15.4 3.0 %collective-permute-start = (bf16[512,128]{1,0:T(8,128)(2,1)}, bf16[512,128]{1,0:T(8,128)(2,1)}, u32[]{:S(2)}, u32[]{:S(2)}) collective-permute-start(bf16[512,128]{1,0:T(8,128)(2,1)} %shard_map.100.refs_0_.own), channel_id=1, source_target_pairs={{0,4},{1,5},{2,6},{3,7},{4,0},{5,1},{6,2},{7,3},{8,12},{9,13},{10,... | collective-permute-start | bytes 393224 | tf_op jit(solution)/shard_map/ppermute | solution.py:592
  18.4 14.0 %shard_map.104 = (f32[4,64,512]{2,1,0:T(8,128)}, f32[8,8,512]{2,1,0:T(8,128)}) custom-call(s32[8,128]{1,0:T(8,128)} %get-tuple-element.22.pool, bf16[8,512,128]{2,1,0:T(8,128)(2,1)} %bitcast.13, bf16[64,4096]{1,0:T(8,128)(2,1)} %bitcast.26), custom_call_target="tpu_custom_call" | custom-call | flops 9663676416 | bytes 3000000 | tf_op jit(solution)/shard_map/pallas_call | solution.py:91
  32.4 0.0 all-to-all-done
  32.4 3.6 %shard_map.105 = (bf16[1536,128]{1,0:T(8,128)(2,1)}, bf16[1536,128]{1,0:T(8,128)(2,1)}, bf16[1536,128]{1,0:T(8,128)(2,1)}) custom-call(s32[3]{0:T(128)} %pad_add_fusion.where, s32[8,8]{1,0:T(8,128)} %bitcast.9.handed, bf16[8,512,128]{2,1,0:T(8,128)(2,1)} %bitcast.14, bf16[64,4096]{1,0:T(8,128)(2,1)} %bitcast.27), custom_call_target="tpu_custom_call" | custom-call | flops 100000 | bytes 2359296 | tf_op jit(solution)/shard_map/pallas_call | solution.py:91
  36.1 2.5 %shard_map.106 = bf16[1536,128]{1,0:T(8,128)(2,1)} custom-call(s32[3]{0:T(128)} %pad_add_fusion.where, s32[8,8]{1,0:T(8,128)} %bitcast.9.handed, bf16[8,512,128]{2,1,0:T(8,128)(2,1)} %bitcast.15, bf16[64,4096]{1,0:T(8,128)(2,1)} %bitcast.28), custom_call_target="tpu_custom_call" | custom-call | flops 100000 | bytes 786432 | tf_op jit(solution)/shard_map/pallas_call | solution.py:91
  38.6 1.5 %collective-permute-start.7 = (bf16[1536,128]{1,0:T(8,128)(2,1)}, bf16[1536,128]{1,0:T(8,128)(2,1)}, u32[]{:S(2)}, u32[]{:S(2)}) collective-permute-start(bf16[1536,128]{1,0:T(8,128)(2,1)} %get-tuple-element.26), channel_id=1, source_target_pairs={{0,5},{1,4},{2,7},{3,6},{4,1},{5,0},{6,3},{7,2},{8,13},{9,12},{10,... | collective-permute-start | bytes 1179656 | tf_op jit(solution)/shard_map/ppermute | solution.py:592
  40.1 2.5 %collective-permute-start.6 = (bf16[1536,128]{1,0:T(8,128)(2,1)}, bf16[1536,128]{1,0:T(8,128)(2,1)}, u32[]{:S(2)}, u32[]{:S(2)}) collective-permute-start(bf16[1536,128]{1,0:T(8,128)(2,1)} %shard_map.106), channel_id=1, source_target_pairs={{0,4},{1,5},{2,6},{3,7},{4,0},{5,1},{6,2},{7,3},{8,12},{9,13},{10,... | collective-permute-start | bytes 1179656 | tf_op jit(solution)/shard_map/ppermute | solution.py:592
  42.6 0.0 collective-permute-done.refs_1_.across_own
  42.6 3.8 %shard_map.102 = (bf16[2560,128]{1,0:T(8,128)(2,1)}, bf16[2560,128]{1,0:T(8,128)(2,1)}, bf16[2560,128]{1,0:T(8,128)(2,1)}) custom-call(s32[3]{0:T(128)} %pad_add_fusion.where, s32[8,8]{1,0:T(8,128)} %bitcast.9.handed, bf16[8,512,128]{2,1,0:T(8,128)(2,1)} %bitcast.16, bf16[64,4096]{1,0:T(8,128)(2,1)} %bitcast.29, bf16[512,128]{1,0:T(8,128)(2,1)} %shard_map.100.refs_0_.own, ...), custom_call_target="tpu_custom_call" | custom-call | flops 100000 | bytes 3932160 | tf_op jit(solution)/shard_map/pallas_call | solution.py:91
  46.5 0.8 collective-permute-start.1
  47.2 0.5 collective-permute-start.2
  47.7 2.3 %collective-permute-start.3 = (bf16[2560,128]{1,0:T(8,128)(2,1)}, bf16[2560,128]{1,0:T(8,128)(2,1)}, u32[]{:S(2)}, u32[]{:S(2)}) collective-permute-start(bf16[2560,128]{1,0:T(8,128)(2,1)} %get-tuple-element.20), channel_id=1, source_target_pairs={{0,3},{1,2},{2,1},{3,0},{4,7},{5,6},{6,5},{7,4},{8,11},{9,10},{10,... | collective-permute-start | bytes 1966088 | tf_op jit(solution)/shard_map/ppermute | solution.py:592
  50.0 13.6 %shard_map.107.refs_3_ = f32[4,64,512]{2,1,0:T(8,128)} custom-call(s32[8,128]{1,0:T(8,128)} %get-tuple-element.22.pool, bf16[8,512,128]{2,1,0:T(8,128)(2,1)} %bitcast.17, bf16[64,4096]{1,0:T(8,128)(2,1)} %bitcast.30, f32[8,8,512]{2,1,0:T(8,128)} %get-tuple-element.23.refs_0_.tsq), custom_call_target="tpu_custom_call" | custom-call | flops 9663676416 | bytes 3000000 | tf_op jit(solution)/shard_map/pallas_call | solution.py:91
  63.7 5.3 %collective-permute-done.7.refs_1_ = bf16[1536,128]{1,0:T(8,128)(2,1)} collective-permute-done((bf16[1536,128]{1,0:T(8,128)(2,1)}, bf16[1536,128]{1,0:T(8,128)(2,1)}, u32[]{:S(2)}, u32[]{:S(2)}) %collective-permute-start.7) | collective-permute-done | bytes 393248 | tf_op jit(solution)/shard_map/ppermute | solution.py:592
  69.0 1.5 collective-permute-start.4
  70.5 7.2 %collective-permute-done.6.refs_0_ = bf16[1536,128]{1,0:T(8,128)(2,1)} collective-permute-done((bf16[1536,128]{1,0:T(8,128)(2,1)}, bf16[1536,128]{1,0:T(8,128)(2,1)}, u32[]{:S(2)}, u32[]{:S(2)}) %collective-permute-start.6) | collective-permute-done | bytes 393248 | tf_op jit(solution)/shard_map/ppermute | solution.py:592
  77.7 1.1 collective-permute-start.5
  78.8 0.0 copy-start
  78.8 1.2 copy-done
  80.1 0.0 copy-start.8
  80.1 0.7 copy-done.8
  80.7 0.0 copy-start.11
  80.7 1.0 copy-done.11
  81.8 0.0 copy-start.12
  81.8 1.0 copy-done.12
  82.8 0.0 copy-start.13
  82.8 0.9 copy-done.13
  83.7 3.4 %shard_map.108.refs_3_ = f32[8,64,512]{2,1,0:T(8,128)S(1)} custom-call(s32[8,128]{1,0:T(8,128)S(1)} %copy-done.8, bf16[8,512,128]{2,1,0:T(8,128)(2,1)S(1)} %bitcast.18, f32[8,8,512]{2,1,0:T(8,128)S(1)} %copy-done.13, bf16[1536,128]{1,0:T(8,128)(2,1)} %collective-permute-done.6.refs_0_, bf16[1536,128]{1,0:T(8,128)(2,1)} %collective-permute-done.7.refs_1_, ...), custom_call_target="tpu_custom_call" | custom-call | flops 6442450944 | bytes 3000000 | tf_op jit(solution)/shard_map/pallas_call | solution.py:91
  87.2 0.0 copy-start.1
  87.2 0.0 copy-start.14
  87.2 0.0 collective-permute-done.1.refs_0_
  87.2 0.0 collective-permute-done.2.refs_1_
  87.2 23.2 %collective-permute-done.3.refs_2_ = bf16[2560,128]{1,0:T(8,128)(2,1)} collective-permute-done((bf16[2560,128]{1,0:T(8,128)(2,1)}, bf16[2560,128]{1,0:T(8,128)(2,1)}, u32[]{:S(2)}, u32[]{:S(2)}) %collective-permute-start.3) | collective-permute-done | bytes 655392 | tf_op jit(solution)/shard_map/ppermute | solution.py:592
  110.4 0.0 copy-done.5
  110.4 0.0 copy-done.6
  110.4 0.0 copy-done.10
  110.4 3.4 %shard_map.103 = (bf16[8,512,128]{2,1,0:T(8,128)(2,1)S(1)}, bf16[384,128]{1,0:T(8,128)(2,1)S(1)}) custom-call(s32[3]{0:T(128)S(1)} %copy-done.6, s32[1,256]{1,0:T(1,128)S(1)} %copy-done.10, bf16[512,128]{1,0:T(8,128)(2,1)S(1)} %copy-done.5, bf16[512,128]{1,0:T(8,128)(2,1)} %collective-permute-done.refs_1_.across_own, ...), custom_call_target="tpu_custom_call" | custom-call | flops 1000000000 | bytes 2000000 | tf_op jit(solution)/shard_map/pallas_call | solution.py:91
  113.9 0.0 copy-start.9
  113.9 0.1 collective-permute-start.10
  114.0 0.3 collective-permute-start.8
  114.2 1.8 %collective-permute-start.9 = (bf16[384,128]{1,0:T(8,128)(2,1)S(1)}, bf16[384,128]{1,0:T(8,128)(2,1)S(1)}, u32[]{:S(2)}, u32[]{:S(2)}) collective-permute-start(bf16[384,128]{1,0:T(8,128)(2,1)S(1)} %get-tuple-element.28.refs_0_), channel_id=1, source_target_pairs={{0,16},{8,24},{16,0},{24,8},{1,17},{9,25},{17,1},{25,9},{2,18},{10... | collective-permute-start | bytes 294920 | tf_op jit(solution)/shard_map/ppermute | solution.py:592
  116.1 0.0 copy-done.1
  116.1 0.0 copy-done.14
  116.1 11.7 %shard_map.109.refs_2_ = f32[8,64,512]{2,1,0:T(8,128)S(1)} custom-call(s32[8,128]{1,0:T(8,128)S(1)} %copy-done.8, bf16[8,512,128]{2,1,0:T(8,128)(2,1)S(1)} %bitcast.19, f32[8,8,512]{2,1,0:T(8,128)S(1)} %copy-done.14, bf16[2560,128]{1,0:T(8,128)(2,1)} %collective-permute-done.1.refs_0_, ...), custom_call_target="tpu_custom_call", output_to_operand_aliasing={{}: (6, {})} | custom-call | flops 9663676416 | bytes 3000000 | tf_op jit(solution)/shard_map/pallas_call | solution.py:91
  127.8 0.0 copy-start.2
  127.8 0.0 copy-start.3
  127.9 0.0 copy-start.4
  127.9 0.0 copy-start.7
  127.9 0.0 collective-permute-done.4.refs_0_
  127.9 0.0 collective-permute-done.5.refs_1_
  127.9 0.0 copy-done.9
  127.9 13.4 %shard_map.110.acc = f32[8,64,512]{2,1,0:T(8,128)S(1)} custom-call(s32[8,128]{1,0:T(8,128)S(1)} %copy-done.9, bf16[8,512,128]{2,1,0:T(8,128)(2,1)S(1)} %bitcast.20, f32[8,8,512]{2,1,0:T(8,128)S(1)} %copy-done.14, bf16[1536,128]{1,0:T(8,128)(2,1)S(1)} %collective-permute-done.4.refs_0_, ...), custom_call_target="tpu_custom_call", output_to_operand_aliasing={{}: (5, {})} | custom-call | flops 6442450944 | bytes 3000000 | tf_op jit(solution)/shard_map/pallas_call | solution.py:91
  141.3 0.0 collective-permute-done.10.refs_3_
  141.3 0.0 collective-permute-done.8.refs_1_
  141.4 0.0 collective-permute-done.9.refs_2_
  141.4 0.0 copy-done.2
  141.4 0.0 copy-done.3
  141.4 0.0 copy-done.4
  141.4 0.0 copy-done.7
  141.4 4.6 %shard_map.111 = f32[64,4096]{1,0:T(8,128)} custom-call(s32[3]{0:T(128)S(1)} %copy-done.6, s32[1,4]{1,0:T(1,128)S(1)} %copy-done.7, bf16[8,512,128]{2,1,0:T(8,128)(2,1)S(1)} %get-tuple-element.21.mids, f32[8,64,512]{2,1,0:T(8,128)S(1)} %shard_map.110.acc, bf16[256,256]{1,0:T(8,128)(2,1)S(1)} %bitcast.24, bf16[2048,256]{1,0:T(8,128)(2,1)S(1)} %bitcast.22, ...), custom_call_target="tpu_custom_call" | custom-call | flops 1000000000 | bytes 6000000 | tf_op jit(solution)/shard_map/pallas_call | solution.py:91
  (3 shorter events, 0.0 us)
Async XLA Ops:
  2.3 30.2 %all-to-all-start = ((s32[8,1,8]{2,1,0:T(1,128)}), s32[8,1,8]{2,1,0:T(1,128)}, u32[]{:S(2)}, u32[]{:S(2)}) async-start(s32[8,1,8]{2,1,0:T(1,128)} %bitcast.31), calls=%async_computation | async-start | bytes 8192 | tf_op jit(solution)/shard_map/all_to_all | solution.py:626
  15.4 27.2 %collective-permute-start = (bf16[512,128]{1,0:T(8,128)(2,1)}, bf16[512,128]{1,0:T(8,128)(2,1)}, u32[]{:S(2)}, u32[]{:S(2)}) collective-permute-start(bf16[512,128]{1,0:T(8,128)(2,1)} %shard_map.100.refs_0_.own), channel_id=1, source_target_pairs={{0,4},{1,5},{2,6},{3,7},{4,0},{5,1},{6,2},{7,3},{8,12},{9,13},{10,... | collective-permute-start | bytes 393224 | tf_op jit(solution)/shard_map/ppermute | solution.py:592
  38.6 30.4 %collective-permute-start.7 = (bf16[1536,128]{1,0:T(8,128)(2,1)}, bf16[1536,128]{1,0:T(8,128)(2,1)}, u32[]{:S(2)}, u32[]{:S(2)}) collective-permute-start(bf16[1536,128]{1,0:T(8,128)(2,1)} %get-tuple-element.26), channel_id=1, source_target_pairs={{0,5},{1,4},{2,7},{3,6},{4,1},{5,0},{6,3},{7,2},{8,13},{9,12},{10,... | collective-permute-start | bytes 1179656 | tf_op jit(solution)/shard_map/ppermute | solution.py:592
  40.1 37.6 %collective-permute-start.6 = (bf16[1536,128]{1,0:T(8,128)(2,1)}, bf16[1536,128]{1,0:T(8,128)(2,1)}, u32[]{:S(2)}, u32[]{:S(2)}) collective-permute-start(bf16[1536,128]{1,0:T(8,128)(2,1)} %shard_map.106), channel_id=1, source_target_pairs={{0,4},{1,5},{2,6},{3,7},{4,0},{5,1},{6,2},{7,3},{8,12},{9,13},{10,... | collective-permute-start | bytes 1179656 | tf_op jit(solution)/shard_map/ppermute | solution.py:592
  46.5 40.7 %collective-permute-start.1 = (bf16[2560,128]{1,0:T(8,128)(2,1)}, bf16[2560,128]{1,0:T(8,128)(2,1)}, u32[]{:S(2)}, u32[]{:S(2)}) collective-permute-start(bf16[2560,128]{1,0:T(8,128)(2,1)} %get-tuple-element.18), channel_id=1, source_target_pairs={{0,1},{1,0},{2,3},{3,2},{4,5},{5,4},{6,7},{7,6},{8,9},{9,8},{10,11... | collective-permute-start | bytes 1966088 | tf_op jit(solution)/shard_map/ppermute | solution.py:592
  47.2 40.0 %collective-permute-start.2 = (bf16[2560,128]{1,0:T(8,128)(2,1)}, bf16[2560,128]{1,0:T(8,128)(2,1)}, u32[]{:S(2)}, u32[]{:S(2)}) collective-permute-start(bf16[2560,128]{1,0:T(8,128)(2,1)} %get-tuple-element.19), channel_id=1, source_target_pairs={{0,2},{1,3},{2,0},{3,1},{4,6},{5,7},{6,4},{7,5},{8,10},{9,11},{10,... | collective-permute-start | bytes 1966088 | tf_op jit(solution)/shard_map/ppermute | solution.py:592
  47.7 62.7 %collective-permute-start.3 = (bf16[2560,128]{1,0:T(8,128)(2,1)}, bf16[2560,128]{1,0:T(8,128)(2,1)}, u32[]{:S(2)}, u32[]{:S(2)}) collective-permute-start(bf16[2560,128]{1,0:T(8,128)(2,1)} %get-tuple-element.20), channel_id=1, source_target_pairs={{0,3},{1,2},{2,1},{3,0},{4,7},{5,6},{6,5},{7,4},{8,11},{9,10},{10,... | collective-permute-start | bytes 1966088 | tf_op jit(solution)/shard_map/ppermute | solution.py:592
  69.0 58.9 %collective-permute-start.4 = (bf16[1536,128]{1,0:T(8,128)(2,1)}, bf16[1536,128]{1,0:T(8,128)(2,1)S(1)}, u32[]{:S(2)}, u32[]{:S(2)}) collective-permute-start(bf16[1536,128]{1,0:T(8,128)(2,1)} %get-tuple-element.24), channel_id=1, source_target_pairs={{0,6},{1,7},{2,4},{3,5},{4,2},{5,3},{6,0},{7,1},{8,14},{9,15},{10,... | collective-permute-start | bytes 1179656 | tf_op jit(solution)/shard_map/ppermute | solution.py:592
  77.7 50.2 %collective-permute-start.5 = (bf16[1536,128]{1,0:T(8,128)(2,1)}, bf16[1536,128]{1,0:T(8,128)(2,1)S(1)}, u32[]{:S(2)}, u32[]{:S(2)}) collective-permute-start(bf16[1536,128]{1,0:T(8,128)(2,1)} %get-tuple-element.25), channel_id=1, source_target_pairs={{0,7},{1,6},{2,5},{3,4},{4,3},{5,2},{6,1},{7,0},{8,15},{9,14},{10,... | collective-permute-start | bytes 1179656 | tf_op jit(solution)/shard_map/ppermute | solution.py:592
  78.8 1.2 copy-start
  80.1 0.7 copy-start.8
  80.7 1.0 copy-start.11
  81.8 1.0 copy-start.12
  82.8 0.9 copy-start.13
  83.7 26.7 %copy-start.5 = (bf16[512,128]{1,0:T(8,128)(2,1)S(1)}, bf16[512,128]{1,0:T(8,128)(2,1)}, u32[]{:S(2)}) copy-start(bf16[512,128]{1,0:T(8,128)(2,1)} %shard_map.100.refs_0_.own) | copy-start | bytes 393220
  83.7 26.7 %copy-start.6 = (s32[3]{0:T(128)S(1)}, s32[3]{0:T(128)}, u32[]{:S(2)}) copy-start(s32[3]{0:T(128)} %pad_add_fusion.where) | copy-start | bytes 40
  83.7 26.7 %copy-start.10 = (s32[1,256]{1,0:T(1,128)S(1)}, s32[1,256]{1,0:T(1,128)}, u32[]{:S(2)}) copy-start(s32[1,256]{1,0:T(1,128)} %skel_top.1) | copy-start | bytes 3076
  87.2 28.9 %copy-start.1 = (bf16[4096,128]{1,0:T(8,128)(2,1)S(1)}, bf16[4096,128]{1,0:T(8,128)(2,1)}, u32[]{:S(2)}) copy-start(bf16[4096,128]{1,0:T(8,128)(2,1)} %param.10) | copy-start | bytes 3145732
  87.2 28.9 %copy-start.14 = (f32[8,8,512]{2,1,0:T(8,128)S(1)}, f32[8,8,512]{2,1,0:T(8,128)}, u32[]{:S(2)}) copy-start(f32[8,8,512]{2,1,0:T(8,128)} %get-tuple-element.23.refs_0_.tsq) | copy-start | bytes 393220
  113.9 14.0 %copy-start.9 = (s32[8,128]{1,0:T(8,128)S(1)}, s32[8,128]{1,0:T(8,128)}, u32[]{:S(2)}) copy-start(s32[8,128]{1,0:T(8,128)} %get-tuple-element.22.pool) | copy-start | bytes 12292
  113.9 27.5 %collective-permute-start.10 = (bf16[384,128]{1,0:T(8,128)(2,1)S(1)}, bf16[384,128]{1,0:T(8,128)(2,1)S(1)}, u32[]{:S(2)}, u32[]{:S(2)}) collective-permute-start(bf16[384,128]{1,0:T(8,128)(2,1)S(1)} %get-tuple-element.28.refs_0_), channel_id=1, source_target_pairs={{0,24},{8,16},{16,8},{24,0},{1,25},{9,17},{17,9},{25,1},{2,26},{10... | collective-permute-start | bytes 294920 | tf_op jit(solution)/shard_map/ppermute | solution.py:592
  114.0 27.4 %collective-permute-start.8 = (bf16[384,128]{1,0:T(8,128)(2,1)S(1)}, bf16[384,128]{1,0:T(8,128)(2,1)S(1)}, u32[]{:S(2)}, u32[]{:S(2)}) collective-permute-start(bf16[384,128]{1,0:T(8,128)(2,1)S(1)} %get-tuple-element.28.refs_0_), channel_id=1, source_target_pairs={{0,8},{8,0},{16,24},{24,16},{1,9},{9,1},{17,25},{25,17},{2,10},{10... | collective-permute-start | bytes 294920 | tf_op jit(solution)/shard_map/ppermute | solution.py:592
  114.2 27.1 %collective-permute-start.9 = (bf16[384,128]{1,0:T(8,128)(2,1)S(1)}, bf16[384,128]{1,0:T(8,128)(2,1)S(1)}, u32[]{:S(2)}, u32[]{:S(2)}) collective-permute-start(bf16[384,128]{1,0:T(8,128)(2,1)S(1)} %get-tuple-element.28.refs_0_), channel_id=1, source_target_pairs={{0,16},{8,24},{16,0},{24,8},{1,17},{9,25},{17,1},{25,9},{2,18},{10... | collective-permute-start | bytes 294920 | tf_op jit(solution)/shard_map/ppermute | solution.py:592
  127.8 13.5 %copy-start.2 = (bf16[8,512,256]{2,1,0:T(8,128)(2,1)S(1)}, bf16[8,512,256]{2,1,0:T(8,128)(2,1)}, u32[]{:S(2)}) copy-start(bf16[8,512,256]{2,1,0:T(8,128)(2,1)} %leaf_interp.1) | copy-start | bytes 6291460
  127.8 13.5 %copy-start.3 = (bf16[1,2048,256]{2,1,0:T(8,128)(2,1)S(1)}, bf16[1,2048,256]{2,1,0:T(8,128)(2,1)}, u32[]{:S(2)}) copy-start(bf16[1,2048,256]{2,1,0:T(8,128)(2,1)} %param.15) | copy-start | bytes 3145732
  127.9 13.5 %copy-start.4 = (bf16[1,256,256]{2,1,0:T(8,128)(2,1)S(1)}, bf16[1,256,256]{2,1,0:T(8,128)(2,1)}, u32[]{:S(2)}) copy-start(bf16[1,256,256]{2,1,0:T(8,128)(2,1)} %param.18) | copy-start | bytes 393220
  127.9 13.5 %copy-start.7 = (s32[1,4]{1,0:T(1,128)S(1)}, s32[1,4]{1,0:T(1,128)}, u32[]{:S(2)}) copy-start(s32[1,4]{1,0:T(1,128)} %partners.1) | copy-start | bytes 52

commit v5 on v4

--- a/solution.py
+++ b/solution.py
@@ -39,8 +39,9 @@
 
 
 def source_term(x):
-    ones = jnp.ones((2 * x.shape[1], LANES), bf16)
-    return dot(squares(x), ones) * (-kernel_rate * LOG2E)
+    xf = x.astype(f32)
+    total = jnp.sum(xf * xf, axis=1, keepdims=True) * (-kernel_rate * LOG2E)
+    return jnp.broadcast_to(total, (x.shape[0], LANES))
 
 
 def target_term(x):
@@ -160,7 +161,10 @@
 
 def pack_kernel(leaf_size, distances, count, where, handed, points, charges, *refs):
     blocks, refs = refs[:count], refs[count:]
-    outs, (x, q, mid, sem_x, sem_q, sem_m, sem_out) = refs[: len(distances)], refs[len(distances) :]
+    outs, refs = refs[: len(distances)], refs[len(distances) :]
+    if count:
+        pair, refs = refs[0], refs[1:]
+    x, q, mid, sem_x, sem_q, sem_m, sem_out = refs
     self_index = where[1]
     rhs = charges.shape[0]
     rows = leaf_size + leaf_size // LANES * rhs
@@ -178,8 +182,10 @@
                     copy_in(charges.at[:, lanes], q.at[put], sem_q.at[put]),
                 )
             )
-    for waited in mid_copies:
+    for at, waited in enumerate(mid_copies):
         waited.wait()
+        to = pair.at[at * mid.shape[1] : (at + 1) * mid.shape[1], :]
+        given.append(copy_in(mid.at[at], to, sem_m.at[at]))
     tiles = leaf_size // LANES
     for at, out in enumerate(outs):
         for slot in range(CAP):
@@ -198,15 +204,6 @@
                         q.at[put, :, lanes], out.at[row : row + rhs, :], sem_out.at[put, 1 + tile]
                     )
                 )
-        for block in range(count):
-            row = CAP * rows + block * mid.shape[1]
-            given.append(
-                copy_in(
-                    mid.at[block],
-                    out.at[row : row + mid.shape[1], :],
-                    sem_out.at[at * CAP, 1 + tiles + block],
-                )
-            )
     for one in given:
         one.wait()
 
@@ -216,12 +213,14 @@
     rhs = charges.shape[0]
     rows = CAP * (leaf_size + leaf_size // LANES * rhs)
     each = blocks[0].shape[0] if blocks else 16
-    rows += len(blocks) * each
+    shapes = [(rows, coords) for _ in distances]
+    if blocks:
+        shapes.append((len(blocks) * each, coords))
     places = len(distances) * CAP
     sem = pltpu.SemaphoreType.DMA
     return call(
         functools.partial(pack_kernel, leaf_size, distances, len(blocks)),
-        [jax.ShapeDtypeStruct((rows, coords), bf16) for _ in distances],
+        [jax.ShapeDtypeStruct(shape, bf16) for shape in shapes],
         [smem(), smem()] + [in_hbm()] * (2 + len(blocks)),
         cost(1e5, 2 * len(distances) * rows * coords * 2),
         (where, handed, points, charges) + blocks,
@@ -232,10 +231,10 @@
             sem((places,)),
             sem((places,)),
             sem((max(len(blocks), 1),)),
-            sem((places, 1 + leaf_size // LANES + len(blocks))),
+            sem((places, 1 + leaf_size // LANES)),
         ],
         own=None,
-        outs=[in_hbm()] * len(distances),
+        outs=[in_hbm()] * len(shapes),
     )
 
 
@@ -408,7 +407,9 @@
         near_cost(len(got) * leaf_dev, leaf_size, coords, rhs),
         (pool, points, tsq, *got, *inits),
         scratch=scratch,
-        own=(leaf_dev * rhs * 4 + places * (coords * 2 + LANES * 4 + rhs * 2)) * leaf_size
+        own=None
+        if stage == "first"
+        else (leaf_dev * rhs * 4 + places * (coords * 2 + LANES * 4 + rhs * 2)) * leaf_size
         + (2 << 20),
         alias={3 + len(got): 0} if stage == "middle" else None,
     )
@@ -436,6 +437,19 @@
     index = (found[:leaf_dev] * 16.0 + found[leaf_dev:]).astype(i32)
     row = lax.broadcasted_iota(i32, (leaf_dev, skel), 0)
     return jnp.sum(jnp.where(row == leaf, index + row * leaf_size, 0), axis=0, keepdims=True)
+
+
+def as_column(row):
+    return jnp.broadcast_to(row.astype(f32), (LANES, row.shape[1])).T.astype(i32)
+
+
+def pick_rows(index, base, block):
+    lane = lax.broadcasted_iota(i32, index.shape, 1)
+    tiles = [
+        (index == lane + (base + at)).astype(f32).astype(bf16)
+        for at in range(0, block.shape[0], LANES)
+    ]
+    return dot(jnp.concatenate(tiles, axis=1), block)
 
 
 def up_kernel(*refs):
@@ -452,14 +466,11 @@
         m_copies.append(copy_in(interp_mid.at[rows], mid_w.at[rows], sem_m.at[m]))
     t_copy = copy_in(interp_top, top_w, sem_t)
 
-    rows = skeleton_rows(skel_leaf[...], skel_mid[...], leaf_size)
-    at = lax.broadcasted_iota(i32, (leaf_size, skel), 0)
-    columns = (((0,), (0,)), ((), ()))
+    rows = as_column(skeleton_rows(skel_leaf[...], skel_mid[...], leaf_size))
     picked = jnp.zeros((skel, x.shape[2]), f32)
     for m in leaves:
-        one_hot = (at == rows - m * leaf_size).astype(f32).astype(bf16)
         x_copies[m].wait()
-        picked = picked + lax.dot_general(one_hot, x[m], columns, preferred_element_type=f32)
+        picked = picked + pick_rows(rows, m * leaf_size, x[m])
     out[:skel, :] = picked.astype(bf16)
     total = jnp.zeros((q.shape[0], skel), f32)
     q_copy.wait()
@@ -498,49 +509,42 @@
     return lax.rem(distance, half) * 2 + lax.div(distance, half)
 
 
-def top_kernel(near_rows, where, skel_top, own, across_own, *refs):
-    inner = len(refs) - 3
-    got, (mids, out, sem) = refs[:inner], refs[inner:]
+def top_kernel(where, skel_top, *refs):
+    pairs, (mids, out, sem) = refs[:-3], refs[-3:]
     size, rows, _ = mids.shape
     skel = skel_top.shape[1]
-    copies = [copy_in(own, mids.at[0], sem.at[0]), copy_in(across_own, mids.at[1], sem.at[1])]
-    for at, message in enumerate(got, 1):
-        for side in range(2):
-            row = near_rows + side * rows
-            to = at * 2 + side
-            copies.append(copy_in(message.at[row : row + rows, :], mids.at[to], sem.at[to]))
+    copies = []
+    for to in range(size):
+        row = to % 2 * rows
+        source = pairs[to // 2].at[row : row + rows, :]
+        copies.append(copy_in(source, mids.at[to], sem.at[to]))
     picked = skel_top[...]
     distance = jnp.bitwise_xor(lax.div(picked, skel), where[1])
-    index = place(distance, size) * skel + lax.rem(picked, skel)
-    at = lax.broadcasted_iota(i32, (skel, skel), 0)
-    columns = (((0,), (0,)), ((), ()))
+    index = as_column(place(distance, size) * skel + lax.rem(picked, skel))
     points = jnp.zeros((skel, mids.shape[2]), f32)
     first = skel + (rows - skel) // 2
     weight = jnp.zeros((rows - first, mids.shape[2]), f32)
     for p in range(size):
-        one_hot = (at == index - p * skel).astype(f32).astype(bf16)
         copies[p].wait()
-        points = points + lax.dot_general(
-            one_hot, mids[p, :skel, :], columns, preferred_element_type=f32
-        )
+        points = points + pick_rows(index, p * skel, mids[p, :skel, :])
         weight = weight + mids[p, first:, :].astype(f32)
     out[:skel, :] = points.astype(bf16)
     out[skel:, :] = weight.astype(bf16)
 
 
-def top_prepare(near_rows, where, skel_top, own, across_own, got):
-    rows, coords = own.shape
+def top_prepare(where, skel_top, pairs):
+    rows, coords = pairs[0].shape[0] // 2, pairs[0].shape[1]
     skel = skel_top.shape[1]
-    size = 2 + 2 * len(got)
+    size = 2 * len(pairs)
     return call(
-        functools.partial(top_kernel, near_rows),
+        top_kernel,
         [
             jax.ShapeDtypeStruct((size, rows, coords), bf16),
             jax.ShapeDtypeStruct((skel + (rows - skel) // 2, coords), bf16),
         ],
-        [smem(), vmem()] + [in_hbm()] * (2 + len(got)),
+        [smem(), vmem()] + [in_hbm()] * len(pairs),
         cost(1e9, 2e6),
-        (where, skel_top, own, across_own, *got),
+        (where, skel_top, *pairs),
         scratch=[pltpu.SemaphoreType.DMA((size,))],
         own=2 << 20,
     )
@@ -615,7 +619,6 @@
     self_index = lax.axis_index("sub")
     leaf_dev, leaf_size, _ = leaf_interpolant.shape
     coords = points.shape[1]
-    rhs = charges.shape[1]
     near_count = near_leaves.shape[1]
     group_first = lax.axis_index("leaf") * group
     blocks = points.reshape(leaf_dev, leaf_size, coords)
@@ -637,21 +640,20 @@
         asked = pack(where, handed, blocks, charges_t, distances, *carried)
         for distance, one in zip(distances, asked):
             got[distance] = swapped(one, "sub", group, distance)
+    pair = asked[-1]
+    pairs = [pair] + [swapped(pair, "sub", group, d) for d in inner]
 
     half = leaf_dev // 2
     sum0, tsq = near_local(pool, near_count, blocks, charges_t, (0, half))
     sum1 = near_local(pool, near_count, blocks, charges_t, (half, leaf_dev), tsq)
     sums = [sum0, sum1]
 
-    near_rows = CAP * (leaf_size + leaf_size // LANES * rhs)
-    mids, top_own = top_prepare(
-        near_rows, where, skel_top, message, across_message, [got[d] for d in inner]
-    )
+    mids, top_own = top_prepare(where, skel_top, pairs)
     tops = [top_own]
     for distance in range(1, groups):
         tops.append(swapped(top_own, "leaf", groups, distance))
 
-    for at, span in enumerate((first + second, inner, third + last)):
+    for at, span in enumerate((first + second, third, inner, last)):
         stage = "first" if at == 0 else "middle"
         part = [got[distance] for distance in span]
         sums = [near_remote(pool, near_count, blocks, tsq, span[0], part, sums, stage)]

time: 147 us -> 161 us (1.095)
  the two profiles are of different devices: /device:TPU:2 before, /device:TPU:9 now
where the time goes in v5:
time: 161 us; the launch traced here: 160 us
  Pallas kernels  81.7 us (51%)
  starting transfers between devices  40.5 us (25%)
  waiting for transfers between devices  24.2 us (15%)
  local copies, waits for them, and re-layouts  12.4 us (8%)
    pallas_call x13, Pallas kernels, call(): pl.pallas_call(kernel, out_shape=out_shape, in_specs=in_specs, out_specs=...  81.7 us
    ppermute x14, starting transfers between devices, swapped(): return lax.ppermute(value, axis, [(i, i ^ distance) for i in range(size)])  34.8 us
    ppermute x14, waiting for transfers between devices, swapped(): return lax.ppermute(value, axis, [(i, i ^ distance) for i in range(size)])  24.2 us
    unnamed x46, local copies, waits for them, and re-layouts  12.4 us
    all_to_all x1, starting transfers between devices, body(): lax.all_to_all(chosen, 'sub', split_axis=0, concat_axis=0, tiled=True)  5.72 us
  transfers between devices with their start and end apart: 15, of which 4 were waited for; matrix products, arithmetic and copies ran while one was open for 0% of the time, Pallas kernels for 47%

profile of v5, /device:TPU:9, one launch (start us, length us, event | category | flops | bytes accessed | tf_op | source)
XLA Modules:
  0.0 159.7 jit_solution(9861682480809865879)
XLA Ops:
  0.0 0.7 pad_add_fusion.where
  0.7 1.7 %shard_map.100 = (s32[8,8]{1,0:T(8,128)}, s32[8,128]{1,0:T(8,128)}) custom-call(s32[3]{0:T(128)} %pad_add_fusion.where, s32[8,12]{1,0:T(8,128)} %near.1), custom_call_target="tpu_custom_call" | custom-call | flops 1000000 | bytes 100000 | tf_op jit(solution)/shard_map/pallas_call | solution.py:92
  2.3 5.7 %all-to-all-start = ((s32[8,1,8]{2,1,0:T(1,128)}), s32[8,1,8]{2,1,0:T(1,128)}, u32[]{:S(2)}, u32[]{:S(2)}) async-start(s32[8,1,8]{2,1,0:T(1,128)} %bitcast.32), calls=%async_computation | async-start | bytes 8192 | tf_op jit(solution)/shard_map/all_to_all | solution.py:629
  8.0 6.6 %shard_map.101.refs_0_ = bf16[512,128]{1,0:T(8,128)(2,1)} custom-call(bf16[8,512,128]{2,1,0:T(8,128)(2,1)} %bitcast.12, bf16[64,4096]{1,0:T(8,128)(2,1)} %bitcast.26, bf16[8,512,256]{2,1,0:T(8,128)(2,1)} %leaf_interp.1, bf16[2048,256]{1,0:T(8,128)(2,1)} %bitcast.22, bf16[256,256]{1,0:T(8,128)(2,1)} %bitcast.24, s32[8,256]{1,0:T(8,128)} %refs_5_.1, ...), custom_call_target="tpu_custom_call" | custom-call | flops 3000000000 | bytes 5000000 | tf_op jit(solution)/shard_map/pallas_call | solution.py:92
  14.6 2.1 %collective-permute-start = (bf16[512,128]{1,0:T(8,128)(2,1)}, bf16[512,128]{1,0:T(8,128)(2,1)}, u32[]{:S(2)}, u32[]{:S(2)}) collective-permute-start(bf16[512,128]{1,0:T(8,128)(2,1)} %shard_map.101.refs_0_), channel_id=1, source_target_pairs={{0,4},{1,5},{2,6},{3,7},{4,0},{5,1},{6,2},{7,3},{8,12},{9,13},{10,... | collective-permute-start | bytes 393224 | tf_op jit(solution)/shard_map/ppermute | solution.py:596
  16.8 12.8 %shard_map.104 = (f32[4,64,512]{2,1,0:T(8,128)}, f32[8,8,512]{2,1,0:T(8,128)}) custom-call(s32[8,128]{1,0:T(8,128)} %get-tuple-element.21.pool, bf16[8,512,128]{2,1,0:T(8,128)(2,1)} %bitcast.13, bf16[64,4096]{1,0:T(8,128)(2,1)} %bitcast.27), custom_call_target="tpu_custom_call" | custom-call | flops 9663676416 | bytes 3000000 | tf_op jit(solution)/shard_map/pallas_call | solution.py:92
  29.5 0.0 all-to-all-done
  29.6 3.6 %shard_map.105 = (bf16[1536,128]{1,0:T(8,128)(2,1)}, bf16[1536,128]{1,0:T(8,128)(2,1)}, bf16[1536,128]{1,0:T(8,128)(2,1)}) custom-call(s32[3]{0:T(128)} %pad_add_fusion.where, s32[8,8]{1,0:T(8,128)} %bitcast.5.handed, bf16[8,512,128]{2,1,0:T(8,128)(2,1)} %bitcast.14, bf16[64,4096]{1,0:T(8,128)(2,1)} %bitcast.28), custom_call_target="tpu_custom_call" | custom-call | flops 100000 | bytes 2359296 | tf_op jit(solution)/shard_map/pallas_call | solution.py:92
  33.1 2.6 %shard_map.106 = bf16[1536,128]{1,0:T(8,128)(2,1)} custom-call(s32[3]{0:T(128)} %pad_add_fusion.where, s32[8,8]{1,0:T(8,128)} %bitcast.5.handed, bf16[8,512,128]{2,1,0:T(8,128)(2,1)} %bitcast.15, bf16[64,4096]{1,0:T(8,128)(2,1)} %bitcast.29), custom_call_target="tpu_custom_call" | custom-call | flops 100000 | bytes 786432 | tf_op jit(solution)/shard_map/pallas_call | solution.py:92
  35.7 2.1 %collective-permute-start.10 = (bf16[1536,128]{1,0:T(8,128)(2,1)}, bf16[1536,128]{1,0:T(8,128)(2,1)}, u32[]{:S(2)}, u32[]{:S(2)}) collective-permute-start(bf16[1536,128]{1,0:T(8,128)(2,1)} %get-tuple-element.28), channel_id=1, source_target_pairs={{0,5},{1,4},{2,7},{3,6},{4,1},{5,0},{6,3},{7,2},{8,13},{9,12},{10,... | collective-permute-start | bytes 1179656 | tf_op jit(solution)/shard_map/ppermute | solution.py:596
  37.8 2.0 %collective-permute-start.9 = (bf16[1536,128]{1,0:T(8,128)(2,1)}, bf16[1536,128]{1,0:T(8,128)(2,1)}, u32[]{:S(2)}, u32[]{:S(2)}) collective-permute-start(bf16[1536,128]{1,0:T(8,128)(2,1)} %shard_map.106), channel_id=1, source_target_pairs={{0,4},{1,5},{2,6},{3,7},{4,0},{5,1},{6,2},{7,3},{8,12},{9,13},{10,... | collective-permute-start | bytes 1179656 | tf_op jit(solution)/shard_map/ppermute | solution.py:596
  39.7 0.0 collective-permute-done.refs_1_
  39.7 3.7 %shard_map.102 = (bf16[1536,128]{1,0:T(8,128)(2,1)}, bf16[1536,128]{1,0:T(8,128)(2,1)}, bf16[1536,128]{1,0:T(8,128)(2,1)}, bf16[1024,128]{1,0:T(8,128)(2,1)}) custom-call(s32[3]{0:T(128)} %pad_add_fusion.where, s32[8,8]{1,0:T(8,128)} %bitcast.5.handed, bf16[8,512,128]{2,1,0:T(8,128)(2,1)} %bitcast.16, bf16[64,4096]{1,0:T(8,128)(2,1)} %bitcast.30, ...), custom_call_target="tpu_custom_call" | custom-call | flops 100000 | bytes 2359296 | tf_op jit(solution)/shard_map/pallas_call | solution.py:92
  43.4 0.1 collective-permute-start.1
  43.5 0.1 collective-permute-start.2
  43.5 2.6 %collective-permute-start.3 = (bf16[1024,128]{1,0:T(8,128)(2,1)}, bf16[1024,128]{1,0:T(8,128)(2,1)}, u32[]{:S(2)}, u32[]{:S(2)}) collective-permute-start(bf16[1024,128]{1,0:T(8,128)(2,1)} %get-tuple-element.19.refs_0_), channel_id=1, source_target_pairs={{0,3},{1,2},{2,1},{3,0},{4,7},{5,6},{6,5},{7,4},{8,11},{9,10},{10,... | collective-permute-start | bytes 786440 | tf_op jit(solution)/shard_map/ppermute | solution.py:596
  46.1 12.4 %shard_map.107.refs_3_ = f32[4,64,512]{2,1,0:T(8,128)} custom-call(s32[8,128]{1,0:T(8,128)} %get-tuple-element.21.pool, bf16[8,512,128]{2,1,0:T(8,128)(2,1)} %bitcast.17, bf16[64,4096]{1,0:T(8,128)(2,1)} %bitcast.31, f32[8,8,512]{2,1,0:T(8,128)} %get-tuple-element.22.refs_0_.tsq), custom_call_target="tpu_custom_call" | custom-call | flops 9663676416 | bytes 3000000 | tf_op jit(solution)/shard_map/pallas_call | solution.py:92
  58.5 0.0 collective-permute-done.1.refs_1_
  58.5 0.6 collective-permute-start.8
  59.1 0.9 collective-permute-done.2.refs_2_
  60.0 0.8 collective-permute-start.4
  60.8 6.7 %collective-permute-done.3.refs_3_ = bf16[1024,128]{1,0:T(8,128)(2,1)} collective-permute-done((bf16[1024,128]{1,0:T(8,128)(2,1)}, bf16[1024,128]{1,0:T(8,128)(2,1)}, u32[]{:S(2)}, u32[]{:S(2)}) %collective-permute-start.3) | collective-permute-done | bytes 262176 | tf_op jit(solution)/shard_map/ppermute | solution.py:596
  67.5 0.0 collective-permute-start.5
  67.5 0.7 copy-done.14
  68.2 0.9 copy-done.17
  69.2 0.7 copy-done.20
  69.8 3.1 %shard_map.103 = (bf16[8,512,128]{2,1,0:T(8,128)(2,1)S(1)}, bf16[384,128]{1,0:T(8,128)(2,1)S(1)}) custom-call(s32[3]{0:T(128)S(1)} %copy-done.14, s32[1,256]{1,0:T(1,128)S(1)} %copy-done.20, bf16[1024,128]{1,0:T(8,128)(2,1)S(1)} %copy-done.17, bf16[1024,128]{1,0:T(8,128)(2,1)} %collective-permute-done.1.refs_1_, ...), custom_call_target="tpu_custom_call" | custom-call | flops 1000000000 | bytes 2000000 | tf_op jit(solution)/shard_map/pallas_call | solution.py:92
  72.9 0.0 copy-start.4
  72.9 1.0 copy-done.4
  73.9 0.6 copy-done.12
  74.5 0.0 collective-permute-done.10.refs_1_
  74.5 0.0 collective-permute-start.6
  74.5 14.3 %collective-permute-done.9.refs_0_ = bf16[1536,128]{1,0:T(8,128)(2,1)} collective-permute-done((bf16[1536,128]{1,0:T(8,128)(2,1)}, bf16[1536,128]{1,0:T(8,128)(2,1)}, u32[]{:S(2)}, u32[]{:S(2)}) %collective-permute-start.9) | collective-permute-done | bytes 393248 | tf_op jit(solution)/shard_map/ppermute | solution.py:596
  88.9 2.2 %collective-permute-start.7 = (bf16[1536,128]{1,0:T(8,128)(2,1)}, bf16[1536,128]{1,0:T(8,128)(2,1)}, u32[]{:S(2)}, u32[]{:S(2)}) collective-permute-start(bf16[1536,128]{1,0:T(8,128)(2,1)} %get-tuple-element.26), channel_id=1, source_target_pairs={{0,3},{1,2},{2,1},{3,0},{4,7},{5,6},{6,5},{7,4},{8,11},{9,10},{10,... | collective-permute-start | bytes 1179656 | tf_op jit(solution)/shard_map/ppermute | solution.py:596
  91.0 4.0 %shard_map.108.refs_1_ = f32[8,64,512]{2,1,0:T(8,128)} custom-call(s32[8,128]{1,0:T(8,128)} %get-tuple-element.21.pool, bf16[8,512,128]{2,1,0:T(8,128)(2,1)} %bitcast.18, f32[8,8,512]{2,1,0:T(8,128)} %get-tuple-element.22.refs_0_.tsq, bf16[1536,128]{1,0:T(8,128)(2,1)} %collective-permute-done.9.refs_0_, bf16[1536,128]{1,0:T(8,128)(2,1)} %collective-permute-done.10.refs_1_, ...), custom_call_target="tpu_custom_call" | custom-call | flops 6442450944 | bytes 3000000 | tf_op jit(solution)/shard_map/pallas_call | solution.py:92
  95.0 2.3 %collective-permute-done.8.refs_0_ = bf16[1536,128]{1,0:T(8,128)(2,1)} collective-permute-done((bf16[1536,128]{1,0:T(8,128)(2,1)}, bf16[1536,128]{1,0:T(8,128)(2,1)}, u32[]{:S(2)}, u32[]{:S(2)}) %collective-permute-start.8) | collective-permute-done | bytes 393248 | tf_op jit(solution)/shard_map/ppermute | solution.py:596
  97.3 16.3 %collective-permute-start.11 = (bf16[384,128]{1,0:T(8,128)(2,1)}, bf16[384,128]{1,0:T(8,128)(2,1)S(1)}, u32[]{:S(2)}, u32[]{:S(2)}) collective-permute-start(bf16[384,128]{1,0:T(8,128)(2,1)} %copy-done.12), channel_id=1, source_target_pairs={{0,8},{8,0},{16,24},{24,16},{1,9},{9,1},{17,25},{25,17},{2,10},{10... | collective-permute-start | bytes 294920 | tf_op jit(solution)/shard_map/ppermute | solution.py:596
  113.6 1.2 copy-done
  114.9 1.2 copy-done.6
  116.1 0.7 copy-done.18
  116.8 0.9 copy-done.21
  117.7 2.5 %shard_map.109.refs_3_ = f32[8,64,512]{2,1,0:T(8,128)S(1)} custom-call(s32[8,128]{1,0:T(8,128)S(1)} %copy-done.18, bf16[8,512,128]{2,1,0:T(8,128)(2,1)S(1)} %bitcast.19, f32[8,8,512]{2,1,0:T(8,128)S(1)} %copy-done.21, bf16[1536,128]{1,0:T(8,128)(2,1)} %collective-permute-done.8.refs_0_, f32[8,64,512]{2,1,0:T(8,128)S(1)} %copy-done.6), custom_call_target="tpu_custom_call", output_to_operand_aliasing={{}: (4, {})} | custom-call | flops 3221225472 | bytes 3000000 | tf_op jit(solution)/shard_map/pallas_call | solution.py:92
  120.2 1.0 copy-done.7
  121.2 0.0 collective-permute-done.5.refs_0_
  121.2 2.2 %collective-permute-start.12 = (bf16[384,128]{1,0:T(8,128)(2,1)S(1)}, bf16[384,128]{1,0:T(8,128)(2,1)S(1)}, u32[]{:S(2)}, u32[]{:S(2)}) collective-permute-start(bf16[384,128]{1,0:T(8,128)(2,1)S(1)} %copy-done.13), channel_id=1, source_target_pairs={{0,16},{8,24},{16,0},{24,8},{1,17},{9,25},{17,1},{25,9},{2,18},{10... | collective-permute-start | bytes 294920 | tf_op jit(solution)/shard_map/ppermute | solution.py:596
  123.4 0.0 collective-permute-done.6.refs_1_
  123.4 3.8 %collective-permute-start.13 = (bf16[384,128]{1,0:T(8,128)(2,1)S(1)}, bf16[384,128]{1,0:T(8,128)(2,1)S(1)}, u32[]{:S(2)}, u32[]{:S(2)}) collective-permute-start(bf16[384,128]{1,0:T(8,128)(2,1)S(1)} %copy-done.13), channel_id=1, source_target_pairs={{0,24},{8,16},{16,8},{24,0},{1,25},{9,17},{17,9},{25,1},{2,26},{10... | collective-permute-start | bytes 294920 | tf_op jit(solution)/shard_map/ppermute | solution.py:596
  127.2 0.0 collective-permute-done.7.refs_2_
  127.2 0.0 copy-done.19
  127.2 1.2 copy-done.8
  128.5 17.2 %shard_map.110.refs_1_ = f32[8,64,512]{2,1,0:T(8,128)S(1)} custom-call(s32[8,128]{1,0:T(8,128)S(1)} %copy-done.19, bf16[8,512,128]{2,1,0:T(8,128)(2,1)S(1)} %bitcast.20, f32[8,8,512]{2,1,0:T(8,128)S(1)} %copy-done.22, bf16[1536,128]{1,0:T(8,128)(2,1)} %collective-permute-done.5.refs_0_, ...), custom_call_target="tpu_custom_call", output_to_operand_aliasing={{}: (6, {})} | custom-call | flops 9663676416 | bytes 3000000 | tf_op jit(solution)/shard_map/pallas_call | solution.py:92
  145.7 0.0 copy-start.2
  145.7 0.0 copy-start.3
  145.7 0.0 copy-start.5
  145.7 0.0 copy-start.11
  145.7 0.0 copy-start.16
  145.7 0.0 collective-permute-done.4.refs_0_
  145.8 7.5 %shard_map.111.acc = f32[8,64,512]{2,1,0:T(8,128)S(1)} custom-call(s32[8,128]{1,0:T(8,128)S(1)} %copy-done.19, bf16[8,512,128]{2,1,0:T(8,128)(2,1)S(1)} %bitcast.21, f32[8,8,512]{2,1,0:T(8,128)S(1)} %copy-done.22, bf16[1536,128]{1,0:T(8,128)(2,1)} %collective-permute-done.4.refs_0_, f32[8,64,512]{2,1,0:T(8,128)S(1)} %shard_map.110.refs_1_), custom_call_target="tpu_custom_call", output_to_operand_aliasing={{}: (4, {})} | custom-call | flops 3221225472 | bytes 3000000 | tf_op jit(solution)/shard_map/pallas_call | solution.py:92
  153.3 1.0 copy-done.9
  154.2 0.0 collective-permute-done.11.refs_1_
  154.2 0.0 collective-permute-done.12.refs_2_
  154.2 0.0 collective-permute-done.13.refs_3_
  154.3 1.2 copy-done.10
  155.5 4.2 %shard_map.112 = f32[64,4096]{1,0:T(8,128)} custom-call(s32[3]{0:T(128)S(1)} %copy-done.15, s32[1,4]{1,0:T(1,128)S(1)} %copy-done.16, bf16[8,512,128]{2,1,0:T(8,128)(2,1)S(1)} %copy-done.5, f32[8,64,512]{2,1,0:T(8,128)S(1)} %copy-done.10, bf16[256,256]{1,0:T(8,128)(2,1)S(1)} %bitcast.25, bf16[2048,256]{1,0:T(8,128)(2,1)S(1)} %bitcast.23, ...), custom_call_target="tpu_custom_call" | custom-call | flops 1000000000 | bytes 6000000 | tf_op jit(solution)/shard_map/pallas_call | solution.py:92
  (26 shorter events, 0.0 us)
Async XLA Ops:
  2.3 27.2 %all-to-all-start = ((s32[8,1,8]{2,1,0:T(1,128)}), s32[8,1,8]{2,1,0:T(1,128)}, u32[]{:S(2)}, u32[]{:S(2)}) async-start(s32[8,1,8]{2,1,0:T(1,128)} %bitcast.32), calls=%async_computation | async-start | bytes 8192 | tf_op jit(solution)/shard_map/all_to_all | solution.py:629
  14.6 25.1 %collective-permute-start = (bf16[512,128]{1,0:T(8,128)(2,1)}, bf16[512,128]{1,0:T(8,128)(2,1)}, u32[]{:S(2)}, u32[]{:S(2)}) collective-permute-start(bf16[512,128]{1,0:T(8,128)(2,1)} %shard_map.101.refs_0_), channel_id=1, source_target_pairs={{0,4},{1,5},{2,6},{3,7},{4,0},{5,1},{6,2},{7,3},{8,12},{9,13},{10,... | collective-permute-start | bytes 393224 | tf_op jit(solution)/shard_map/ppermute | solution.py:596
  35.7 38.9 %collective-permute-start.10 = (bf16[1536,128]{1,0:T(8,128)(2,1)}, bf16[1536,128]{1,0:T(8,128)(2,1)}, u32[]{:S(2)}, u32[]{:S(2)}) collective-permute-start(bf16[1536,128]{1,0:T(8,128)(2,1)} %get-tuple-element.28), channel_id=1, source_target_pairs={{0,5},{1,4},{2,7},{3,6},{4,1},{5,0},{6,3},{7,2},{8,13},{9,12},{10,... | collective-permute-start | bytes 1179656 | tf_op jit(solution)/shard_map/ppermute | solution.py:596
  37.8 51.1 %collective-permute-start.9 = (bf16[1536,128]{1,0:T(8,128)(2,1)}, bf16[1536,128]{1,0:T(8,128)(2,1)}, u32[]{:S(2)}, u32[]{:S(2)}) collective-permute-start(bf16[1536,128]{1,0:T(8,128)(2,1)} %shard_map.106), channel_id=1, source_target_pairs={{0,4},{1,5},{2,6},{3,7},{4,0},{5,1},{6,2},{7,3},{8,12},{9,13},{10,... | collective-permute-start | bytes 1179656 | tf_op jit(solution)/shard_map/ppermute | solution.py:596
  43.4 15.2 %collective-permute-start.1 = (bf16[1024,128]{1,0:T(8,128)(2,1)}, bf16[1024,128]{1,0:T(8,128)(2,1)}, u32[]{:S(2)}, u32[]{:S(2)}) collective-permute-start(bf16[1024,128]{1,0:T(8,128)(2,1)} %get-tuple-element.19.refs_0_), channel_id=1, source_target_pairs={{0,1},{1,0},{2,3},{3,2},{4,5},{5,4},{6,7},{7,6},{8,9},{9,8},{10,11... | collective-permute-start | bytes 786440 | tf_op jit(solution)/shard_map/ppermute | solution.py:596
  43.5 16.6 %collective-permute-start.2 = (bf16[1024,128]{1,0:T(8,128)(2,1)}, bf16[1024,128]{1,0:T(8,128)(2,1)}, u32[]{:S(2)}, u32[]{:S(2)}) collective-permute-start(bf16[1024,128]{1,0:T(8,128)(2,1)} %get-tuple-element.19.refs_0_), channel_id=1, source_target_pairs={{0,2},{1,3},{2,0},{3,1},{4,6},{5,7},{6,4},{7,5},{8,10},{9,11},{10,... | collective-permute-start | bytes 786440 | tf_op jit(solution)/shard_map/ppermute | solution.py:596
  43.5 24.0 %collective-permute-start.3 = (bf16[1024,128]{1,0:T(8,128)(2,1)}, bf16[1024,128]{1,0:T(8,128)(2,1)}, u32[]{:S(2)}, u32[]{:S(2)}) collective-permute-start(bf16[1024,128]{1,0:T(8,128)(2,1)} %get-tuple-element.19.refs_0_), channel_id=1, source_target_pairs={{0,3},{1,2},{2,1},{3,0},{4,7},{5,6},{6,5},{7,4},{8,11},{9,10},{10,... | collective-permute-start | bytes 786440 | tf_op jit(solution)/shard_map/ppermute | solution.py:596
  58.5 38.7 %collective-permute-start.8 = (bf16[1536,128]{1,0:T(8,128)(2,1)}, bf16[1536,128]{1,0:T(8,128)(2,1)}, u32[]{:S(2)}, u32[]{:S(2)}) collective-permute-start(bf16[1536,128]{1,0:T(8,128)(2,1)} %get-tuple-element.27), channel_id=1, source_target_pairs={{0,6},{1,7},{2,4},{3,5},{4,2},{5,3},{6,0},{7,1},{8,14},{9,15},{10,... | collective-permute-start | bytes 1179656 | tf_op jit(solution)/shard_map/ppermute | solution.py:596
  60.0 85.7 %collective-permute-start.4 = (bf16[1536,128]{1,0:T(8,128)(2,1)}, bf16[1536,128]{1,0:T(8,128)(2,1)}, u32[]{:S(2)}, u32[]{:S(2)}) collective-permute-start(bf16[1536,128]{1,0:T(8,128)(2,1)} %get-tuple-element.23), channel_id=1, source_target_pairs={{0,7},{1,6},{2,5},{3,4},{4,3},{5,2},{6,1},{7,0},{8,15},{9,14},{10,... | collective-permute-start | bytes 1179656 | tf_op jit(solution)/shard_map/ppermute | solution.py:596
  67.5 53.6 %collective-permute-start.5 = (bf16[1536,128]{1,0:T(8,128)(2,1)}, bf16[1536,128]{1,0:T(8,128)(2,1)}, u32[]{:S(2)}, u32[]{:S(2)}) collective-permute-start(bf16[1536,128]{1,0:T(8,128)(2,1)} %get-tuple-element.24), channel_id=1, source_target_pairs={{0,1},{1,0},{2,3},{3,2},{4,5},{5,4},{6,7},{7,6},{8,9},{9,8},{10,11... | collective-permute-start | bytes 1179656 | tf_op jit(solution)/shard_map/ppermute | solution.py:596
  67.5 0.7 copy-start.14
  68.2 0.9 copy-start.17
  69.2 0.7 copy-start.20
  72.9 1.0 copy-start.4
  73.9 0.6 copy-start.12
  74.5 48.8 %collective-permute-start.6 = (bf16[1536,128]{1,0:T(8,128)(2,1)}, bf16[1536,128]{1,0:T(8,128)(2,1)}, u32[]{:S(2)}, u32[]{:S(2)}) collective-permute-start(bf16[1536,128]{1,0:T(8,128)(2,1)} %get-tuple-element.25), channel_id=1, source_target_pairs={{0,2},{1,3},{2,0},{3,1},{4,6},{5,7},{6,4},{7,5},{8,10},{9,11},{10,... | collective-permute-start | bytes 1179656 | tf_op jit(solution)/shard_map/ppermute | solution.py:596
  88.9 38.3 %collective-permute-start.7 = (bf16[1536,128]{1,0:T(8,128)(2,1)}, bf16[1536,128]{1,0:T(8,128)(2,1)}, u32[]{:S(2)}, u32[]{:S(2)}) collective-permute-start(bf16[1536,128]{1,0:T(8,128)(2,1)} %get-tuple-element.26), channel_id=1, source_target_pairs={{0,3},{1,2},{2,1},{3,0},{4,7},{5,6},{6,5},{7,4},{8,11},{9,10},{10,... | collective-permute-start | bytes 1179656 | tf_op jit(solution)/shard_map/ppermute | solution.py:596
  97.3 56.9 %collective-permute-start.11 = (bf16[384,128]{1,0:T(8,128)(2,1)}, bf16[384,128]{1,0:T(8,128)(2,1)S(1)}, u32[]{:S(2)}, u32[]{:S(2)}) collective-permute-start(bf16[384,128]{1,0:T(8,128)(2,1)} %copy-done.12), channel_id=1, source_target_pairs={{0,8},{8,0},{16,24},{24,16},{1,9},{9,1},{17,25},{25,17},{2,10},{10... | collective-permute-start | bytes 294920 | tf_op jit(solution)/shard_map/ppermute | solution.py:596
  113.6 1.2 copy-start
  114.9 1.2 copy-start.6
  116.1 0.7 copy-start.18
  116.8 0.9 copy-start.21
  117.7 3.5 %copy-start.13 = (bf16[384,128]{1,0:T(8,128)(2,1)S(1)}, bf16[384,128]{1,0:T(8,128)(2,1)}, u32[]{:S(2)}) copy-start(bf16[384,128]{1,0:T(8,128)(2,1)} %copy-done.12) | copy-start | bytes 294916
  117.7 9.5 %copy-start.1 = (bf16[4096,128]{1,0:T(8,128)(2,1)S(1)}, bf16[4096,128]{1,0:T(8,128)(2,1)}, u32[]{:S(2)}) copy-start(bf16[4096,128]{1,0:T(8,128)(2,1)} %param.10) | copy-start | bytes 3145732
  117.7 9.5 %copy-start.19 = (s32[8,128]{1,0:T(8,128)S(1)}, s32[8,128]{1,0:T(8,128)}, u32[]{:S(2)}) copy-start(s32[8,128]{1,0:T(8,128)} %get-tuple-element.21.pool) | copy-start | bytes 12292
  117.7 9.5 %copy-start.22 = (f32[8,8,512]{2,1,0:T(8,128)S(1)}, f32[8,8,512]{2,1,0:T(8,128)}, u32[]{:S(2)}) copy-start(f32[8,8,512]{2,1,0:T(8,128)} %get-tuple-element.22.refs_0_.tsq) | copy-start | bytes 393220
  120.2 1.0 copy-start.7
  121.2 33.1 %collective-permute-start.12 = (bf16[384,128]{1,0:T(8,128)(2,1)S(1)}, bf16[384,128]{1,0:T(8,128)(2,1)S(1)}, u32[]{:S(2)}, u32[]{:S(2)}) collective-permute-start(bf16[384,128]{1,0:T(8,128)(2,1)S(1)} %copy-done.13), channel_id=1, source_target_pairs={{0,16},{8,24},{16,0},{24,8},{1,17},{9,25},{17,1},{25,9},{2,18},{10... | collective-permute-start | bytes 294920 | tf_op jit(solution)/shard_map/ppermute | solution.py:596
  123.4 30.9 %collective-permute-start.13 = (bf16[384,128]{1,0:T(8,128)(2,1)S(1)}, bf16[384,128]{1,0:T(8,128)(2,1)S(1)}, u32[]{:S(2)}, u32[]{:S(2)}) collective-permute-start(bf16[384,128]{1,0:T(8,128)(2,1)S(1)} %copy-done.13), channel_id=1, source_target_pairs={{0,24},{8,16},{16,8},{24,0},{1,25},{9,17},{17,9},{25,1},{2,26},{10... | collective-permute-start | bytes 294920 | tf_op jit(solution)/shard_map/ppermute | solution.py:596
  127.2 1.2 copy-start.8
  145.7 8.6 %copy-start.2 = (bf16[8,512,256]{2,1,0:T(8,128)(2,1)S(1)}, bf16[8,512,256]{2,1,0:T(8,128)(2,1)}, u32[]{:S(2)}) copy-start(bf16[8,512,256]{2,1,0:T(8,128)(2,1)} %leaf_interp.1) | copy-start | bytes 6291460
  145.7 8.6 %copy-start.3 = (bf16[1,2048,256]{2,1,0:T(8,128)(2,1)S(1)}, bf16[1,2048,256]{2,1,0:T(8,128)(2,1)}, u32[]{:S(2)}) copy-start(bf16[1,2048,256]{2,1,0:T(8,128)(2,1)} %param.15) | copy-start | bytes 3145732
  145.7 8.6 %copy-start.5 = (bf16[8,512,128]{2,1,0:T(8,128)(2,1)S(1)}, bf16[8,512,128]{2,1,0:T(8,128)(2,1)}, u32[]{:S(2)}) copy-start(bf16[8,512,128]{2,1,0:T(8,128)(2,1)} %copy-done.4) | copy-start | bytes 3145732
  145.7 8.6 %copy-start.11 = (bf16[1,256,256]{2,1,0:T(8,128)(2,1)S(1)}, bf16[1,256,256]{2,1,0:T(8,128)(2,1)}, u32[]{:S(2)}) copy-start(bf16[1,256,256]{2,1,0:T(8,128)(2,1)} %param.18) | copy-start | bytes 393220
  145.7 8.6 %copy-start.15 = (s32[3]{0:T(128)S(1)}, s32[3]{0:T(128)}, u32[]{:S(2)}) copy-start(s32[3]{0:T(128)} %pad_add_fusion.where) | copy-start | bytes 40
  145.7 8.6 %copy-start.16 = (s32[1,4]{1,0:T(1,128)S(1)}, s32[1,4]{1,0:T(1,128)}, u32[]{:S(2)}) copy-start(s32[1,4]{1,0:T(1,128)} %partners.1) | copy-start | bytes 52
  153.2 1.0 copy-start.9
  154.3 1.2 copy-start.10

commit v6 on v5

--- a/solution.py
+++ b/solution.py
@@ -331,11 +331,9 @@
     )
 
 
-def near_remote_kernel(near_count, first, parts, stage, pool, points, tsq, *refs):
+def near_remote_kernel(near_count, first, parts, pool, points, tsq, *refs):
     got, refs = refs[:parts], refs[parts:]
-    taken = 2 if stage == "first" else 1
-    inits, refs = refs[:taken], refs[taken:]
-    acc, tl, sl, x, pts, ssq, qs, sem_got, sem_x, sem_acc = refs
+    init, out, tl, sl, x, pts, ssq, qs, acc, sem_got, sem_x, sem_acc = refs
     leaf_dev, leaf_size, _ = points.shape
     rhs = acc.shape[1]
     tiles = leaf_size // LANES
@@ -356,21 +354,14 @@
                 )
             moves.append(one)
     x_copy = copy_in(points, x, sem_x)
-    acc_copies = []
-    if stage == "first":
-        base = 0
-        for at, init in enumerate(inits):
-            rows = pl.ds(base, init.shape[0])
-            acc_copies.append(copy_in(init, acc.at[rows], sem_acc.at[at]))
-            base += init.shape[0]
+    acc_copy = copy_in(init, acc, sem_acc)
     for at, one in enumerate(moves):
         one[0].wait()
         ssq[at] = source_term(pts[at])
         for move in one[1:]:
             move.wait()
     x_copy.wait()
-    for move in acc_copies:
-        move.wait()
+    acc_copy.wait()
 
     low = leaf_dev + first * CAP
 
@@ -381,37 +372,35 @@
         return kernel_tile(pts[source], ssq[source], x[target], tsq[target])
 
     run_pairs(pool, near_count, (0, leaf_dev), keep, tl, sl, tile_of, lambda s: qs[s], acc, 0)
-
-
-def near_remote(pool, near_count, points, tsq, first, got, inits, stage):
+    copy_in(acc, out, sem_acc).wait()
+
+
+def near_remote(pool, near_count, points, tsq, first, got, init):
     leaf_dev, leaf_size, coords = points.shape
-    rhs = inits[0].shape[1]
+    rhs = init.shape[1]
     places = len(got) * CAP
-    sums = (leaf_dev, rhs, leaf_size)
-    scratch = [
-        pltpu.SMEM((leaf_dev * near_count + 1,), i32),
-        pltpu.SMEM((leaf_dev * near_count + 1,), i32),
-        pltpu.VMEM(points.shape, bf16),
-        pltpu.VMEM((places, leaf_size, coords), bf16),
-        pltpu.VMEM((places, leaf_size, LANES), f32),
-        pltpu.VMEM((places, rhs, leaf_size), bf16),
-        pltpu.SemaphoreType.DMA((places, 1 + leaf_size // LANES)),
-        pltpu.SemaphoreType.DMA,
-        pltpu.SemaphoreType.DMA((2,)),
-    ]
-    spec = in_hbm() if stage == "first" else vmem()
+    sem = pltpu.SemaphoreType.DMA
     return call(
-        functools.partial(near_remote_kernel, near_count, first, len(got), stage),
-        jax.ShapeDtypeStruct(sums, f32),
-        [smem(), in_hbm(), vmem()] + [in_hbm()] * len(got) + [spec] * len(inits),
+        functools.partial(near_remote_kernel, near_count, first, len(got)),
+        jax.ShapeDtypeStruct(init.shape, f32),
+        [smem(), in_hbm(), vmem()] + [in_hbm()] * (len(got) + 1),
         near_cost(len(got) * leaf_dev, leaf_size, coords, rhs),
-        (pool, points, tsq, *got, *inits),
-        scratch=scratch,
-        own=None
-        if stage == "first"
-        else (leaf_dev * rhs * 4 + places * (coords * 2 + LANES * 4 + rhs * 2)) * leaf_size
-        + (2 << 20),
-        alias={3 + len(got): 0} if stage == "middle" else None,
+        (pool, points, tsq, *got, init),
+        scratch=[
+            pltpu.SMEM((leaf_dev * near_count + 1,), i32),
+            pltpu.SMEM((leaf_dev * near_count + 1,), i32),
+            pltpu.VMEM(points.shape, bf16),
+            pltpu.VMEM((places, leaf_size, coords), bf16),
+            pltpu.VMEM((places, leaf_size, LANES), f32),
+            pltpu.VMEM((places, rhs, leaf_size), bf16),
+            pltpu.VMEM(init.shape, f32),
+            sem((places, 1 + leaf_size // LANES)),
+            sem,
+            sem,
+        ],
+        own=None,
+        outs=[in_hbm()],
+        alias={3 + len(got): 0},
     )
 
 
@@ -546,14 +535,19 @@
         cost(1e9, 2e6),
         (where, skel_top, *pairs),
         scratch=[pltpu.SemaphoreType.DMA((size,))],
-        own=2 << 20,
-    )
-
-
-def far_kernel(where, partners, mids, acc, interp_top, interp_mid, leaf_interp, *refs):
-    tops, out = refs[:-1], refs[-1]
+        own=None,
+    )
+
+
+def far_kernel(where, partners, mids_in, acc, interp_top, mid_in, leaf_in, *refs):
+    tops, refs = refs[:-9], refs[-9:]
+    out, mids, sums, interp_mid, leaf_interp, sem_p, sem_a, sem_m, sem_l = refs
     leaf_dev, leaf_size, skel = leaf_interp.shape
     rhs = acc.shape[1]
+    p_copy = copy_in(mids_in, mids, sem_p)
+    m_copy = copy_in(mid_in, interp_mid, sem_m)
+    l_copies = [copy_in(leaf_in.at[m], leaf_interp.at[m], sem_l.at[m]) for m in range(leaf_dev)]
+    a_copy = copy_in(acc, sums, sem_a)
 
     def pair(source_ref, target, target_sq):
         source = source_ref[:skel, :]
@@ -566,6 +560,7 @@
     top_sum = jnp.zeros((rhs, skel), f32)
     for other in tops[1:]:
         top_sum = top_sum + pair(other, target, target_sq)
+    p_copy.wait()
     target = mids[0, :skel, :]
     target_sq = target_term(target)
     mid_sum = jnp.zeros((rhs, skel), f32)
@@ -573,10 +568,14 @@
         distance = jnp.bitwise_xor(partners[0, at] - where[2], where[1])
         mid_sum = mid_sum + pair(mids.at[place(distance, mids.shape[0])], target, target_sq)
     total = (mid_sum + dot_rows(top_sum.astype(bf16), interp_top[...])).astype(bf16)
+    m_copy.wait()
     for m in range(leaf_dev):
         leaf_down = dot_rows(total, interp_mid[m * skel : (m + 1) * skel, :]).astype(bf16)
+        l_copies[m].wait()
         distant = dot_rows(leaf_down, leaf_interp[m])
-        out[:, m * leaf_size : (m + 1) * leaf_size] = acc[m] + distant
+        if m == 0:
+            a_copy.wait()
+        out[:, m * leaf_size : (m + 1) * leaf_size] = sums[m] + distant
 
 
 def far(where, partners, mids, acc, tops, interp_top, interp_mid, leaf_interp):
@@ -585,10 +584,20 @@
     return call(
         far_kernel,
         jax.ShapeDtypeStruct((rhs, leaf_dev * leaf_size), f32),
-        [smem()] * 2 + [vmem()] * (5 + len(tops)),
+        [smem()] * 2 + [in_hbm()] * 2 + [vmem()] + [in_hbm()] * 2 + [vmem()] * len(tops),
         cost(1e9, 6e6, 5e5),
         (where, partners, mids, acc, interp_top, interp_mid, leaf_interp, *tops),
-        own=1 << 20,
+        scratch=[
+            pltpu.VMEM(mids.shape, bf16),
+            pltpu.VMEM(acc.shape, f32),
+            pltpu.VMEM(interp_mid.shape, bf16),
+            pltpu.VMEM(leaf_interp.shape, bf16),
+            pltpu.SemaphoreType.DMA,
+            pltpu.SemaphoreType.DMA,
+            pltpu.SemaphoreType.DMA,
+            pltpu.SemaphoreType.DMA((leaf_dev,)),
+        ],
+        own=None,
     )
 
 
@@ -636,29 +645,26 @@
     first, second, third, last = across(group)
     inner = list(range(1, group // 2))
     got = {}
-    for distances, carried in ((first, ()), (second + third + last, ()), (inner, (message, across_message))):
+    for distances, carried in ((first + second + third + last, ()), (inner, (message, across_message))):
         asked = pack(where, handed, blocks, charges_t, distances, *carried)
         for distance, one in zip(distances, asked):
             got[distance] = swapped(one, "sub", group, distance)
     pair = asked[-1]
     pairs = [pair] + [swapped(pair, "sub", group, d) for d in inner]
 
-    half = leaf_dev // 2
-    sum0, tsq = near_local(pool, near_count, blocks, charges_t, (0, half))
-    sum1 = near_local(pool, near_count, blocks, charges_t, (half, leaf_dev), tsq)
-    sums = [sum0, sum1]
+    local_sum, tsq = near_local(pool, near_count, blocks, charges_t, (0, leaf_dev))
+    total = local_sum
 
     mids, top_own = top_prepare(where, skel_top, pairs)
     tops = [top_own]
     for distance in range(1, groups):
         tops.append(swapped(top_own, "leaf", groups, distance))
 
-    for at, span in enumerate((first + second, third, inner, last)):
-        stage = "first" if at == 0 else "middle"
+    for span in (first + second, inner, third, last):
         part = [got[distance] for distance in span]
-        sums = [near_remote(pool, near_count, blocks, tsq, span[0], part, sums, stage)]
+        total = near_remote(pool, near_count, blocks, tsq, span[0], part, total)
     total = far(
-        where, mid_partners, mids, sums[0], tops, interp_top[0], interp_mid[0], leaf_interpolant
+        where, mid_partners, mids, total, tops, interp_top[0], interp_mid[0], leaf_interpolant
     )
     return total.T
 

time: 161 us -> 142 us (0.88)
  waiting for transfers between devices: 24.2 us -> 8.88 us
  local copies, waits for them, and re-layouts: 12.4 us -> 0 us
  blocking collectives: 0 us -> 7.98 us
    ppermute x14, waiting for transfers between devices: 24.2 us -> 8.88 us  [swapped(): return lax.ppermute(value, axis, [(i, i ^ distance) for i in range(size)])]
    unnamed x46 -> x0, local copies, waits for them, and re-layouts: 12.4 us -> none
    all_to_all x0 -> x1, blocking collectives: none -> 7.98 us  [body(): lax.all_to_all(chosen, 'sub', split_axis=0, concat_axis=0, tiled=True)]
    ppermute x14, starting transfers between devices: 34.8 us -> 40.6 us  [swapped(): return lax.ppermute(value, axis, [(i, i ^ distance) for i in range(size)])]
    all_to_all x1 -> x0, starting transfers between devices: 5.72 us -> none  [body(): lax.all_to_all(chosen, 'sub', split_axis=0, concat_axis=0, tiled=True)]
    pallas_call x13 -> x11, Pallas kernels: 81.7 us -> 83.3 us  [call(): pl.pallas_call(kernel, out_shape=out_shape, in_specs=in_specs, out_specs=...]
  transfers between devices with their start and end apart: 15 -> 14, of which waited for: 4 -> 1; matrix products, arithmetic and copies ran while one was open for 0% -> 0% of each run, Pallas kernels for 47% -> 49%
where the time goes in v6:
time: 142 us
  Pallas kernels  83.3 us (59%)
  starting transfers between devices  40.6 us (29%)
  waiting for transfers between devices  8.88 us (6%)
  blocking collectives  7.98 us (6%)
    pallas_call x11, Pallas kernels, call(): pl.pallas_call(kernel, out_shape=out_shape, in_specs=in_specs, out_specs=...  83.3 us
    ppermute x14, starting transfers between devices, swapped(): return lax.ppermute(value, axis, [(i, i ^ distance) for i in range(size)])  40.6 us
    ppermute x14, waiting for transfers between devices, swapped(): return lax.ppermute(value, axis, [(i, i ^ distance) for i in range(size)])  8.88 us
    all_to_all x1, blocking collectives, body(): lax.all_to_all(chosen, 'sub', split_axis=0, concat_axis=0, tiled=True)  7.98 us
  transfers between devices with their start and end apart: 14, of which 1 were waited for; matrix products, arithmetic and copies ran while one was open for 0% of the time, Pallas kernels for 49%

profile of v6, /device:TPU:9, one launch (start us, length us, event | category | flops | bytes accessed | tf_op | source)
XLA Modules:
  0.0 141.7 jit_solution(16372856551762790372)
XLA Ops:
  0.0 6.6 %shard_map.101.refs_0_ = bf16[512,128]{1,0:T(8,128)(2,1)} custom-call(bf16[8,512,128]{2,1,0:T(8,128)(2,1)} %bitcast.12, bf16[64,4096]{1,0:T(8,128)(2,1)} %bitcast.20, bf16[8,512,256]{2,1,0:T(8,128)(2,1)} %leaf_in.1, bf16[2048,256]{1,0:T(8,128)(2,1)} %bitcast.24, bf16[256,256]{1,0:T(8,128)(2,1)} %bitcast.26, s32[8,256]{1,0:T(8,128)} %refs_5_.1, s32[1,256]{1,0:T(1,128)} %refs_6_.1), custom_call_target="tpu_custom_call" | custom-call | flops 3000000000 | bytes 5000000 | tf_op jit(solution)/shard_map/pallas_call | solution.py:92
  6.6 2.4 %collective-permute-start = (bf16[512,128]{1,0:T(8,128)(2,1)}, bf16[512,128]{1,0:T(8,128)(2,1)}, u32[]{:S(2)}, u32[]{:S(2)}) collective-permute-start(bf16[512,128]{1,0:T(8,128)(2,1)} %shard_map.101.refs_0_), channel_id=1, source_target_pairs={{0,4},{1,5},{2,6},{3,7},{4,0},{5,1},{6,2},{7,3},{8,12},{9,13},{10,... | collective-permute-start | bytes 393224 | tf_op jit(solution)/shard_map/ppermute | solution.py:605
  9.0 0.6 pad_add_fusion.where
  9.6 1.7 %shard_map.100 = (s32[8,8]{1,0:T(8,128)}, s32[8,128]{1,0:T(8,128)}) custom-call(s32[3]{0:T(128)} %pad_add_fusion.where, s32[8,12]{1,0:T(8,128)} %near.1), custom_call_target="tpu_custom_call" | custom-call | flops 1000000 | bytes 100000 | tf_op jit(solution)/shard_map/pallas_call | solution.py:92
  11.2 8.0 %all_to_all.11 = s32[8,1,8]{2,1,0:T(1,128)} all-to-all(s32[8,1,8]{2,1,0:T(1,128)} %bitcast.30), channel_id=1, replica_groups=mesh['leaf'=4,'sub'=8] {'sub'}, dimensions={0} | all-to-all | bytes 512 | tf_op jit(solution)/shard_map/all_to_all | solution.py:638
  19.2 4.0 %shard_map.105 = (bf16[1536,128]{1,0:T(8,128)(2,1)}, bf16[1536,128]{1,0:T(8,128)(2,1)}, bf16[1536,128]{1,0:T(8,128)(2,1)}, bf16[1536,128]{1,0:T(8,128)(2,1)}) custom-call(s32[3]{0:T(128)} %pad_add_fusion.where, s32[8,8]{1,0:T(8,128)} %bitcast.28, bf16[8,512,128]{2,1,0:T(8,128)(2,1)} %bitcast.13, bf16[64,4096]{1,0:T(8,128)(2,1)} %bitcast.21), custom_call_target="tpu_custom_call" | custom-call | flops 100000 | bytes 3145728 | tf_op jit(solution)/shard_map/pallas_call | solution.py:92
  23.2 1.0 collective-permute-start.10
  24.2 1.8 %collective-permute-start.9 = (bf16[1536,128]{1,0:T(8,128)(2,1)}, bf16[1536,128]{1,0:T(8,128)(2,1)}, u32[]{:S(2)}, u32[]{:S(2)}) collective-permute-start(bf16[1536,128]{1,0:T(8,128)(2,1)} %get-tuple-element.29), channel_id=1, source_target_pairs={{0,4},{1,5},{2,6},{3,7},{4,0},{5,1},{6,2},{7,3},{8,12},{9,13},{10,... | collective-permute-start | bytes 1179656 | tf_op jit(solution)/shard_map/ppermute | solution.py:605
  26.1 0.0 collective-permute-done.refs_1_
  26.1 3.7 %shard_map.102 = (bf16[1536,128]{1,0:T(8,128)(2,1)}, bf16[1536,128]{1,0:T(8,128)(2,1)}, bf16[1536,128]{1,0:T(8,128)(2,1)}, bf16[1024,128]{1,0:T(8,128)(2,1)}) custom-call(s32[3]{0:T(128)} %pad_add_fusion.where, s32[8,8]{1,0:T(8,128)} %bitcast.29, bf16[8,512,128]{2,1,0:T(8,128)(2,1)} %bitcast.14, bf16[64,4096]{1,0:T(8,128)(2,1)} %bitcast.22, ...), custom_call_target="tpu_custom_call" | custom-call | flops 100000 | bytes 2359296 | tf_op jit(solution)/shard_map/pallas_call | solution.py:92
  29.7 0.7 collective-permute-start.1
  30.4 1.1 collective-permute-start.2
  31.5 1.0 collective-permute-start.3
  32.4 21.2 %shard_map.104 = (f32[8,64,512]{2,1,0:T(8,128)}, f32[8,8,512]{2,1,0:T(8,128)}) custom-call(s32[8,128]{1,0:T(8,128)} %get-tuple-element.22.pool, bf16[8,512,128]{2,1,0:T(8,128)(2,1)} %bitcast.15, bf16[64,4096]{1,0:T(8,128)(2,1)} %bitcast.23), custom_call_target="tpu_custom_call" | custom-call | flops 19327352832 | bytes 3000000 | tf_op jit(solution)/shard_map/pallas_call | solution.py:92
  53.6 0.0 collective-permute-done.1.refs_1_
  53.6 2.1 %collective-permute-start.5 = (bf16[1536,128]{1,0:T(8,128)(2,1)}, bf16[1536,128]{1,0:T(8,128)(2,1)}, u32[]{:S(2)}, u32[]{:S(2)}) collective-permute-start(bf16[1536,128]{1,0:T(8,128)(2,1)} %get-tuple-element.25), channel_id=1, source_target_pairs={{0,6},{1,7},{2,4},{3,5},{4,2},{5,3},{6,0},{7,1},{8,14},{9,15},{10,... | collective-permute-start | bytes 1179656 | tf_op jit(solution)/shard_map/ppermute | solution.py:605
  55.7 0.0 collective-permute-done.2.refs_2_
  55.7 0.9 collective-permute-start.4
  56.6 0.0 collective-permute-done.3.refs_3_
  56.6 0.3 collective-permute-start.6
  57.0 4.0 %shard_map.103 = (bf16[8,512,128]{2,1,0:T(8,128)(2,1)}, bf16[384,128]{1,0:T(8,128)(2,1)}) custom-call(s32[3]{0:T(128)} %pad_add_fusion.where, s32[1,256]{1,0:T(1,128)} %skel_top.1, bf16[1024,128]{1,0:T(8,128)(2,1)} %get-tuple-element.20.refs_0_, bf16[1024,128]{1,0:T(8,128)(2,1)} %collective-permute-done.1.refs_1_, ...), custom_call_target="tpu_custom_call" | custom-call | flops 1000000000 | bytes 2000000 | tf_op jit(solution)/shard_map/pallas_call | solution.py:92
  61.0 0.0 collective-permute-done.10.refs_1_
  61.0 2.5 %collective-permute-start.7 = (bf16[1536,128]{1,0:T(8,128)(2,1)}, bf16[1536,128]{1,0:T(8,128)(2,1)}, u32[]{:S(2)}, u32[]{:S(2)}) collective-permute-start(bf16[1536,128]{1,0:T(8,128)(2,1)} %get-tuple-element.27), channel_id=1, source_target_pairs={{0,2},{1,3},{2,0},{3,1},{4,6},{5,7},{6,4},{7,5},{8,10},{9,11},{10,... | collective-permute-start | bytes 1179656 | tf_op jit(solution)/shard_map/ppermute | solution.py:605
  63.5 8.8 %collective-permute-done.9.refs_0_ = bf16[1536,128]{1,0:T(8,128)(2,1)} collective-permute-done((bf16[1536,128]{1,0:T(8,128)(2,1)}, bf16[1536,128]{1,0:T(8,128)(2,1)}, u32[]{:S(2)}, u32[]{:S(2)}) %collective-permute-start.9) | collective-permute-done | bytes 393248 | tf_op jit(solution)/shard_map/ppermute | solution.py:605
  72.3 5.9 %collective-permute-start.8 = (bf16[1536,128]{1,0:T(8,128)(2,1)}, bf16[1536,128]{1,0:T(8,128)(2,1)}, u32[]{:S(2)}, u32[]{:S(2)}) collective-permute-start(bf16[1536,128]{1,0:T(8,128)(2,1)} %get-tuple-element.28), channel_id=1, source_target_pairs={{0,3},{1,2},{2,1},{3,0},{4,7},{5,6},{6,5},{7,4},{8,11},{9,10},{10,... | collective-permute-start | bytes 1179656 | tf_op jit(solution)/shard_map/ppermute | solution.py:605
  78.2 4.0 %shard_map.106.refs_3_ = f32[8,64,512]{2,1,0:T(8,128)} custom-call(s32[8,128]{1,0:T(8,128)} %get-tuple-element.22.pool, bf16[8,512,128]{2,1,0:T(8,128)(2,1)} %bitcast.16, f32[8,8,512]{2,1,0:T(8,128)} %get-tuple-element.23.tsq, bf16[1536,128]{1,0:T(8,128)(2,1)} %collective-permute-done.9.refs_0_, ...), custom_call_target="tpu_custom_call", output_to_operand_aliasing={{}: (5, {})} | custom-call | flops 6442450944 | bytes 3000000 | tf_op jit(solution)/shard_map/pallas_call | solution.py:92
  82.3 0.0 collective-permute-done.6.refs_0_
  82.3 10.2 %collective-permute-start.11 = (bf16[384,128]{1,0:T(8,128)(2,1)}, bf16[384,128]{1,0:T(8,128)(2,1)}, u32[]{:S(2)}, u32[]{:S(2)}) collective-permute-start(bf16[384,128]{1,0:T(8,128)(2,1)} %get-tuple-element.32.refs_0_), channel_id=1, source_target_pairs={{0,8},{8,0},{16,24},{24,16},{1,9},{9,1},{17,25},{25,17},{2,10},{10... | collective-permute-start | bytes 294920 | tf_op jit(solution)/shard_map/ppermute | solution.py:605
  92.5 0.0 collective-permute-done.7.refs_1_
  92.5 10.7 %collective-permute-start.12 = (bf16[384,128]{1,0:T(8,128)(2,1)}, bf16[384,128]{1,0:T(8,128)(2,1)}, u32[]{:S(2)}, u32[]{:S(2)}) collective-permute-start(bf16[384,128]{1,0:T(8,128)(2,1)} %get-tuple-element.32.refs_0_), channel_id=1, source_target_pairs={{0,16},{8,24},{16,0},{24,8},{1,17},{9,25},{17,1},{25,9},{2,18},{10... | collective-permute-start | bytes 294920 | tf_op jit(solution)/shard_map/ppermute | solution.py:605
  103.2 0.0 collective-permute-done.8.refs_2_
  103.2 0.0 collective-permute-start.13
  103.2 18.4 %shard_map.107.refs_1_ = f32[8,64,512]{2,1,0:T(8,128)} custom-call(s32[8,128]{1,0:T(8,128)} %get-tuple-element.22.pool, bf16[8,512,128]{2,1,0:T(8,128)(2,1)} %bitcast.17, f32[8,8,512]{2,1,0:T(8,128)} %get-tuple-element.23.tsq, bf16[1536,128]{1,0:T(8,128)(2,1)} %collective-permute-done.6.refs_0_, ...), custom_call_target="tpu_custom_call", output_to_operand_aliasing={{}: (6, {})} | custom-call | flops 9663676416 | bytes 3000000 | tf_op jit(solution)/shard_map/pallas_call | solution.py:92
  121.6 0.0 collective-permute-done.5.refs_0_
  121.7 3.8 %shard_map.108.refs_1_ = f32[8,64,512]{2,1,0:T(8,128)} custom-call(s32[8,128]{1,0:T(8,128)} %get-tuple-element.22.pool, bf16[8,512,128]{2,1,0:T(8,128)(2,1)} %bitcast.18, f32[8,8,512]{2,1,0:T(8,128)} %get-tuple-element.23.tsq, bf16[1536,128]{1,0:T(8,128)(2,1)} %collective-permute-done.5.refs_0_, ...), custom_call_target="tpu_custom_call", output_to_operand_aliasing={{}: (4, {})} | custom-call | flops 3221225472 | bytes 3000000 | tf_op jit(solution)/shard_map/pallas_call | solution.py:92
  125.5 0.0 collective-permute-done.4.refs_0_
  125.5 8.6 %shard_map.109.acc = f32[8,64,512]{2,1,0:T(8,128)} custom-call(s32[8,128]{1,0:T(8,128)} %get-tuple-element.22.pool, bf16[8,512,128]{2,1,0:T(8,128)(2,1)} %bitcast.19, f32[8,8,512]{2,1,0:T(8,128)} %get-tuple-element.23.tsq, bf16[1536,128]{1,0:T(8,128)(2,1)} %collective-permute-done.4.refs_0_, ...), custom_call_target="tpu_custom_call", output_to_operand_aliasing={{}: (4, {})} | custom-call | flops 3221225472 | bytes 3000000 | tf_op jit(solution)/shard_map/pallas_call | solution.py:92
  134.1 0.0 collective-permute-done.11.refs_1_
  134.1 0.0 collective-permute-done.12.refs_2_
  134.2 0.0 collective-permute-done.13.refs_3_
  134.2 7.3 %shard_map.110 = f32[64,4096]{1,0:T(8,128)} custom-call(s32[3]{0:T(128)} %pad_add_fusion.where, s32[1,4]{1,0:T(1,128)} %partners.1, bf16[8,512,128]{2,1,0:T(8,128)(2,1)} %get-tuple-element.21.mids_in, f32[8,64,512]{2,1,0:T(8,128)} %shard_map.109.acc, bf16[256,256]{1,0:T(8,128)(2,1)} %bitcast.27, bf16[2048,256]{1,0:T(8,128)(2,1)} %bitcast.25, ...), custom_call_target="tpu_custom_call" | custom-call | flops 1000000000 | bytes 6000000 | tf_op jit(solution)/shard_map/pallas_call | solution.py:92
Async XLA Ops:
  6.6 19.5 %collective-permute-start = (bf16[512,128]{1,0:T(8,128)(2,1)}, bf16[512,128]{1,0:T(8,128)(2,1)}, u32[]{:S(2)}, u32[]{:S(2)}) collective-permute-start(bf16[512,128]{1,0:T(8,128)(2,1)} %shard_map.101.refs_0_), channel_id=1, source_target_pairs={{0,4},{1,5},{2,6},{3,7},{4,0},{5,1},{6,2},{7,3},{8,12},{9,13},{10,... | collective-permute-start | bytes 393224 | tf_op jit(solution)/shard_map/ppermute | solution.py:605
  23.2 37.7 %collective-permute-start.10 = (bf16[1536,128]{1,0:T(8,128)(2,1)}, bf16[1536,128]{1,0:T(8,128)(2,1)}, u32[]{:S(2)}, u32[]{:S(2)}) collective-permute-start(bf16[1536,128]{1,0:T(8,128)(2,1)} %get-tuple-element.30), channel_id=1, source_target_pairs={{0,5},{1,4},{2,7},{3,6},{4,1},{5,0},{6,3},{7,2},{8,13},{9,12},{10,... | collective-permute-start | bytes 1179656 | tf_op jit(solution)/shard_map/ppermute | solution.py:605
  24.2 48.1 %collective-permute-start.9 = (bf16[1536,128]{1,0:T(8,128)(2,1)}, bf16[1536,128]{1,0:T(8,128)(2,1)}, u32[]{:S(2)}, u32[]{:S(2)}) collective-permute-start(bf16[1536,128]{1,0:T(8,128)(2,1)} %get-tuple-element.29), channel_id=1, source_target_pairs={{0,4},{1,5},{2,6},{3,7},{4,0},{5,1},{6,2},{7,3},{8,12},{9,13},{10,... | collective-permute-start | bytes 1179656 | tf_op jit(solution)/shard_map/ppermute | solution.py:605
  29.7 23.9 %collective-permute-start.1 = (bf16[1024,128]{1,0:T(8,128)(2,1)}, bf16[1024,128]{1,0:T(8,128)(2,1)}, u32[]{:S(2)}, u32[]{:S(2)}) collective-permute-start(bf16[1024,128]{1,0:T(8,128)(2,1)} %get-tuple-element.20.refs_0_), channel_id=1, source_target_pairs={{0,1},{1,0},{2,3},{3,2},{4,5},{5,4},{6,7},{7,6},{8,9},{9,8},{10,11... | collective-permute-start | bytes 786440 | tf_op jit(solution)/shard_map/ppermute | solution.py:605
  30.4 25.3 %collective-permute-start.2 = (bf16[1024,128]{1,0:T(8,128)(2,1)}, bf16[1024,128]{1,0:T(8,128)(2,1)}, u32[]{:S(2)}, u32[]{:S(2)}) collective-permute-start(bf16[1024,128]{1,0:T(8,128)(2,1)} %get-tuple-element.20.refs_0_), channel_id=1, source_target_pairs={{0,2},{1,3},{2,0},{3,1},{4,6},{5,7},{6,4},{7,5},{8,10},{9,11},{10,... | collective-permute-start | bytes 786440 | tf_op jit(solution)/shard_map/ppermute | solution.py:605
  31.5 25.2 %collective-permute-start.3 = (bf16[1024,128]{1,0:T(8,128)(2,1)}, bf16[1024,128]{1,0:T(8,128)(2,1)}, u32[]{:S(2)}, u32[]{:S(2)}) collective-permute-start(bf16[1024,128]{1,0:T(8,128)(2,1)} %get-tuple-element.20.refs_0_), channel_id=1, source_target_pairs={{0,3},{1,2},{2,1},{3,0},{4,7},{5,6},{6,5},{7,4},{8,11},{9,10},{10,... | collective-permute-start | bytes 786440 | tf_op jit(solution)/shard_map/ppermute | solution.py:605
  53.6 68.0 %collective-permute-start.5 = (bf16[1536,128]{1,0:T(8,128)(2,1)}, bf16[1536,128]{1,0:T(8,128)(2,1)}, u32[]{:S(2)}, u32[]{:S(2)}) collective-permute-start(bf16[1536,128]{1,0:T(8,128)(2,1)} %get-tuple-element.25), channel_id=1, source_target_pairs={{0,6},{1,7},{2,4},{3,5},{4,2},{5,3},{6,0},{7,1},{8,14},{9,15},{10,... | collective-permute-start | bytes 1179656 | tf_op jit(solution)/shard_map/ppermute | solution.py:605
  55.7 69.8 %collective-permute-start.4 = (bf16[1536,128]{1,0:T(8,128)(2,1)}, bf16[1536,128]{1,0:T(8,128)(2,1)}, u32[]{:S(2)}, u32[]{:S(2)}) collective-permute-start(bf16[1536,128]{1,0:T(8,128)(2,1)} %get-tuple-element.24), channel_id=1, source_target_pairs={{0,7},{1,6},{2,5},{3,4},{4,3},{5,2},{6,1},{7,0},{8,15},{9,14},{10,... | collective-permute-start | bytes 1179656 | tf_op jit(solution)/shard_map/ppermute | solution.py:605
  56.6 25.6 %collective-permute-start.6 = (bf16[1536,128]{1,0:T(8,128)(2,1)}, bf16[1536,128]{1,0:T(8,128)(2,1)}, u32[]{:S(2)}, u32[]{:S(2)}) collective-permute-start(bf16[1536,128]{1,0:T(8,128)(2,1)} %get-tuple-element.26), channel_id=1, source_target_pairs={{0,1},{1,0},{2,3},{3,2},{4,5},{5,4},{6,7},{7,6},{8,9},{9,8},{10,11... | collective-permute-start | bytes 1179656 | tf_op jit(solution)/shard_map/ppermute | solution.py:605
  61.0 31.5 %collective-permute-start.7 = (bf16[1536,128]{1,0:T(8,128)(2,1)}, bf16[1536,128]{1,0:T(8,128)(2,1)}, u32[]{:S(2)}, u32[]{:S(2)}) collective-permute-start(bf16[1536,128]{1,0:T(8,128)(2,1)} %get-tuple-element.27), channel_id=1, source_target_pairs={{0,2},{1,3},{2,0},{3,1},{4,6},{5,7},{6,4},{7,5},{8,10},{9,11},{10,... | collective-permute-start | bytes 1179656 | tf_op jit(solution)/shard_map/ppermute | solution.py:605
  72.3 30.9 %collective-permute-start.8 = (bf16[1536,128]{1,0:T(8,128)(2,1)}, bf16[1536,128]{1,0:T(8,128)(2,1)}, u32[]{:S(2)}, u32[]{:S(2)}) collective-permute-start(bf16[1536,128]{1,0:T(8,128)(2,1)} %get-tuple-element.28), channel_id=1, source_target_pairs={{0,3},{1,2},{2,1},{3,0},{4,7},{5,6},{6,5},{7,4},{8,11},{9,10},{10,... | collective-permute-start | bytes 1179656 | tf_op jit(solution)/shard_map/ppermute | solution.py:605
  82.3 51.9 %collective-permute-start.11 = (bf16[384,128]{1,0:T(8,128)(2,1)}, bf16[384,128]{1,0:T(8,128)(2,1)}, u32[]{:S(2)}, u32[]{:S(2)}) collective-permute-start(bf16[384,128]{1,0:T(8,128)(2,1)} %get-tuple-element.32.refs_0_), channel_id=1, source_target_pairs={{0,8},{8,0},{16,24},{24,16},{1,9},{9,1},{17,25},{25,17},{2,10},{10... | collective-permute-start | bytes 294920 | tf_op jit(solution)/shard_map/ppermute | solution.py:605
  92.5 41.7 %collective-permute-start.12 = (bf16[384,128]{1,0:T(8,128)(2,1)}, bf16[384,128]{1,0:T(8,128)(2,1)}, u32[]{:S(2)}, u32[]{:S(2)}) collective-permute-start(bf16[384,128]{1,0:T(8,128)(2,1)} %get-tuple-element.32.refs_0_), channel_id=1, source_target_pairs={{0,16},{8,24},{16,0},{24,8},{1,17},{9,25},{17,1},{25,9},{2,18},{10... | collective-permute-start | bytes 294920 | tf_op jit(solution)/shard_map/ppermute | solution.py:605
  103.2 31.0 %collective-permute-start.13 = (bf16[384,128]{1,0:T(8,128)(2,1)}, bf16[384,128]{1,0:T(8,128)(2,1)}, u32[]{:S(2)}, u32[]{:S(2)}) collective-permute-start(bf16[384,128]{1,0:T(8,128)(2,1)} %get-tuple-element.32.refs_0_), channel_id=1, source_target_pairs={{0,24},{8,16},{16,8},{24,0},{1,25},{9,17},{17,9},{25,1},{2,26},{10... | collective-permute-start | bytes 294920 | tf_op jit(solution)/shard_map/ppermute | solution.py:605

commit v7 on v5

--- a/solution.py
+++ b/solution.py
@@ -636,11 +636,11 @@
     first, second, third, last = across(group)
     inner = list(range(1, group // 2))
     got = {}
-    for distances, carried in ((first, ()), (second + third + last, ()), (inner, (message, across_message))):
-        asked = pack(where, handed, blocks, charges_t, distances, *carried)
+    for distances in (first + second + inner, third + last):
+        asked = pack(where, handed, blocks, charges_t, distances)
         for distance, one in zip(distances, asked):
             got[distance] = swapped(one, "sub", group, distance)
-    pair = asked[-1]
+    pair = jnp.concatenate((message, across_message), axis=0)
     pairs = [pair] + [swapped(pair, "sub", group, d) for d in inner]
 
     half = leaf_dev // 2
@@ -653,7 +653,7 @@
     for distance in range(1, groups):
         tops.append(swapped(top_own, "leaf", groups, distance))
 
-    for at, span in enumerate((first + second, third, inner, last)):
+    for at, span in enumerate((inner + first + second, third + last)):
         stage = "first" if at == 0 else "middle"
         part = [got[distance] for distance in span]
         sums = [near_remote(pool, near_count, blocks, tsq, span[0], part, sums, stage)]

time: 161 us -> 137 us (0.85)
  the two profiles are of different devices: /device:TPU:9 before, /device:TPU:5 now
where the time goes in v7:
time: 137 us; the launch traced here: 136 us
  Pallas kernels  76.2 us (56%)
  starting transfers between devices  46.4 us (34%)
  local copies, waits for them, and re-layouts  8.54 us (6%)
  waiting for transfers between devices  2.54 us (2%)
  other arithmetic  2.34 us (2%)
    pallas_call x10, Pallas kernels, call(): pl.pallas_call(kernel, out_shape=out_shape, in_specs=in_specs, out_specs=...  76.2 us
    ppermute x14, starting transfers between devices, swapped(): return lax.ppermute(value, axis, [(i, i ^ distance) for i in range(size)])  42.4 us
    unnamed x30, local copies, waits for them, and re-layouts  8.54 us
    all_to_all x1, starting transfers between devices, body(): lax.all_to_all(chosen, 'sub', split_axis=0, concat_axis=0, tiled=True)  4.03 us
  transfers between devices with their start and end apart: 15, of which 1 were waited for; matrix products, arithmetic and copies ran while one was open for 2% of the time, Pallas kernels for 48%

profile of v7, /device:TPU:5, one launch (start us, length us, event | category | flops | bytes accessed | tf_op | source)
XLA Modules:
  0.0 136.2 jit_solution(15267571929300363699)
XLA Ops:
  0.0 6.6 %shard_map.100 = bf16[512,128]{1,0:T(8,128)(2,1)} custom-call(bf16[8,512,128]{2,1,0:T(8,128)(2,1)} %bitcast.12, bf16[64,4096]{1,0:T(8,128)(2,1)} %bitcast.23, bf16[8,512,256]{2,1,0:T(8,128)(2,1)} %leaf_interp.1, bf16[2048,256]{1,0:T(8,128)(2,1)} %bitcast.19, bf16[256,256]{1,0:T(8,128)(2,1)} %bitcast.21, s32[8,256]{1,0:T(8,128)} %refs_5_.1, s32[1,256]{1,0:T(1,128)} %refs_6_.1), custom_call_target="tpu_custom_call" | custom-call | flops 3000000000 | bytes 5000000 | tf_op jit(solution)/shard_map/pallas_call | solution.py:92
  6.6 2.4 %collective-permute-start = (bf16[512,128]{1,0:T(8,128)(2,1)}, bf16[512,128]{1,0:T(8,128)(2,1)}, u32[]{:S(2)}, u32[]{:S(2)}) collective-permute-start(bf16[512,128]{1,0:T(8,128)(2,1)} %shard_map.100), channel_id=1, source_target_pairs={{0,4},{1,5},{2,6},{3,7},{4,0},{5,1},{6,2},{7,3},{8,12},{9,13},{10,... | collective-permute-start | bytes 393224 | tf_op jit(solution)/shard_map/ppermute | solution.py:596
  9.0 0.7 pad_add_fusion.where
  9.6 1.7 %shard_map.102 = (s32[8,8]{1,0:T(8,128)}, s32[8,128]{1,0:T(8,128)}) custom-call(s32[3]{0:T(128)} %pad_add_fusion.where, s32[8,12]{1,0:T(8,128)} %near.1), custom_call_target="tpu_custom_call" | custom-call | flops 1000000 | bytes 100000 | tf_op jit(solution)/shard_map/pallas_call | solution.py:92
  11.3 4.0 %all-to-all-start = ((s32[8,1,8]{2,1,0:T(1,128)}), s32[8,1,8]{2,1,0:T(1,128)}, u32[]{:S(2)}, u32[]{:S(2)}) async-start(s32[8,1,8]{2,1,0:T(1,128)} %bitcast.28), calls=%async_computation | async-start | bytes 8192 | tf_op jit(solution)/shard_map/all_to_all | solution.py:629
  15.3 0.0 collective-permute-done
  15.3 1.7 %pad_maximum_fusion.refs_0_ = bf16[1024,128]{1,0:T(8,128)(2,1)} fusion(bf16[512,128]{1,0:T(8,128)(2,1)} %collective-permute-done, bf16[512,128]{1,0:T(8,128)(2,1)} %shard_map.100), kind=kLoop, calls=%fused_computation | loop fusion | flops 524288 | bytes 524288 | tf_op jit(solution)/shard_map/concatenate | solution.py:643
  17.0 0.2 collective-permute-start.1
  17.2 1.3 collective-permute-start.2
  18.5 1.2 collective-permute-start.3
  19.6 12.8 %shard_map.103 = (f32[4,64,512]{2,1,0:T(8,128)}, f32[8,8,512]{2,1,0:T(8,128)}) custom-call(s32[8,128]{1,0:T(8,128)} %get-tuple-element.19.pool, bf16[8,512,128]{2,1,0:T(8,128)(2,1)} %bitcast.13, bf16[64,4096]{1,0:T(8,128)(2,1)} %bitcast.24), custom_call_target="tpu_custom_call" | custom-call | flops 9663676416 | bytes 3000000 | tf_op jit(solution)/shard_map/pallas_call | solution.py:92
  32.4 0.0 all-to-all-done
  32.4 4.2 %shard_map.105 = (bf16[1536,128]{1,0:T(8,128)(2,1)}, bf16[1536,128]{1,0:T(8,128)(2,1)}, bf16[1536,128]{1,0:T(8,128)(2,1)}, bf16[1536,128]{1,0:T(8,128)(2,1)}, bf16[1536,128]{1,0:T(8,128)(2,1)}) custom-call(s32[3]{0:T(128)} %pad_add_fusion.where, s32[8,8]{1,0:T(8,128)} %bitcast.9.handed, bf16[8,512,128]{2,1,0:T(8,128)(2,1)} %bitcast.14, bf16[64,4096]{1,0:T(8,128)(2,1)} %bitcast.25), custom_call_target="tpu_custom_call" | custom-call | flops 100000 | bytes 3932160 | tf_op jit(solution)/shard_map/pallas_call | solution.py:92
  36.6 4.3 %collective-permute-start.10 = (bf16[1536,128]{1,0:T(8,128)(2,1)}, bf16[1536,128]{1,0:T(8,128)(2,1)}, u32[]{:S(2)}, u32[]{:S(2)}) collective-permute-start(bf16[1536,128]{1,0:T(8,128)(2,1)} %get-tuple-element.28), channel_id=1, source_target_pairs={{0,5},{1,4},{2,7},{3,6},{4,1},{5,0},{6,3},{7,2},{8,13},{9,12},{10,... | collective-permute-start | bytes 1179656 | tf_op jit(solution)/shard_map/ppermute | solution.py:596
  40.9 1.1 collective-permute-start.6
  42.0 0.0 collective-permute-done.1.refs_1_
  42.0 1.3 collective-permute-start.7
  43.3 0.0 collective-permute-done.2.refs_2_
  43.3 0.2 collective-permute-start.8
  43.5 0.0 collective-permute-done.3.refs_3_
  43.5 0.0 collective-permute-start.9
  43.5 11.5 %shard_map.106.refs_6_ = f32[4,64,512]{2,1,0:T(8,128)} custom-call(s32[8,128]{1,0:T(8,128)} %get-tuple-element.19.pool, bf16[8,512,128]{2,1,0:T(8,128)(2,1)} %bitcast.15, bf16[64,4096]{1,0:T(8,128)(2,1)} %bitcast.26, f32[8,8,512]{2,1,0:T(8,128)} %get-tuple-element.20.refs_0_.tsq), custom_call_target="tpu_custom_call" | custom-call | flops 9663676416 | bytes 3000000 | tf_op jit(solution)/shard_map/pallas_call | solution.py:92
  55.1 3.0 %shard_map.104 = (bf16[1536,128]{1,0:T(8,128)(2,1)}, bf16[1536,128]{1,0:T(8,128)(2,1)}) custom-call(s32[3]{0:T(128)} %pad_add_fusion.where, s32[8,8]{1,0:T(8,128)} %bitcast.9.handed, bf16[8,512,128]{2,1,0:T(8,128)(2,1)} %bitcast.16, bf16[64,4096]{1,0:T(8,128)(2,1)} %bitcast.27), custom_call_target="tpu_custom_call" | custom-call | flops 100000 | bytes 1572864 | tf_op jit(solution)/shard_map/pallas_call | solution.py:92
  58.1 0.0 copy-start.9
  58.1 0.7 copy-done.9
  58.7 0.7 copy-done.13
  59.4 3.6 %shard_map.101 = (bf16[8,512,128]{2,1,0:T(8,128)(2,1)S(1)}, bf16[384,128]{1,0:T(8,128)(2,1)}) custom-call(s32[3]{0:T(128)S(1)} %copy-done.9, s32[1,256]{1,0:T(1,128)S(1)} %copy-done.13, bf16[1024,128]{1,0:T(8,128)(2,1)} %pad_maximum_fusion.refs_0_, bf16[1024,128]{1,0:T(8,128)(2,1)} %collective-permute-done.1.refs_1_, ...), custom_call_target="tpu_custom_call" | custom-call | flops 1000000000 | bytes 2000000 | tf_op jit(solution)/shard_map/pallas_call | solution.py:92
  63.1 0.0 copy-start.3
  63.1 1.0 copy-done.3
  64.0 0.0 collective-permute-done.10.refs_4_
  64.0 5.1 %collective-permute-start.4 = (bf16[1536,128]{1,0:T(8,128)(2,1)}, bf16[1536,128]{1,0:T(8,128)(2,1)}, u32[]{:S(2)}, u32[]{:S(2)}) collective-permute-start(bf16[1536,128]{1,0:T(8,128)(2,1)} %get-tuple-element.22), channel_id=1, source_target_pairs={{0,6},{1,7},{2,4},{3,5},{4,2},{5,3},{6,0},{7,1},{8,14},{9,15},{10,... | collective-permute-start | bytes 1179656 | tf_op jit(solution)/shard_map/ppermute | solution.py:596
  69.2 0.0 collective-permute-done.6.refs_0_
  69.2 0.2 collective-permute-start.5
  69.4 0.0 collective-permute-done.7.refs_1_
  69.4 4.7 %collective-permute-start.11 = (bf16[384,128]{1,0:T(8,128)(2,1)}, bf16[384,128]{1,0:T(8,128)(2,1)}, u32[]{:S(2)}, u32[]{:S(2)}) collective-permute-start(bf16[384,128]{1,0:T(8,128)(2,1)} %get-tuple-element.30.refs_0_), channel_id=1, source_target_pairs={{0,8},{8,0},{16,24},{24,16},{1,9},{9,1},{17,25},{25,17},{2,10},{10... | collective-permute-start | bytes 294920 | tf_op jit(solution)/shard_map/ppermute | solution.py:596
  74.1 2.5 %collective-permute-done.8.refs_2_ = bf16[1536,128]{1,0:T(8,128)(2,1)} collective-permute-done((bf16[1536,128]{1,0:T(8,128)(2,1)}, bf16[1536,128]{1,0:T(8,128)(2,1)}, u32[]{:S(2)}, u32[]{:S(2)}) %collective-permute-start.8) | collective-permute-done | bytes 393248 | tf_op jit(solution)/shard_map/ppermute | solution.py:596
  76.6 1.0 collective-permute-start.12
  77.6 0.0 collective-permute-done.9.refs_3_
  77.6 19.4 %collective-permute-start.13 = (bf16[384,128]{1,0:T(8,128)(2,1)}, bf16[384,128]{1,0:T(8,128)(2,1)}, u32[]{:S(2)}, u32[]{:S(2)}) collective-permute-start(bf16[384,128]{1,0:T(8,128)(2,1)} %get-tuple-element.30.refs_0_), channel_id=1, source_target_pairs={{0,24},{8,16},{16,8},{24,0},{1,25},{9,17},{17,9},{25,1},{2,26},{10... | collective-permute-start | bytes 294920 | tf_op jit(solution)/shard_map/ppermute | solution.py:596
  97.0 19.8 %shard_map.107.refs_2_ = f32[8,64,512]{2,1,0:T(8,128)} custom-call(s32[8,128]{1,0:T(8,128)} %get-tuple-element.19.pool, bf16[8,512,128]{2,1,0:T(8,128)(2,1)} %bitcast.17, f32[8,8,512]{2,1,0:T(8,128)} %get-tuple-element.20.refs_0_.tsq, bf16[1536,128]{1,0:T(8,128)(2,1)} %collective-permute-done.6.refs_0_, bf16[1536,128]{1,0:T(8,128)(2,1)} %collective-permute-done.7.refs_1_, ...), custom_call_target="tpu_custom_call" | custom-call | flops 16106127360 | bytes 3000000 | tf_op jit(solution)/shard_map/pallas_call | solution.py:92
  116.8 0.0 collective-permute-done.4.refs_0_
  116.8 0.0 collective-permute-done.5.refs_1_
  116.8 0.0 copy-start
  116.8 1.2 copy-done
  118.1 1.2 copy-done.5
  119.3 0.7 copy-done.12
  120.0 0.9 copy-done.14
  120.9 0.0 copy-start.10
  120.9 0.0 copy-start.11
  120.9 8.3 %shard_map.108.acc = f32[8,64,512]{2,1,0:T(8,128)S(1)} custom-call(s32[8,128]{1,0:T(8,128)S(1)} %copy-done.12, bf16[8,512,128]{2,1,0:T(8,128)(2,1)S(1)} %bitcast.18, f32[8,8,512]{2,1,0:T(8,128)S(1)} %copy-done.14, bf16[1536,128]{1,0:T(8,128)(2,1)} %collective-permute-done.4.refs_0_, ...), custom_call_target="tpu_custom_call", output_to_operand_aliasing={{}: (5, {})} | custom-call | flops 6442450944 | bytes 3000000 | tf_op jit(solution)/shard_map/pallas_call | solution.py:92
  129.3 0.0 copy-start.6
  129.3 1.0 copy-done.6
  130.2 0.0 collective-permute-done.11.refs_1_
  130.2 0.0 collective-permute-done.12.refs_2_
  130.2 0.0 collective-permute-done.13.refs_3_
  130.2 0.0 copy-done.1
  130.3 0.0 copy-done.2
  130.3 0.0 copy-done.4
  130.3 0.0 copy-done.8
  130.3 0.0 copy-done.10
  130.3 0.0 copy-done.11
  130.3 0.0 copy-start.7
  130.3 1.2 copy-done.7
  131.5 4.7 %shard_map.109 = f32[64,4096]{1,0:T(8,128)} custom-call(s32[3]{0:T(128)S(1)} %copy-done.10, s32[1,4]{1,0:T(1,128)S(1)} %copy-done.11, bf16[8,512,128]{2,1,0:T(8,128)(2,1)S(1)} %copy-done.4, f32[8,64,512]{2,1,0:T(8,128)S(1)} %copy-done.7, bf16[256,256]{1,0:T(8,128)(2,1)S(1)} %bitcast.22, bf16[2048,256]{1,0:T(8,128)(2,1)S(1)} %bitcast.20, ...), custom_call_target="tpu_custom_call" | custom-call | flops 1000000000 | bytes 6000000 | tf_op jit(solution)/shard_map/pallas_call | solution.py:92
  (8 shorter events, 0.0 us)
Async XLA Ops:
  6.6 8.7 %collective-permute-start = (bf16[512,128]{1,0:T(8,128)(2,1)}, bf16[512,128]{1,0:T(8,128)(2,1)}, u32[]{:S(2)}, u32[]{:S(2)}) collective-permute-start(bf16[512,128]{1,0:T(8,128)(2,1)} %shard_map.100), channel_id=1, source_target_pairs={{0,4},{1,5},{2,6},{3,7},{4,0},{5,1},{6,2},{7,3},{8,12},{9,13},{10,... | collective-permute-start | bytes 393224 | tf_op jit(solution)/shard_map/ppermute | solution.py:596
  11.3 21.1 %all-to-all-start = ((s32[8,1,8]{2,1,0:T(1,128)}), s32[8,1,8]{2,1,0:T(1,128)}, u32[]{:S(2)}, u32[]{:S(2)}) async-start(s32[8,1,8]{2,1,0:T(1,128)} %bitcast.28), calls=%async_computation | async-start | bytes 8192 | tf_op jit(solution)/shard_map/all_to_all | solution.py:629
  17.0 25.0 %collective-permute-start.1 = (bf16[1024,128]{1,0:T(8,128)(2,1)}, bf16[1024,128]{1,0:T(8,128)(2,1)}, u32[]{:S(2)}, u32[]{:S(2)}) collective-permute-start(bf16[1024,128]{1,0:T(8,128)(2,1)} %pad_maximum_fusion.refs_0_), channel_id=1, source_target_pairs={{0,1},{1,0},{2,3},{3,2},{4,5},{5,4},{6,7},{7,6},{8,9},{9,8},{10,11... | collective-permute-start | bytes 786440 | tf_op jit(solution)/shard_map/ppermute | solution.py:596
  17.2 26.1 %collective-permute-start.2 = (bf16[1024,128]{1,0:T(8,128)(2,1)}, bf16[1024,128]{1,0:T(8,128)(2,1)}, u32[]{:S(2)}, u32[]{:S(2)}) collective-permute-start(bf16[1024,128]{1,0:T(8,128)(2,1)} %pad_maximum_fusion.refs_0_), channel_id=1, source_target_pairs={{0,2},{1,3},{2,0},{3,1},{4,6},{5,7},{6,4},{7,5},{8,10},{9,11},{10,... | collective-permute-start | bytes 786440 | tf_op jit(solution)/shard_map/ppermute | solution.py:596
  18.5 25.1 %collective-permute-start.3 = (bf16[1024,128]{1,0:T(8,128)(2,1)}, bf16[1024,128]{1,0:T(8,128)(2,1)}, u32[]{:S(2)}, u32[]{:S(2)}) collective-permute-start(bf16[1024,128]{1,0:T(8,128)(2,1)} %pad_maximum_fusion.refs_0_), channel_id=1, source_target_pairs={{0,3},{1,2},{2,1},{3,0},{4,7},{5,6},{6,5},{7,4},{8,11},{9,10},{10,... | collective-permute-start | bytes 786440 | tf_op jit(solution)/shard_map/ppermute | solution.py:596
  36.6 27.4 %collective-permute-start.10 = (bf16[1536,128]{1,0:T(8,128)(2,1)}, bf16[1536,128]{1,0:T(8,128)(2,1)}, u32[]{:S(2)}, u32[]{:S(2)}) collective-permute-start(bf16[1536,128]{1,0:T(8,128)(2,1)} %get-tuple-element.28), channel_id=1, source_target_pairs={{0,5},{1,4},{2,7},{3,6},{4,1},{5,0},{6,3},{7,2},{8,13},{9,12},{10,... | collective-permute-start | bytes 1179656 | tf_op jit(solution)/shard_map/ppermute | solution.py:596
  40.9 28.3 %collective-permute-start.6 = (bf16[1536,128]{1,0:T(8,128)(2,1)}, bf16[1536,128]{1,0:T(8,128)(2,1)}, u32[]{:S(2)}, u32[]{:S(2)}) collective-permute-start(bf16[1536,128]{1,0:T(8,128)(2,1)} %get-tuple-element.24), channel_id=1, source_target_pairs={{0,1},{1,0},{2,3},{3,2},{4,5},{5,4},{6,7},{7,6},{8,9},{9,8},{10,11... | collective-permute-start | bytes 1179656 | tf_op jit(solution)/shard_map/ppermute | solution.py:596
  42.0 27.4 %collective-permute-start.7 = (bf16[1536,128]{1,0:T(8,128)(2,1)}, bf16[1536,128]{1,0:T(8,128)(2,1)}, u32[]{:S(2)}, u32[]{:S(2)}) collective-permute-start(bf16[1536,128]{1,0:T(8,128)(2,1)} %get-tuple-element.25), channel_id=1, source_target_pairs={{0,2},{1,3},{2,0},{3,1},{4,6},{5,7},{6,4},{7,5},{8,10},{9,11},{10,... | collective-permute-start | bytes 1179656 | tf_op jit(solution)/shard_map/ppermute | solution.py:596
  43.3 33.3 %collective-permute-start.8 = (bf16[1536,128]{1,0:T(8,128)(2,1)}, bf16[1536,128]{1,0:T(8,128)(2,1)}, u32[]{:S(2)}, u32[]{:S(2)}) collective-permute-start(bf16[1536,128]{1,0:T(8,128)(2,1)} %get-tuple-element.26), channel_id=1, source_target_pairs={{0,3},{1,2},{2,1},{3,0},{4,7},{5,6},{6,5},{7,4},{8,11},{9,10},{10,... | collective-permute-start | bytes 1179656 | tf_op jit(solution)/shard_map/ppermute | solution.py:596
  43.5 34.1 %collective-permute-start.9 = (bf16[1536,128]{1,0:T(8,128)(2,1)}, bf16[1536,128]{1,0:T(8,128)(2,1)}, u32[]{:S(2)}, u32[]{:S(2)}) collective-permute-start(bf16[1536,128]{1,0:T(8,128)(2,1)} %get-tuple-element.27), channel_id=1, source_target_pairs={{0,4},{1,5},{2,6},{3,7},{4,0},{5,1},{6,2},{7,3},{8,12},{9,13},{10,... | collective-permute-start | bytes 1179656 | tf_op jit(solution)/shard_map/ppermute | solution.py:596
  58.1 0.7 copy-start.9
  58.7 0.7 copy-start.13
  63.1 1.0 copy-start.3
  64.0 52.8 %collective-permute-start.4 = (bf16[1536,128]{1,0:T(8,128)(2,1)}, bf16[1536,128]{1,0:T(8,128)(2,1)}, u32[]{:S(2)}, u32[]{:S(2)}) collective-permute-start(bf16[1536,128]{1,0:T(8,128)(2,1)} %get-tuple-element.22), channel_id=1, source_target_pairs={{0,6},{1,7},{2,4},{3,5},{4,2},{5,3},{6,0},{7,1},{8,14},{9,15},{10,... | collective-permute-start | bytes 1179656 | tf_op jit(solution)/shard_map/ppermute | solution.py:596
  69.2 47.6 %collective-permute-start.5 = (bf16[1536,128]{1,0:T(8,128)(2,1)}, bf16[1536,128]{1,0:T(8,128)(2,1)}, u32[]{:S(2)}, u32[]{:S(2)}) collective-permute-start(bf16[1536,128]{1,0:T(8,128)(2,1)} %get-tuple-element.23), channel_id=1, source_target_pairs={{0,7},{1,6},{2,5},{3,4},{4,3},{5,2},{6,1},{7,0},{8,15},{9,14},{10,... | collective-permute-start | bytes 1179656 | tf_op jit(solution)/shard_map/ppermute | solution.py:596
  69.4 60.8 %collective-permute-start.11 = (bf16[384,128]{1,0:T(8,128)(2,1)}, bf16[384,128]{1,0:T(8,128)(2,1)}, u32[]{:S(2)}, u32[]{:S(2)}) collective-permute-start(bf16[384,128]{1,0:T(8,128)(2,1)} %get-tuple-element.30.refs_0_), channel_id=1, source_target_pairs={{0,8},{8,0},{16,24},{24,16},{1,9},{9,1},{17,25},{25,17},{2,10},{10... | collective-permute-start | bytes 294920 | tf_op jit(solution)/shard_map/ppermute | solution.py:596
  76.6 53.6 %collective-permute-start.12 = (bf16[384,128]{1,0:T(8,128)(2,1)}, bf16[384,128]{1,0:T(8,128)(2,1)}, u32[]{:S(2)}, u32[]{:S(2)}) collective-permute-start(bf16[384,128]{1,0:T(8,128)(2,1)} %get-tuple-element.30.refs_0_), channel_id=1, source_target_pairs={{0,16},{8,24},{16,0},{24,8},{1,17},{9,25},{17,1},{25,9},{2,18},{10... | collective-permute-start | bytes 294920 | tf_op jit(solution)/shard_map/ppermute | solution.py:596
  77.6 52.6 %collective-permute-start.13 = (bf16[384,128]{1,0:T(8,128)(2,1)}, bf16[384,128]{1,0:T(8,128)(2,1)}, u32[]{:S(2)}, u32[]{:S(2)}) collective-permute-start(bf16[384,128]{1,0:T(8,128)(2,1)} %get-tuple-element.30.refs_0_), channel_id=1, source_target_pairs={{0,24},{8,16},{16,8},{24,0},{1,25},{9,17},{17,9},{25,1},{2,26},{10... | collective-permute-start | bytes 294920 | tf_op jit(solution)/shard_map/ppermute | solution.py:596
  116.8 1.2 copy-start
  118.1 1.2 copy-start.5
  119.3 0.7 copy-start.12
  120.0 0.9 copy-start.14
  120.9 9.4 %copy-start.1 = (bf16[8,512,256]{2,1,0:T(8,128)(2,1)S(1)}, bf16[8,512,256]{2,1,0:T(8,128)(2,1)}, u32[]{:S(2)}) copy-start(bf16[8,512,256]{2,1,0:T(8,128)(2,1)} %leaf_interp.1) | copy-start | bytes 6291460
  120.9 9.4 %copy-start.2 = (bf16[1,2048,256]{2,1,0:T(8,128)(2,1)S(1)}, bf16[1,2048,256]{2,1,0:T(8,128)(2,1)}, u32[]{:S(2)}) copy-start(bf16[1,2048,256]{2,1,0:T(8,128)(2,1)} %param.15) | copy-start | bytes 3145732
  120.9 9.4 %copy-start.4 = (bf16[8,512,128]{2,1,0:T(8,128)(2,1)S(1)}, bf16[8,512,128]{2,1,0:T(8,128)(2,1)}, u32[]{:S(2)}) copy-start(bf16[8,512,128]{2,1,0:T(8,128)(2,1)} %copy-done.3) | copy-start | bytes 3145732
  120.9 9.4 %copy-start.8 = (bf16[1,256,256]{2,1,0:T(8,128)(2,1)S(1)}, bf16[1,256,256]{2,1,0:T(8,128)(2,1)}, u32[]{:S(2)}) copy-start(bf16[1,256,256]{2,1,0:T(8,128)(2,1)} %param.18) | copy-start | bytes 393220
  120.9 9.4 %copy-start.10 = (s32[3]{0:T(128)S(1)}, s32[3]{0:T(128)}, u32[]{:S(2)}) copy-start(s32[3]{0:T(128)} %pad_add_fusion.where) | copy-start | bytes 40
  120.9 9.4 %copy-start.11 = (s32[1,4]{1,0:T(1,128)S(1)}, s32[1,4]{1,0:T(1,128)}, u32[]{:S(2)}) copy-start(s32[1,4]{1,0:T(1,128)} %partners.1) | copy-start | bytes 52
  129.3 1.0 copy-start.6
  130.3 1.2 copy-start.7
